TPU v7x, 32 devices: a whole 2x2x4 slice. The times are simulated.
32 devices in a mesh: frame: 8 (over y, x, core), tile: 4 (over z).
Axes of the slice: x: 2, y: 2, z: 4, core: 2. Of those that a mesh axis runs over, the one named last changes fastest.
Arguments:
- features: bfloat16 [8, 32, 4096], P('frame', None, 'tile'), may hold values from -6 to 6
- views: int32 [8, 4], replicated, may hold values from 0 to 7, as said below
- offsets: int32 [8, 4, 32, 32], P('frame', None, None, 'tile'), may hold values from -2 to 2
- kernels: bfloat16 [32, 128, 128], replicated, may hold values from -0.5 to 0.5
- reg_weight: bfloat16 [3, 8, 32], replicated, may hold values from -0.625 to 0.625
- head_weight: float32 [8], replicated, may hold values from -2 to 2
- depth_cot: float32 [8, 4096], P('frame', 'tile'), may hold values from -120 to 120
Outputs:
- depth: float32 [8, 4096], P('frame', 'tile')
- feature_grad: float32 [8, 32, 4096], P('frame', None, 'tile')
Inputs may be any that keep to these rules, and one draw needn't show every extreme that they name: `views`: row f lists 4 different frames, none of them f.
All inputs are finite; a program needn't handle non-finite values.
Results may differ from a plain program's by a relative error of at most 0.017.
The roundings to bfloat16 on the way count: a program that leaves them out, or rounds other values in their place, can miss the bound.
Values may be sent and summed in bfloat16 or wider, within the bound.
No kernel may reach another device: no remote copies, remote signals or barrier semaphores. Data moves between devices by JAX's collectives and lax.ppermute only.
A program may use at most 64 MiB of HBM per device.

v0:
```python
import jax
import jax.numpy as jnp
from jax import lax
from jax.sharding import PartitionSpec as P

V = 4
HB = 2


def padded_2(cells, sides, width):
    for axis, dim in sides:
        count = lax.axis_size(axis)
        ends = count - 1
        head = lax.slice_in_dim(cells, 0, width, axis=dim)
        tail = lax.slice_in_dim(cells, cells.shape[dim] - width, cells.shape[dim], axis=dim)
        cells = jnp.concatenate(
            [
                lax.ppermute(tail, axis, [(i, (i + 1) % count) for i in range(ends)]),
                cells,
                lax.ppermute(head, axis, [((i + 1) % count, i) for i in range(ends)]),
            ],
            axis=dim,
        )
    return cells


def passed_along(block, axis, distance):
    devices = range(lax.axis_size(axis))
    route = [((i - distance) % len(devices), i) for i in devices]
    return lax.ppermute(block, axis, route)


def warp_block(reference_feat, sources, block_index, kernel):
    frames, vcount, channels, padded_len = sources.shape
    blocks = sources.reshape(frames, vcount, channels, padded_len // 128, 128)
    picker = jax.vmap(jax.vmap(lambda blockset, where_at: jnp.take(blockset, where_at, axis=1)))
    picked = picker(blocks, block_index).astype(jnp.bfloat16)
    pixels = block_index.shape[2] * 128
    warped = jnp.dot(picked.reshape(-1, 128), kernel, preferred_element_type=jnp.float32)
    warped = warped.reshape(frames, vcount, channels, pixels)
    stacked = jnp.concatenate([reference_feat[:, None], warped], axis=1)
    average = jnp.sum(stacked, axis=1) / (V + 1)
    centred = stacked - average[:, None]
    return (jnp.sum(centred * centred, axis=1) / (V + 1)).astype(jnp.bfloat16)


def local_depth(reference_feat, sources, offsets, kernels, reg_weight, head_weight):
    block_count = offsets.shape[3]
    plane_count = kernels.shape[0]
    base_index = jnp.arange(block_count, dtype=jnp.int32) + HB
    plane_index = jnp.transpose(offsets, (2, 0, 1, 3)) + base_index

    def per_plane(plane_items):
        return warp_block(reference_feat, sources, plane_items[0], plane_items[1])

    volume = lax.map(jax.checkpoint(per_plane), (plane_index, kernels))
    padded = jnp.pad(volume, ((1, 1), (0, 0), (0, 0), (0, 0)))
    hidden = jnp.einsum(
        "rc,dacp->darp", reg_weight[0], padded[0:plane_count], preferred_element_type=jnp.float32
    )
    for tap_index in range(1, 3):
        hidden = hidden + jnp.einsum(
            "rc,dacp->darp",
            reg_weight[tap_index],
            padded[tap_index : tap_index + plane_count],
            preferred_element_type=jnp.float32,
        )
    scores = 4.0 * jnp.tanh(jnp.sum(hidden * head_weight[None, None, :, None], axis=2))
    weights = jnp.exp(scores)
    values = (jnp.arange(plane_count, dtype=jnp.float32) + 1.0) / plane_count
    return jnp.sum(weights * values[:, None, None], axis=0) / jnp.sum(weights, axis=0)


def per_device(features, views, offsets, kernels, reg_weight, head_weight, depth_cot):
    local_frames, channels, pixels = features.shape
    rim_width = HB * 128
    frame_pos = lax.axis_index("frame")
    frame_count = lax.axis_size("frame")
    my_views = lax.dynamic_slice_in_dim(views, frame_pos * local_frames, local_frames, 0)
    owners = my_views // local_frames
    slot_ids = my_views % local_frames
    slot_range = jnp.arange(local_frames, dtype=jnp.int32)
    padded = padded_2(features, (("tile", 2),), rim_width)
    gathered = jnp.zeros((local_frames, V, channels, padded.shape[2]), jnp.bfloat16)

    def choose(current, travelling, source_dev):
        matches = (owners == source_dev)[:, :, None] & (
            slot_ids[:, :, None] == slot_range[None, None, :]
        )
        selector = matches.astype(jnp.bfloat16)
        taken = jnp.einsum(
            "ajk,kcp->ajcp", selector, travelling, preferred_element_type=jnp.float32
        ).astype(jnp.bfloat16)
        return jnp.where(jnp.any(matches, axis=2)[:, :, None, None], taken, current)

    gathered = choose(gathered, padded, frame_pos)

    def pair_step(step_num, carry):
        forward_part, backward_part, current = carry
        forward_part = passed_along(forward_part, "frame", 1)
        backward_part = passed_along(backward_part, "frame", -1)
        current = choose(current, forward_part, (frame_pos - step_num) % frame_count)
        current = choose(current, backward_part, (frame_pos + step_num) % frame_count)
        return (forward_part, backward_part, current)

    gathered = lax.fori_loop(1, frame_count // 2 + 1, pair_step, (padded, padded, gathered))[2]
    ref_copy = features.astype(jnp.float32)
    src_copy = gathered.astype(jnp.float32)
    depth_map, pullback = jax.vjp(
        lambda ref_part, src_part: local_depth(
            ref_part, src_part, offsets, kernels, reg_weight, head_weight
        ),
        ref_copy,
        src_copy,
    )
    ref_grad, src_grad = pullback(depth_cot)

    def contribution(dest_dev):
        matches = (owners == dest_dev)[:, :, None] & (
            slot_ids[:, :, None] == slot_range[None, None, :]
        )
        return jnp.einsum(
            "ajk,ajcp->kcp", matches.astype(jnp.float32), src_grad, precision=lax.Precision.HIGHEST
        )

    returned = contribution((frame_pos - 1) % frame_count)

    def back_step(step_num, summed):
        summed = passed_along(summed.astype(jnp.bfloat16), "frame", 1).astype(summed.dtype)
        return summed + contribution((frame_pos - step_num - 1) % frame_count)

    returned = lax.fori_loop(1, frame_count, back_step, returned)
    core_grad = returned[:, :, rim_width : rim_width + pixels] + ref_grad
    rim_pair = jnp.concatenate(
        [returned[:, :, :rim_width], returned[:, :, rim_width + pixels :]], axis=2
    )
    rim_halo = padded_2(rim_pair.astype(jnp.bfloat16), (("tile", 2),), rim_width).astype(
        rim_pair.dtype
    )
    from_prev = rim_halo[:, :, :rim_width]
    from_next = rim_halo[:, :, 3 * rim_width :]
    core_grad = core_grad + jnp.pad(from_prev, ((0, 0), (0, 0), (0, pixels - rim_width)))
    core_grad = core_grad + jnp.pad(from_next, ((0, 0), (0, 0), (pixels - rim_width, 0)))
    return (depth_map, core_grad)


def solution(mesh):
    return jax.shard_map(
        per_device,
        mesh=mesh,
        in_specs=(
            P("frame", None, "tile"),
            P(),
            P("frame", None, None, "tile"),
            P(),
            P(),
            P(),
            P("frame", "tile"),
        ),
        out_specs=(P("frame", "tile"), P("frame", None, "tile")),
        check_vma=False,
    )
```

profile of v0, /device:TPU:0, one launch (start us, length us, event | category | flops | bytes accessed | tf_op | source)
XLA Modules:
  0.0 461.2 jit_solution(6214336498144365450)
XLA Ops:
  1.4 4.9 %collective-permute-start.3 = (bf16[1,32,256]{2,1,0:T(8,128)(2,1)S(1)}, bf16[1,32,256]{2,1,0:T(8,128)(2,1)S(1)}, u32[]{:S(2)}, u32[]{:S(2)}) collective-permute-start(bf16[1,32,256]{2,1,0:T(8,128)(2,1)S(1)} %get-tuple-element.664), channel_id=1, source_target_pairs={{0,1},{1,2},{2,3},{4,5},{5,6},{6,7},{8,9},{9,10},{10,11},{12,13},{... | collective-permute-start | bytes 49160 | tf_op jit(solution)/shard_map/ppermute | solution.py:18
  9.7 2.2 collective-permute-done.4
  12.2 22.7 %while.61 = (s32[]{:T(128)}, bf16[1,32,1536]{2,1,0:T(8,128)(2,1)S(1)}, bf16[1,32,1536]{2,1,0:T(8,128)(2,1)S(1)}, bf16[1,4,32,1536]{3,2,1,0:T(8,128)(2,1)S(1)}, s...) while((s32[]{:T(128)}, bf16[1,32,1536]{2,1,0:T(8,128)(2,1)S(1)}, ...), condition=%wide.region_1.2_spmd, body=%wide.region_0.1_spmd.sunk | while | flops 1277994 | bytes 2949647 | solution.py:106
  12.2 2.6 collective-permute-start.1
  14.9 2.3 collective-permute-done
  20.2 2.3 collective-permute-done
  25.6 2.7 collective-permute-done
  31.4 3.1 collective-permute-done
  34.9 88.7 %while.62 = (s32[]{:T(128)}, bf16[32,1,32,1024]{3,2,1,0:T(8,128)(2,1)}, s32[32,1,4,8]{3,2,1,0:T(4,128)S(1)}, bf16[1,4,32,12,128]{4,2,3,1,0:T(8,128)(2,1)S(1)}, b...) while((s32[]{:T(128)}, ...), condition=%wide.region_5.6_spmd, body=%wide.region_2.5_spmd.sunk | while | flops 34538208 | bytes 5082797 | solution.py:56
  123.7 2.3 fusion.38
  132.2 282.4 %while.64 = (s32[]{:T(128)}, f32[1,4,32,1536]{3,2,1,0:T(8,128)S(1)}, f32[1,32,1024]{2,1,0:T(8,128)S(1)}, s32[32,1,4,8]{3,2,1,0:T(4,128)S(1)}, bf16[32,128,128]{2...) while((s32[]{:T(128)}, ...), condition=%wide.region_13.14_spmd.clone, body=%wide.region_9.13_spmd.clone.sunk | while | flops 69862496 | bytes 23010712 | solution.py:56
  190.0 2.2 scatter_fusion
  242.9 2.2 scatter_fusion
  278.2 2.2 scatter_fusion
  415.9 35.4 %while.63 = (s32[]{:T(128)}, f32[1,32,1536]{2,1,0:T(8,128)S(1)}, s32[]{:T(128)}, s32[1,4]{1,0:T(1,128)S(1)}, f32[1,4,32,1536]{3,2,1,0:T(8,128)S(1)}, /*index=5*/...) while((s32[]{:T(128)}, f32[1,32,1536]{2,1,0:T(8,128)S(1)}, s32[]{:T(128)}, s32[1,4]{1,0:T(1,128)S(1)}, ...), condition=%wide.region_15.16_spmd, body=%wide.region_14.15_spmd.sunk | while | flops 2506771 | bytes 2162982 | solution.py:132
  418.0 3.0 collective-permute-done.2
  422.4 3.6 collective-permute-done.2
  427.4 3.6 collective-permute-done.2
  432.5 3.6 collective-permute-done.2
  437.5 3.6 collective-permute-done.2
  442.6 3.6 collective-permute-done.2
  447.6 3.6 collective-permute-done.2
  451.3 3.5 collective-permute-start.5
  456.3 4.2 collective-permute-done.6
  (1807 shorter events, 389.7 us)
Async XLA Ops:
  0.6 7.0 %copy-start = (s32[8,4]{0,1:T(4,128)S(1)}, s32[8,4]{0,1:T(4,128)}, u32[]{:S(2)}) copy-start(s32[8,4]{0,1:T(4,128)} %param.16) | copy-start | bytes 388
  1.4 7.4 %collective-permute-start.3 = (bf16[1,32,256]{2,1,0:T(8,128)(2,1)S(1)}, bf16[1,32,256]{2,1,0:T(8,128)(2,1)S(1)}, u32[]{:S(2)}, u32[]{:S(2)}) collective-permute-start(bf16[1,32,256]{2,1,0:T(8,128)(2,1)S(1)} %get-tuple-element.664), channel_id=1, source_target_pairs={{0,1},{1,2},{2,3},{4,5},{5,6},{6,7},{8,9},{9,10},{10,11},{12,13},{... | collective-permute-start | bytes 49160 | tf_op jit(solution)/shard_map/ppermute | solution.py:18
  6.3 5.6 %collective-permute-start.4 = (bf16[1,32,256]{2,1,0:T(8,128)(2,1)S(1)}, bf16[1,32,256]{2,1,0:T(8,128)(2,1)S(1)}, u32[]{:S(2)}, u32[]{:S(2)}) collective-permute-start(bf16[1,32,256]{2,1,0:T(8,128)(2,1)S(1)} %get-tuple-element.663), channel_id=1, source_target_pairs={{1,0},{2,1},{3,2},{5,4},{6,5},{7,6},{9,8},{10,9},{11,10},{13,12},{... | collective-permute-start | bytes 49160 | tf_op jit(solution)/shard_map/ppermute | solution.py:20
  12.2 5.0 %collective-permute-start = (bf16[1,32,1536]{2,1,0:T(8,128)(2,1)S(1)}, bf16[1,32,1536]{2,1,0:T(8,128)(2,1)S(1)}, u32[]{:S(2)}, u32[]{:S(2)}) collective-permute-start(bf16[1,32,1536]{2,1,0:T(8,128)(2,1)S(1)} %get-tuple-element.855), channel_id=1, source_target_pairs={{28,0},{0,4},{4,8},{8,12},{12,16},{16,20},{20,24},{24,28},{29,1},{... | collective-permute-start | bytes 294920 | tf_op jit(solution)/shard_map/while/body/eval_jaxpr/ppermute | solution.py:30
  12.2 4.9 %collective-permute-start.1 = (bf16[1,32,1536]{2,1,0:T(8,128)(2,1)S(1)}, bf16[1,32,1536]{2,1,0:T(8,128)(2,1)S(1)}, u32[]{:S(2)}, u32[]{:S(2)}) collective-permute-start(bf16[1,32,1536]{2,1,0:T(8,128)(2,1)S(1)} %get-tuple-element.856), channel_id=1, source_target_pairs={{4,0},{8,4},{12,8},{16,12},{20,16},{24,20},{28,24},{0,28},{5,1},{9... | collective-permute-start | bytes 294920 | tf_op jit(solution)/shard_map/while/body/eval_jaxpr/ppermute | solution.py:30
  17.5 5.1 %collective-permute-start = (bf16[1,32,1536]{2,1,0:T(8,128)(2,1)S(1)}, bf16[1,32,1536]{2,1,0:T(8,128)(2,1)S(1)}, u32[]{:S(2)}, u32[]{:S(2)}) collective-permute-start(bf16[1,32,1536]{2,1,0:T(8,128)(2,1)S(1)} %get-tuple-element.855), channel_id=1, source_target_pairs={{28,0},{0,4},{4,8},{8,12},{12,16},{16,20},{20,24},{24,28},{29,1},{... | collective-permute-start | bytes 294920 | tf_op jit(solution)/shard_map/while/body/eval_jaxpr/ppermute | solution.py:30
  18.4 4.1 collective-permute-start.1
  22.9 5.4 %collective-permute-start = (bf16[1,32,1536]{2,1,0:T(8,128)(2,1)S(1)}, bf16[1,32,1536]{2,1,0:T(8,128)(2,1)S(1)}, u32[]{:S(2)}, u32[]{:S(2)}) collective-permute-start(bf16[1,32,1536]{2,1,0:T(8,128)(2,1)S(1)} %get-tuple-element.855), channel_id=1, source_target_pairs={{28,0},{0,4},{4,8},{8,12},{12,16},{16,20},{20,24},{24,28},{29,1},{... | collective-permute-start | bytes 294920 | tf_op jit(solution)/shard_map/while/body/eval_jaxpr/ppermute | solution.py:30
  24.0 4.4 collective-permute-start.1
  28.7 5.8 %collective-permute-start = (bf16[1,32,1536]{2,1,0:T(8,128)(2,1)S(1)}, bf16[1,32,1536]{2,1,0:T(8,128)(2,1)S(1)}, u32[]{:S(2)}, u32[]{:S(2)}) collective-permute-start(bf16[1,32,1536]{2,1,0:T(8,128)(2,1)S(1)} %get-tuple-element.855), channel_id=1, source_target_pairs={{28,0},{0,4},{4,8},{8,12},{12,16},{16,20},{20,24},{24,28},{29,1},{... | collective-permute-start | bytes 294920 | tf_op jit(solution)/shard_map/while/body/eval_jaxpr/ppermute | solution.py:30
  29.9 4.6 collective-permute-start.1
  34.9 88.7 %copy-start.3 = (bf16[3,8,32]{2,1,0:T(8,128)(2,1)S(1)}, bf16[3,8,32]{2,1,0:T(8,128)(2,1)}, u32[]{:S(2)}) copy-start(bf16[3,8,32]{2,1,0:T(8,128)(2,1)} %param.19) | copy-start | bytes 4612
  123.7 2.3 copy-start.2
  126.6 0.9 copy-start.5
  415.9 44.6 %copy-start.6 = (pred[1024]{0:T(1024)(128)(4,1)S(1)}, pred[1024]{0:T(1024)(128)(4,1)}, u32[]{:S(2)}) copy-start(pred[1024]{0:T(1024)(128)(4,1)} %constant.296.clone.1) | copy-start | bytes 3076
  416.0 5.0 %collective-permute-start.2 = (bf16[1,32,1536]{2,1,0:T(8,128)(2,1)S(1)}, bf16[1,32,1536]{2,1,0:T(8,128)(2,1)S(1)}, u32[]{:S(2)}, u32[]{:S(2)}) collective-permute-start(bf16[1,32,1536]{2,1,0:T(8,128)(2,1)S(1)} %convert_element_type.280), channel_id=1, source_target_pairs={{28,0},{0,4},{4,8},{8,12},{12,16},{16,20},{20,24},{24,28},{29,1},{... | collective-permute-start | bytes 294920 | tf_op jit(solution)/shard_map/while/body/eval_jaxpr/ppermute | solution.py:30
  421.0 5.0 %collective-permute-start.2 = (bf16[1,32,1536]{2,1,0:T(8,128)(2,1)S(1)}, bf16[1,32,1536]{2,1,0:T(8,128)(2,1)S(1)}, u32[]{:S(2)}, u32[]{:S(2)}) collective-permute-start(bf16[1,32,1536]{2,1,0:T(8,128)(2,1)S(1)} %convert_element_type.280), channel_id=1, source_target_pairs={{28,0},{0,4},{4,8},{8,12},{12,16},{16,20},{20,24},{24,28},{29,1},{... | collective-permute-start | bytes 294920 | tf_op jit(solution)/shard_map/while/body/eval_jaxpr/ppermute | solution.py:30
  426.1 5.0 %collective-permute-start.2 = (bf16[1,32,1536]{2,1,0:T(8,128)(2,1)S(1)}, bf16[1,32,1536]{2,1,0:T(8,128)(2,1)S(1)}, u32[]{:S(2)}, u32[]{:S(2)}) collective-permute-start(bf16[1,32,1536]{2,1,0:T(8,128)(2,1)S(1)} %convert_element_type.280), channel_id=1, source_target_pairs={{28,0},{0,4},{4,8},{8,12},{12,16},{16,20},{20,24},{24,28},{29,1},{... | collective-permute-start | bytes 294920 | tf_op jit(solution)/shard_map/while/body/eval_jaxpr/ppermute | solution.py:30
  431.1 5.0 %collective-permute-start.2 = (bf16[1,32,1536]{2,1,0:T(8,128)(2,1)S(1)}, bf16[1,32,1536]{2,1,0:T(8,128)(2,1)S(1)}, u32[]{:S(2)}, u32[]{:S(2)}) collective-permute-start(bf16[1,32,1536]{2,1,0:T(8,128)(2,1)S(1)} %convert_element_type.280), channel_id=1, source_target_pairs={{28,0},{0,4},{4,8},{8,12},{12,16},{16,20},{20,24},{24,28},{29,1},{... | collective-permute-start | bytes 294920 | tf_op jit(solution)/shard_map/while/body/eval_jaxpr/ppermute | solution.py:30
  436.2 5.0 %collective-permute-start.2 = (bf16[1,32,1536]{2,1,0:T(8,128)(2,1)S(1)}, bf16[1,32,1536]{2,1,0:T(8,128)(2,1)S(1)}, u32[]{:S(2)}, u32[]{:S(2)}) collective-permute-start(bf16[1,32,1536]{2,1,0:T(8,128)(2,1)S(1)} %convert_element_type.280), channel_id=1, source_target_pairs={{28,0},{0,4},{4,8},{8,12},{12,16},{16,20},{20,24},{24,28},{29,1},{... | collective-permute-start | bytes 294920 | tf_op jit(solution)/shard_map/while/body/eval_jaxpr/ppermute | solution.py:30
  441.2 5.0 %collective-permute-start.2 = (bf16[1,32,1536]{2,1,0:T(8,128)(2,1)S(1)}, bf16[1,32,1536]{2,1,0:T(8,128)(2,1)S(1)}, u32[]{:S(2)}, u32[]{:S(2)}) collective-permute-start(bf16[1,32,1536]{2,1,0:T(8,128)(2,1)S(1)} %convert_element_type.280), channel_id=1, source_target_pairs={{28,0},{0,4},{4,8},{8,12},{12,16},{16,20},{20,24},{24,28},{29,1},{... | collective-permute-start | bytes 294920 | tf_op jit(solution)/shard_map/while/body/eval_jaxpr/ppermute | solution.py:30
  446.3 5.0 %collective-permute-start.2 = (bf16[1,32,1536]{2,1,0:T(8,128)(2,1)S(1)}, bf16[1,32,1536]{2,1,0:T(8,128)(2,1)S(1)}, u32[]{:S(2)}, u32[]{:S(2)}) collective-permute-start(bf16[1,32,1536]{2,1,0:T(8,128)(2,1)S(1)} %convert_element_type.280), channel_id=1, source_target_pairs={{28,0},{0,4},{4,8},{8,12},{12,16},{16,20},{20,24},{24,28},{29,1},{... | collective-permute-start | bytes 294920 | tf_op jit(solution)/shard_map/while/body/eval_jaxpr/ppermute | solution.py:30
  451.3 4.9 %collective-permute-start.5 = (bf16[1,32,256]{2,1,0:T(8,128)(2,1)S(1)}, bf16[1,32,256]{2,1,0:T(8,128)(2,1)S(1)}, u32[]{:S(2)}, u32[]{:S(2)}) collective-permute-start(bf16[1,32,256]{2,1,0:T(8,128)(2,1)S(1)} %get-tuple-element.658), channel_id=1, source_target_pairs={{0,1},{1,2},{2,3},{4,5},{5,6},{6,7},{8,9},{9,10},{10,11},{12,13},{... | collective-permute-start | bytes 49160 | tf_op jit(solution)/shard_map/ppermute | solution.py:18
  454.8 5.6 %collective-permute-start.6 = (bf16[1,32,256]{2,1,0:T(8,128)(2,1)S(1)}, bf16[1,32,256]{2,1,0:T(8,128)(2,1)S(1)}, u32[]{:S(2)}, u32[]{:S(2)}) collective-permute-start(bf16[1,32,256]{2,1,0:T(8,128)(2,1)S(1)} %get-tuple-element.659), channel_id=1, source_target_pairs={{1,0},{2,1},{3,2},{5,4},{6,5},{7,6},{9,8},{10,9},{11,10},{13,12},{... | collective-permute-start | bytes 49160 | tf_op jit(solution)/shard_map/ppermute | solution.py:20
  (33 other events, 27.8 us)
where the time goes:
time: 468 us; the launch traced here: 461 us
  other arithmetic  165 us (35%)
  local copies, waits for them, and re-layouts  161 us (34%)
  matrix products  60.7 us (13%)
  waiting for transfers between devices  41.8 us (9%)
  starting transfers between devices  22.9 us (5%)
  loops' own time  9 us (2%)
    scatter-add x96, other arithmetic, warp_block(): jnp.take(blockset, where_at, axis=1)  72.9 us
    squeeze x96, local copies, waits for them, and re-layouts, local_depth(): volume = lax.map(jax.checkpoint(per_plane), (plane_index, kernels))  51.5 us
    gather x128, local copies, waits for them, and re-layouts, warp_block(): jnp.take(blockset, where_at, axis=1)  48.3 us
    dot_general x96, matrix products, warp_block(): jnp.dot(picked.reshape(-1, 128), kernel, preferred_element_type=jnp.float32)  44.7 us
    add_any x64, other arithmetic, local_depth(): volume = lax.map(jax.checkpoint(per_plane), (plane_index, kernels))  38.5 us
    ppermute x15, waiting for transfers between devices, passed_along(): return lax.ppermute(block, axis, route)  35.2 us
    dynamic_update_slice x32, other arithmetic, local_depth(): volume = lax.map(jax.checkpoint(per_plane), (plane_index, kernels))  20.4 us
    scatter-add x128, local copies, waits for them, and re-layouts, warp_block(): jnp.take(blockset, where_at, axis=1)  20.3 us
  transfers between devices with their start and end apart: 19, of which 14 were waited for; matrix products, arithmetic and copies ran while one was open for 2% of the time, Pallas kernels for 0%

commit v1 on v0

v1 whole, which is shorter than its diff:
```python
import functools

import jax
import jax.numpy as jnp
from jax import lax
from jax.experimental import pallas as pl
from jax.experimental.pallas import tpu as pltpu
from jax.sharding import PartitionSpec as P

V = 4
HB = 2
BLK = 128
F32 = jnp.float32
BF16 = jnp.bfloat16


def depth_kernel(
    views, offsets, head, feat, gathered, rim_left, rim_right, kernels, reg, cot,
    depth, ref_grad, core_grad, grad_left, grad_right,
    src, centred, partial, dscore, taps, *grads,
):
    frame_count, channels, pixels = gathered.shape
    nblk = pixels // BLK
    planes = kernels.shape[0]
    tap_count, hidden_count = reg.shape[0], reg.shape[1]
    rim = HB * BLK
    views_n = V
    me = lax.axis_index("frame")

    for j in range(views_n):
        owner = views[me, j]
        for q in range(HB):
            src[j, q] = rim_left[owner, :, q * BLK : (q + 1) * BLK]
            src[j, HB + nblk + q] = rim_right[owner, :, q * BLK : (q + 1) * BLK]
        for q in range(nblk):
            src[j, HB + q] = gathered[owner, :, q * BLK : (q + 1) * BLK]
        grads[j][...] = jnp.zeros_like(grads[j])

    taps[...] = jnp.zeros_like(taps)
    for t in range(tap_count):
        row = head[0] * reg[t, 0:1, :].astype(F32)
        for r in range(1, hidden_count):
            row = row + head[r] * reg[t, r : r + 1, :].astype(F32)
        taps[0, t : t + 1, 0:channels] = row
    taps[1] = taps[0].T
    for t in range(tap_count):
        taps[2 + t, 0:channels, :] = jnp.broadcast_to(
            taps[1, 0:channels, t : t + 1], (channels, BLK)
        )

    partial[...] = jnp.zeros_like(partial)
    ref_grad[...] = jnp.zeros_like(ref_grad)
    dscore[0] = jnp.zeros_like(dscore[0])
    dscore[planes + 1] = jnp.zeros_like(dscore[planes + 1])

    def rows_of(b, j):
        start = (b * views_n + j) * channels
        return slice(start, start + channels)

    def forward(d, carry):
        picked = []
        for b in range(nblk):
            for j in range(views_n):
                picked.append(src[j, offsets[0, j, d, b] + (b + HB)])
        warped = jnp.dot(
            jnp.concatenate(picked, axis=0), kernels[d], preferred_element_type=F32
        )
        for b in range(nblk):
            lanes = slice(b * BLK, (b + 1) * BLK)
            xs = [feat[0, :, lanes].astype(F32)]
            xs += [warped[rows_of(b, j)] for j in range(views_n)]
            average = sum(xs[1:], xs[0]) * (1.0 / (views_n + 1))
            cs = [x - average for x in xs]
            for i, c in enumerate(cs):
                centred[d, i, :, lanes] = c
            total = cs[0] * cs[0]
            for c in cs[1:]:
                total = total + c * c
            variance = (total * (1.0 / (views_n + 1))).astype(BF16).astype(F32)
            for t in range(tap_count):
                product = variance * taps[2 + t, 0:channels, :]
                folded = product.reshape(channels // 8, 8, BLK).sum(axis=0)
                partial[d + 2 - t, :, lanes] += folded
        return carry

    lax.fori_loop(0, planes, forward, 0)

    values = (
        lax.broadcasted_iota(jnp.int32, (planes, BLK), 0).astype(F32) + 1.0
    ) / planes
    for b in range(nblk):
        lanes = slice(b * BLK, (b + 1) * BLK)
        raw = partial[1 : planes + 1, :, lanes].sum(axis=1)
        tanh = jnp.tanh(raw)
        weights = jnp.exp(4.0 * tanh)
        norm = jnp.sum(weights, axis=0, keepdims=True)
        result = jnp.sum(weights * values, axis=0, keepdims=True) / norm
        depth[0:1, lanes] = result
        slope = (cot[0:1, lanes] / norm) * (values - result) * weights
        draw = slope * (4.0 * (1.0 - tanh * tanh))
        for d in range(planes):
            dscore[d + 1, :, lanes] = draw[d : d + 1]

    def backward(d, carry):
        rows = []
        for b in range(nblk):
            lanes = slice(b * BLK, (b + 1) * BLK)
            dvar = jnp.zeros((channels, BLK), F32)
            for t in range(tap_count):
                dvar = dvar + taps[2 + t, 0:channels, :] * dscore[d + 2 - t, :, lanes]
            scale = dvar.astype(BF16).astype(F32) * (2.0 / (views_n + 1))
            cs = [centred[d, i, :, lanes] for i in range(views_n + 1)]
            mean = sum(cs[1:], cs[0]) * (1.0 / (views_n + 1))
            ref_grad[:, lanes] += scale * (cs[0] - mean)
            for c in cs[1:]:
                rows.append((scale * (c - mean)).astype(BF16))
        dpicked = lax.dot_general(
            jnp.concatenate(rows, axis=0), kernels[d],
            (((1,), (1,)), ((), ())), preferred_element_type=F32,
        )
        for b in range(nblk):
            for j in range(views_n):
                grads[j][offsets[0, j, d, b] + (b + HB)] += dpicked[rows_of(b, j)]
        return carry

    lax.fori_loop(0, planes, backward, 0)

    for f in range(frame_count):
        core_grad[f] = jnp.zeros_like(core_grad[f])
    for j in range(views_n):
        owner = views[me, j]
        for q in range(nblk):
            core_grad[owner, :, q * BLK : (q + 1) * BLK] = grads[j][HB + q].astype(BF16)
        for q in range(HB):
            grad_left[j, :, q * BLK : (q + 1) * BLK] = grads[j][q].astype(BF16)
            grad_right[j, :, q * BLK : (q + 1) * BLK] = grads[j][HB + nblk + q].astype(BF16)


def merge_kernel(views, from_left, from_right, core, out):
    me = lax.axis_index("frame")
    rim = HB * BLK
    out[...] = core[...]
    pixels = core.shape[2]
    for j in range(V):
        owner = views[me, j]
        out[owner, :, 0:rim] = (
            out[owner, :, 0:rim].astype(F32) + from_left[j].astype(F32)
        ).astype(BF16)
        out[owner, :, pixels - rim :] = (
            out[owner, :, pixels - rim :].astype(F32) + from_right[j].astype(F32)
        ).astype(BF16)


def per_device(features, views, offsets, kernels, reg_weight, head_weight, depth_cot):
    local_frames, channels, pixels = features.shape
    assert local_frames == 1
    frame_count = lax.axis_size("frame")
    tile_count = lax.axis_size("tile")
    rim = HB * BLK
    nblk = pixels // BLK
    planes = kernels.shape[0]
    to_next = [(i, i + 1) for i in range(tile_count - 1)]
    to_prev = [(i + 1, i) for i in range(tile_count - 1)]

    gathered = lax.all_gather(features, "frame", axis=0, tiled=True)
    rim_left = lax.ppermute(gathered[:, :, pixels - rim :], "tile", to_next)
    rim_right = lax.ppermute(gathered[:, :, :rim], "tile", to_prev)

    smem = pl.BlockSpec(memory_space=pltpu.SMEM)
    vmem = pl.BlockSpec(memory_space=pltpu.VMEM)
    depth, ref_grad, core_grad, grad_left, grad_right = pl.pallas_call(
        depth_kernel,
        out_shape=(
            jax.ShapeDtypeStruct((1, pixels), F32),
            jax.ShapeDtypeStruct((channels, pixels), F32),
            jax.ShapeDtypeStruct((frame_count, channels, pixels), BF16),
            jax.ShapeDtypeStruct((V, channels, rim), BF16),
            jax.ShapeDtypeStruct((V, channels, rim), BF16),
        ),
        in_specs=[smem, smem, smem] + [vmem] * 7,
        out_specs=(vmem,) * 5,
        scratch_shapes=[
            pltpu.VMEM((V, nblk + 2 * HB, channels, BLK), BF16),
            pltpu.VMEM((planes, V + 1, channels, pixels), F32),
            pltpu.VMEM((planes + 2, 8, pixels), F32),
            pltpu.VMEM((planes + 2, 1, pixels), F32),
            pltpu.VMEM((5, BLK, BLK), F32),
        ]
        + [pltpu.VMEM((nblk + 2 * HB, channels, BLK), F32)] * V,
        compiler_params=pltpu.CompilerParams(vmem_limit_bytes=48 << 20),
        cost_estimate=pl.CostEstimate(
            flops=4 * planes * V * channels * pixels * BLK, bytes_accessed=4 << 20,
            transcendentals=2 * planes * pixels,
        ),
        name="depth_window",
    )(
        views, offsets, head_weight, features, gathered, rim_left, rim_right, kernels,
        reg_weight, depth_cot,
    )

    from_left = lax.ppermute(grad_right, "tile", to_next)
    from_right = lax.ppermute(grad_left, "tile", to_prev)
    merged = pl.pallas_call(
        merge_kernel,
        out_shape=jax.ShapeDtypeStruct((frame_count, channels, pixels), BF16),
        in_specs=[smem] + [vmem] * 3,
        out_specs=vmem,
        name="merge_rims",
    )(views, from_left, from_right, core_grad)
    pieces = lax.all_to_all(merged, "frame", 0, 0, tiled=True)
    grad = jnp.sum(pieces.astype(F32), axis=0) + ref_grad
    return depth, grad[None]


def solution(mesh):
    return jax.shard_map(
        per_device,
        mesh=mesh,
        in_specs=(
            P("frame", None, "tile"),
            P(),
            P("frame", None, None, "tile"),
            P(),
            P(),
            P(),
            P("frame", "tile"),
        ),
        out_specs=(P("frame", "tile"), P("frame", None, "tile")),
        check_vma=False,
    )
```

time: 468 us -> 71.7 us (0.15); the launches traced: 461 us -> 71.3 us
  other arithmetic: 165 us -> 0.75 us
  local copies, waits for them, and re-layouts: 161 us -> 1.62 us
  matrix products: 60.7 us -> 0 us
  waiting for transfers between devices: 41.8 us -> 7.63 us
  blocking collectives: 0 us -> 24.9 us
  Pallas kernels: 0 us -> 24.1 us
  starting transfers between devices: 22.9 us -> 11.7 us
  loops' own time: 9 us -> 0 us
    scatter-add x96 -> x0, other arithmetic: 72.9 us -> none  [warp_block(): jnp.take(blockset, where_at, axis=1)]
    dot_general x110 -> x0, matrix products: 60.7 us -> none  [the longest x96 44.7 us: warp_block(): jnp.dot(picked.reshape(-1, 128), kernel, preferred_element_type=jnp.float32)]
    squeeze x96 -> x0, local copies, waits for them, and re-layouts: 51.5 us -> none  [local_depth(): volume = lax.map(jax.checkpoint(per_plane), (plane_index, kernels))]
    gather x128 -> x0, local copies, waits for them, and re-layouts: 48.3 us -> none  [warp_block(): jnp.take(blockset, where_at, axis=1)]
    add_any x96 -> x0, other arithmetic: 42.1 us -> none  [the longest x64 38.5 us: local_depth(): volume = lax.map(jax.checkpoint(per_plane), (plane_index, kernels))]
    ppermute x19 -> x4, waiting for transfers between devices: 41.8 us -> 7.63 us  [the longest x1 4.27 us: per_device(): from_right = lax.ppermute(grad_left, 'tile', to_prev)]
    pallas_call x0 -> x2, Pallas kernels: none -> 24.1 us  [the longest x1 22.1 us: per_device(): pl.pallas_call(depth_kernel, out_shape=(jax.ShapeDtypeStruct((1, pixels),...]
    dynamic_update_slice x32 -> x0, other arithmetic: 20.4 us -> none  [local_depth(): volume = lax.map(jax.checkpoint(per_plane), (plane_index, kernels))]
  transfers between devices with their start and end apart: 19 -> 4, of which waited for: 14 -> 4; matrix products, arithmetic and copies ran while one was open for 2% -> 0% of each run, Pallas kernels for 0% -> 0%
where the time goes in v1:
time: 71.7 us; the launch traced here: 71.3 us
  blocking collectives  24.9 us (35%)
  Pallas kernels  24.1 us (34%)
  starting transfers between devices  11.7 us (16%)
  waiting for transfers between devices  7.63 us (11%)
  local copies, waits for them, and re-layouts  1.62 us (2%)
  other arithmetic  0.75 us (1%)
  between operations  0.73 us (1%)
    pallas_call x1, Pallas kernels, per_device(): pl.pallas_call(depth_kernel, out_shape=(jax.ShapeDtypeStruct((1, pixels),...  22.1 us
    all_to_all x1, blocking collectives, per_device(): pieces = lax.all_to_all(merged, 'frame', 0, 0, tiled=True)  13.1 us
    all_gather x1, blocking collectives, per_device(): gathered = lax.all_gather(features, 'frame', axis=0, tiled=True)  11.8 us
    ppermute x1, starting transfers between devices, per_device(): rim_left = lax.ppermute(gathered[:, :, pixels - rim:], 'tile', to_next)  4.55 us
    ppermute x1, starting transfers between devices, per_device(): from_left = lax.ppermute(grad_right, 'tile', to_next)  4.39 us
    ppermute x1, waiting for transfers between devices, per_device(): from_right = lax.ppermute(grad_left, 'tile', to_prev)  4.27 us
    pallas_call x1, Pallas kernels, per_device(): pl.pallas_call(merge_kernel, out_shape=jax.ShapeDtypeStruct((frame_count,...  2 us
    unnamed x24, local copies, waits for them, and re-layouts  1.6 us
  transfers between devices with their start and end apart: 4, of which 4 were waited for; matrix products, arithmetic and copies ran while one was open for 0% of the time, Pallas kernels for 0%

profile of v1, /device:TPU:0, one launch (start us, length us, event | category | flops | bytes accessed | tf_op | source)
XLA Modules:
  0.0 71.3 jit_solution(7744772867043137245)
XLA Ops:
  0.6 0.0 copy-start.3
  0.6 11.8 %all_gather.3.gathered = bf16[8,32,1024]{2,1,0:T(8,128)(2,1)S(1)} all-gather(bf16[1,32,1024]{2,1,0:T(8,128)(2,1)} %feat.1), channel_id=1, replica_groups=mesh['frame'=8,'tile'=4] {'frame'}, dimensions={0}, use_global_device_ids=true | all-gather | bytes 589824 | tf_op jit(solution)/shard_map/all_gather | solution.py:165
  12.4 0.0 copy-start.1
  12.4 1.4 %collective-permute-start.1 = (bf16[8,32,256]{2,1,0:T(8,128)(2,1)S(1)}, bf16[8,32,256]{2,1,0:T(8,128)(2,1)S(1)}, u32[]{:S(2)}, u32[]{:S(2)}) collective-permute-start(bf16[8,32,256]{2,1,0:T(8,128)(2,1)S(1)} %get-tuple-element.12), channel_id=1, source_target_pairs={{1,0},{2,1},{3,2},{5,4},{6,5},{7,6},{9,8},{10,9},{11,10},{13,12},{... | collective-permute-start | bytes 393224 | tf_op jit(solution)/shard_map/ppermute | solution.py:167
  13.9 4.6 %collective-permute-start = (bf16[8,32,256]{2,1,0:T(8,128)(2,1)S(1)}, bf16[8,32,256]{2,1,0:T(8,128)(2,1)S(1)}, u32[]{:S(2)}, u32[]{:S(2)}) collective-permute-start(bf16[8,32,256]{2,1,0:T(8,128)(2,1)S(1)} %get-tuple-element.13), channel_id=1, source_target_pairs={{0,1},{1,2},{2,3},{4,5},{5,6},{6,7},{8,9},{9,10},{10,11},{12,13},{... | collective-permute-start | bytes 393224 | tf_op jit(solution)/shard_map/ppermute | solution.py:166
  18.4 0.1 copy.12.views
  18.5 0.0 copy-start.6
  18.6 0.1 copy.13.offsets
  18.6 1.6 %collective-permute-done.1.rim_right = bf16[8,32,256]{2,1,0:T(8,128)(2,1)S(1)} collective-permute-done((bf16[8,32,256]{2,1,0:T(8,128)(2,1)S(1)}, bf16[8,32,256]{2,1,0:T(8,128)(2,1)S(1)}, u32[]{:S(2)}, u32[]{:S(2)}) %collective-permute-start.1) | collective-permute-done | bytes 131104 | tf_op jit(solution)/shard_map/ppermute | solution.py:167
  20.2 1.2 %collective-permute-done.rim_left = bf16[8,32,256]{2,1,0:T(8,128)(2,1)S(1)} collective-permute-done((bf16[8,32,256]{2,1,0:T(8,128)(2,1)S(1)}, bf16[8,32,256]{2,1,0:T(8,128)(2,1)S(1)}, u32[]{:S(2)}, u32[]{:S(2)}) %collective-permute-start) | collective-permute-done | bytes 131104 | tf_op jit(solution)/shard_map/ppermute | solution.py:166
  21.4 0.0 copy-done.3
  21.4 0.0 copy-done.4
  21.4 22.1 %depth_window.1 = (f32[1,1024]{1,0:T(1,128)}, f32[32,1024]{1,0:T(8,128)S(1)}, bf16[8,32,1024]{2,1,0:T(8,128)(2,1)S(1)}, bf16[4,32,256]{2,1,0:T(8,128)(2,1)S(1)}, bf16[4,32,256]{2,1,0:T(8,128)(2,1)S(1)}) custom-call(s32[8,4]{1,0:T(8,128)S(1)} %copy.12.views, s32[1,4,32,8]{3,2,1,0:T(8,128)S(1)} %copy.13.offsets, f32[8]{0:T(128)S(1)} %copy-done.6, ...), custom_call_target="tpu_custom_call" | custom-call | flops 2147483648 | bytes 4194304 | tf_op jit(solution)/shard_map/depth_window/pallas_call | solution.py:171
  43.5 0.8 %copy-done = bf16[8,32,1024]{2,1,0:T(8,128)(2,1)} copy-done((bf16[8,32,1024]{2,1,0:T(8,128)(2,1)}, bf16[8,32,1024]{2,1,0:T(8,128)(2,1)S(1)}, u32[]{:S(2)}) %copy-start) | copy-done | bytes 524312
  44.3 4.4 %collective-permute-start.2 = (bf16[4,32,256]{2,1,0:T(8,128)(2,1)S(1)}, bf16[4,32,256]{2,1,0:T(8,128)(2,1)S(1)}, u32[]{:S(2)}, u32[]{:S(2)}) collective-permute-start(bf16[4,32,256]{2,1,0:T(8,128)(2,1)S(1)} %get-tuple-element.8), channel_id=1, source_target_pairs={{0,1},{1,2},{2,3},{4,5},{5,6},{6,7},{8,9},{9,10},{10,11},{12,13},{... | collective-permute-start | bytes 196616 | tf_op jit(solution)/shard_map/ppermute | solution.py:201
  48.7 1.3 %collective-permute-start.3 = (bf16[4,32,256]{2,1,0:T(8,128)(2,1)S(1)}, bf16[4,32,256]{2,1,0:T(8,128)(2,1)S(1)}, u32[]{:S(2)}, u32[]{:S(2)}) collective-permute-start(bf16[4,32,256]{2,1,0:T(8,128)(2,1)S(1)} %get-tuple-element.9), channel_id=1, source_target_pairs={{1,0},{2,1},{3,2},{5,4},{6,5},{7,6},{9,8},{10,9},{11,10},{13,12},{... | collective-permute-start | bytes 196616 | tf_op jit(solution)/shard_map/ppermute | solution.py:202
  50.0 0.6 collective-permute-done.2.from_left
  50.6 4.3 %collective-permute-done.3.from_right = bf16[4,32,256]{2,1,0:T(8,128)(2,1)S(1)} collective-permute-done((bf16[4,32,256]{2,1,0:T(8,128)(2,1)S(1)}, bf16[4,32,256]{2,1,0:T(8,128)(2,1)S(1)}, u32[]{:S(2)}, u32[]{:S(2)}) %collective-permute-start.3) | collective-permute-done | bytes 65568 | tf_op jit(solution)/shard_map/ppermute | solution.py:202
  54.9 0.0 copy-done.7
  54.9 0.6 copy-done.8
  55.5 2.0 %merge_rims.1 = bf16[8,32,1024]{2,1,0:T(8,128)(2,1)} custom-call(s32[8,4]{1,0:T(8,128)} %copy-done.2, bf16[4,32,256]{2,1,0:T(8,128)(2,1)} %copy-done.7, bf16[4,32,256]{2,1,0:T(8,128)(2,1)} %copy-done.8, bf16[8,32,1024]{2,1,0:T(8,128)(2,1)} %copy-done), custom_call_target="tpu_custom_call" | custom-call | tf_op jit(solution)/shard_map/merge_rims/pallas_call | solution.py:203
  57.5 13.1 %all_to_all.5 = bf16[8,32,1024]{2,1,0:T(8,128)(2,1)S(1)} all-to-all(bf16[8,32,1024]{2,1,0:T(8,128)(2,1)} %merge_rims.1), channel_id=1, replica_groups=mesh['frame'=8,'tile'=4] {'frame'}, dimensions={0} | all-to-all | bytes 1048576 | tf_op jit(solution)/shard_map/all_to_all | solution.py:210
  70.6 0.1 convert_reduce_fusion
  70.7 0.7 add_bitcast_fusion
  (15 shorter events, 0.0 us)
Async XLA Ops:
  0.6 20.8 %copy-start.3 = (bf16[32,128,128]{2,1,0:T(8,128)(2,1)S(1)}, bf16[32,128,128]{2,1,0:T(8,128)(2,1)}, u32[]{:S(2)}) copy-start(bf16[32,128,128]{2,1,0:T(8,128)(2,1)} %kernels.1) | copy-start | bytes 3145732
  12.4 6.0 %copy-start.10 = (s32[8,4]{0,1:T(4,128)S(1)}, s32[8,4]{0,1:T(4,128)}, u32[]{:S(2)}) copy-start(s32[8,4]{0,1:T(4,128)} %param.8) | copy-start | bytes 388
  12.4 6.1 %copy-start.9 = (s32[1,4,32,8]{2,3,1,0:T(8,128)S(1)}, s32[1,4,32,8]{2,3,1,0:T(8,128)}, u32[]{:S(2)}) copy-start(s32[1,4,32,8]{2,3,1,0:T(8,128)} %param.9) | copy-start | bytes 12292
  12.4 9.0 %copy-start.1 = (bf16[1,32,1024]{2,1,0:T(8,128)(2,1)S(1)}, bf16[1,32,1024]{2,1,0:T(8,128)(2,1)}, u32[]{:S(2)}) copy-start(bf16[1,32,1024]{2,1,0:T(8,128)(2,1)} %feat.1) | copy-start | bytes 196612
  12.4 7.8 %collective-permute-start.1 = (bf16[8,32,256]{2,1,0:T(8,128)(2,1)S(1)}, bf16[8,32,256]{2,1,0:T(8,128)(2,1)S(1)}, u32[]{:S(2)}, u32[]{:S(2)}) collective-permute-start(bf16[8,32,256]{2,1,0:T(8,128)(2,1)S(1)} %get-tuple-element.12), channel_id=1, source_target_pairs={{1,0},{2,1},{3,2},{5,4},{6,5},{7,6},{9,8},{10,9},{11,10},{13,12},{... | collective-permute-start | bytes 393224 | tf_op jit(solution)/shard_map/ppermute | solution.py:167
  13.9 7.5 %collective-permute-start = (bf16[8,32,256]{2,1,0:T(8,128)(2,1)S(1)}, bf16[8,32,256]{2,1,0:T(8,128)(2,1)S(1)}, u32[]{:S(2)}, u32[]{:S(2)}) collective-permute-start(bf16[8,32,256]{2,1,0:T(8,128)(2,1)S(1)} %get-tuple-element.13), channel_id=1, source_target_pairs={{0,1},{1,2},{2,3},{4,5},{5,6},{6,7},{8,9},{9,10},{10,11},{12,13},{... | collective-permute-start | bytes 393224 | tf_op jit(solution)/shard_map/ppermute | solution.py:166
  18.5 2.9 %copy-start.2 = (s32[8,4]{1,0:T(8,128)}, s32[8,4]{1,0:T(8,128)S(1)}, u32[]{:S(2)}) copy-start(s32[8,4]{1,0:T(8,128)S(1)} %copy.12.views) | copy-start | bytes 388
  18.5 2.9 %copy-start.4 = (bf16[3,8,32]{2,1,0:T(8,128)(2,1)S(1)}, bf16[3,8,32]{2,1,0:T(8,128)(2,1)}, u32[]{:S(2)}) copy-start(bf16[3,8,32]{2,1,0:T(8,128)(2,1)} %reg.1) | copy-start | bytes 4612
  18.5 2.9 %copy-start.5 = (f32[1,1024]{1,0:T(1,128)S(1)}, f32[1,1024]{1,0:T(1,128)}, u32[]{:S(2)}) copy-start(f32[1,1024]{1,0:T(1,128)} %cot.1) | copy-start | bytes 12292
  18.5 2.9 %copy-start.6 = (f32[8]{0:T(128)S(1)}, f32[8]{0:T(128)}, u32[]{:S(2)}) copy-start(f32[8]{0:T(128)} %head.1) | copy-start | bytes 100
  43.5 0.8 %copy-start = (bf16[8,32,1024]{2,1,0:T(8,128)(2,1)}, bf16[8,32,1024]{2,1,0:T(8,128)(2,1)S(1)}, u32[]{:S(2)}) copy-start(bf16[8,32,1024]{2,1,0:T(8,128)(2,1)S(1)} %get-tuple-element.10.core) | copy-start | bytes 1572868
  44.3 6.3 %collective-permute-start.2 = (bf16[4,32,256]{2,1,0:T(8,128)(2,1)S(1)}, bf16[4,32,256]{2,1,0:T(8,128)(2,1)S(1)}, u32[]{:S(2)}, u32[]{:S(2)}) collective-permute-start(bf16[4,32,256]{2,1,0:T(8,128)(2,1)S(1)} %get-tuple-element.8), channel_id=1, source_target_pairs={{0,1},{1,2},{2,3},{4,5},{5,6},{6,7},{8,9},{9,10},{10,11},{12,13},{... | collective-permute-start | bytes 196616 | tf_op jit(solution)/shard_map/ppermute | solution.py:201
  48.7 6.2 %collective-permute-start.3 = (bf16[4,32,256]{2,1,0:T(8,128)(2,1)S(1)}, bf16[4,32,256]{2,1,0:T(8,128)(2,1)S(1)}, u32[]{:S(2)}, u32[]{:S(2)}) collective-permute-start(bf16[4,32,256]{2,1,0:T(8,128)(2,1)S(1)} %get-tuple-element.9), channel_id=1, source_target_pairs={{1,0},{2,1},{3,2},{5,4},{6,5},{7,6},{9,8},{10,9},{11,10},{13,12},{... | collective-permute-start | bytes 196616 | tf_op jit(solution)/shard_map/ppermute | solution.py:202
  50.6 4.3 %copy-start.7 = (bf16[4,32,256]{2,1,0:T(8,128)(2,1)}, bf16[4,32,256]{2,1,0:T(8,128)(2,1)S(1)}, u32[]{:S(2)}) copy-start(bf16[4,32,256]{2,1,0:T(8,128)(2,1)S(1)} %collective-permute-done.2.from_left) | copy-start | bytes 196612
  54.9 0.6 copy-start.8

commit v2 on v1

v2 whole, which is shorter than its diff:
```python
import jax
import jax.numpy as jnp
from jax import lax
from jax.experimental import pallas as pl
from jax.experimental.pallas import tpu as pltpu
from jax.sharding import PartitionSpec as P

V = 4
HB = 2
BLK = 128
CHUNKS = 4
BWD = 8
F32 = jnp.float32
BF16 = jnp.bfloat16
VMEM = pl.BlockSpec(memory_space=pltpu.VMEM)
SMEM = pl.BlockSpec(memory_space=pltpu.SMEM)
SMALL = pltpu.CompilerParams(vmem_limit_bytes=4 << 20)


def split3(w):
    high = w.astype(BF16).astype(F32)
    mid = (w - high).astype(BF16).astype(F32)
    return high, mid, w - high - mid


def weights_kernel(head, reg, band, band_t, rows):
    tap_count, hidden_count, channels = reg.shape
    planes = band.shape[0]
    rows[...] = jnp.zeros_like(rows)
    for t in range(tap_count):
        row = head[0] * reg[t, 0:1, :].astype(F32)
        for r in range(1, hidden_count):
            row = row + head[r] * reg[t, r : r + 1, :].astype(F32)
        rows[t : t + 1, 0:channels] = row
    columns = rows[...].T
    lane = lax.broadcasted_iota(jnp.int32, (channels, BLK), 1)
    part = lane // planes
    score = lane % planes
    weights = []
    for t in range(tap_count):
        high, mid, low = split3(
            jnp.broadcast_to(columns[0:channels, t : t + 1], (channels, BLK))
        )
        weights.append(jnp.where(part < 2, high, jnp.where(part == 2, mid, low)))
    for d in range(planes):
        tile = jnp.zeros((channels, BLK), F32)
        for t in range(tap_count):
            tile = jnp.where(score == d - t + 1, weights[t], tile)
        band[d] = tile.astype(BF16)
    per_tile = BLK // channels
    for k in range(planes // per_tile):
        tile = band[k * per_tile : (k + 1) * per_tile].reshape(BLK, BLK)
        band_t[:, k * BLK : (k + 1) * BLK] = tile.astype(F32).T.astype(BF16)


def pick_kernel(views, *refs):
    count = len(refs) - 3
    pieces, (core, first, second) = refs[:count], refs[count:]
    nblk = core.shape[1]
    me = lax.axis_index("frame")
    even = lax.axis_index("tile") % 2 == 0
    for j in range(V):
        slot = views[j, me] ^ me
        for r in range(count):

            @pl.when(slot == r + 1)
            def _(r=r, j=j):
                for q in range(nblk):
                    core[j, q] = pieces[r][0, :, q * BLK : (q + 1) * BLK]

    right, left = slice(nblk - HB, nblk), slice(0, HB)

    @pl.when(even)
    def _():
        first[...] = core[:, right]
        second[...] = core[:, left]

    @pl.when(jnp.logical_not(even))
    def _():
        first[...] = core[:, left]
        second[...] = core[:, right]


def depth_kernel(
    offsets, feat, core, first, second, kernels, band, band_t, cot,
    depth, ref_grad, core_grad, grad_first, grad_second,
    src, base, shifted, means, volume, matrices, arrived, *grads,
):
    channels, pixels = ref_grad.shape
    nblk = pixels // BLK
    planes = kernels.shape[0]
    share = 1.0 / (V + 1)
    chunk = planes // CHUNKS

    def load(k):
        part = pl.ds(k * chunk, chunk)
        return pltpu.make_async_copy(kernels.at[part], matrices.at[part], arrived.at[k])

    for k in range(CHUNKS):
        load(k).start()

    even = lax.axis_index("tile") % 2 == 0
    left, right = slice(0, HB), slice(HB + nblk, None)

    @pl.when(even)
    def _():
        src[:, right] = first[...]
        src[:, left] = second[...]

    @pl.when(jnp.logical_not(even))
    def _():
        src[:, left] = first[...]
        src[:, right] = second[...]

    for j in range(V):
        for q in range(nblk):
            src[j, HB + q] = core[j, q]
        grads[j][...] = jnp.zeros_like(grads[j])
    ref_grad[...] = jnp.zeros_like(ref_grad)
    base[...] = feat[0].astype(F32)

    def rows_of(b, j):
        start = (b * V + j) * channels
        return slice(start, start + channels)

    def forward(d, carry):
        picked = []
        for b in range(nblk):
            for j in range(V):
                picked.append(src[j, offsets[0, j, b, d] + (b + HB)])
        warped = jnp.dot(
            jnp.concatenate(picked, axis=0), matrices[d], preferred_element_type=F32
        )
        for b in range(nblk):
            lanes = slice(b * BLK, (b + 1) * BLK)
            first = base[:, lanes]
            ys = [warped[rows_of(b, j)] - first for j in range(V)]
            for j in range(V):
                shifted[d, j, :, lanes] = ys[j]
            total = (ys[0] + ys[1]) + (ys[2] + ys[3])
            mean = total * share
            squares = (ys[0] * ys[0] + ys[1] * ys[1]) + (ys[2] * ys[2] + ys[3] * ys[3])
            variance = (squares - total * mean) * share
            volume[d, :, lanes] = variance.astype(BF16)
            means[d, :, lanes] = mean + (total - (V + 1) * mean) * share
        return carry

    def forward_chunk(k, carry):
        load(k).wait()
        for i in range(chunk):
            forward(k * chunk + i, carry)
        return carry

    lax.fori_loop(0, CHUNKS, forward_chunk, 0)

    wide = BLK * (2 if nblk % 2 == 0 else 1)
    groups = [slice(i, i + wide) for i in range(0, pixels, wide)]
    values = (
        lax.broadcasted_iota(jnp.int32, (planes, wide), 0).astype(F32) + 1.0
    ) / planes
    raws = []
    for lanes in groups:
        parts = jnp.dot(
            band_t[...], volume[:, :, lanes].reshape(planes * channels, wide),
            preferred_element_type=F32,
        )
        raws.append(
            parts[0:planes]
            + (parts[2 * planes : 3 * planes] + parts[3 * planes : 4 * planes])
        )
    stacks = []
    for lanes, raw in zip(groups, raws):
        tanh = jnp.tanh(raw)
        weights = jnp.exp(4.0 * tanh)
        norm = jnp.sum(weights, axis=0, keepdims=True)
        result = jnp.sum(weights * values, axis=0, keepdims=True) / norm
        depth[0:1, lanes] = result
        slope = (cot[0:1, lanes] / norm) * (values - result) * weights
        draw = slope * (4.0 * (1.0 - tanh * tanh))
        high = draw.astype(BF16)
        low = (draw - high.astype(F32)).astype(BF16)
        stacks.append(jnp.concatenate([high, low, high, high], axis=0))
    for lanes, stack in zip(groups, stacks):
        dvolume = jnp.dot(
            band[...].reshape(planes * channels, BLK), stack, preferred_element_type=F32
        )
        volume[:, :, lanes] = dvolume.astype(BF16).reshape(planes, channels, wide)

    def backward(d, carry):
        rows = []
        for b in range(nblk):
            lanes = slice(b * BLK, (b + 1) * BLK)
            dvar = volume[d, :, lanes].astype(F32)
            mean = means[d, :, lanes]
            ref_grad[:, lanes] -= dvar * mean
            for j in range(V):
                rows.append((dvar * (shifted[d, j, :, lanes] - mean)).astype(BF16))
        dpicked = lax.dot_general(
            jnp.concatenate(rows, axis=0), matrices[d],
            (((1,), (1,)), ((), ())), preferred_element_type=F32,
        )
        for b in range(nblk):
            for j in range(V):
                grads[j][offsets[0, j, b, d] + (b + HB)] += dpicked[rows_of(b, j)]
        return carry

    lax.fori_loop(0, planes, backward, 0, unroll=BWD)

    scale = 2.0 * share
    ref_grad[...] = ref_grad[...] * scale
    for j in range(V):
        core_grad[j] = grads[j][HB : HB + nblk] * scale

    @pl.when(even)
    def _():
        for j in range(V):
            grad_first[j] = (grads[j][right] * scale).astype(BF16)
            grad_second[j] = (grads[j][left] * scale).astype(BF16)

    @pl.when(jnp.logical_not(even))
    def _():
        for j in range(V):
            grad_first[j] = (grads[j][left] * scale).astype(BF16)
            grad_second[j] = (grads[j][right] * scale).astype(BF16)


def merge_kernel(views, core, first, second, near, far, left, right):
    me = lax.axis_index("frame")
    nblk = core.shape[1]
    near[...] = jnp.zeros_like(near)
    far[...] = jnp.zeros_like(far)
    even = lax.axis_index("tile") % 2 == 0

    @pl.when(even)
    def _():
        right[...] = first[...].astype(F32)
        left[...] = second[...].astype(F32)

    @pl.when(jnp.logical_not(even))
    def _():
        left[...] = first[...].astype(F32)
        right[...] = second[...].astype(F32)

    def put(out, j, index):
        for q in range(nblk):
            tile = core[j, q]
            if q < HB:
                tile = tile + left[j, q]
            if q >= nblk - HB:
                tile = tile + right[j, q - (nblk - HB)]
            out[index, :, q * BLK : (q + 1) * BLK] = tile.astype(BF16)

    for j in range(V):
        slot = views[j, me] ^ me

        @pl.when(slot % 2 == 0)
        def _(j=j, slot=slot):
            put(near, j, slot // 2)

        @pl.when(slot % 2 == 1)
        def _(j=j, slot=slot):
            put(far, j, slot // 2)


def pair_kernel(near, received, own, *sent):
    own[...] = near[0].astype(F32) + received[0].astype(F32)
    for i, out in enumerate(sent):
        out[0] = (near[i + 1].astype(F32) + received[i + 1].astype(F32)).astype(BF16)


def exchange(x, distance):
    count = lax.axis_size("frame")
    return lax.ppermute(x, "frame", [(i, i ^ distance) for i in range(count)])


def swap_rims(first, second):
    count = lax.axis_size("tile")
    received = []
    for start, rim in ((0, first), (1, second)):
        pairs = [(i, i + 1) for i in range(start, count - 1, 2)]
        received.append(lax.ppermute(rim, "tile", pairs + [(b, a) for a, b in pairs]))
    return received


def per_device(features, views, offsets, kernels, reg_weight, head_weight, depth_cot):
    local_frames, channels, pixels = features.shape
    frame_count = lax.axis_size("frame")
    assert local_frames == 1 and frame_count & (frame_count - 1) == 0
    nblk = pixels // BLK
    planes = kernels.shape[0]
    shape = jax.ShapeDtypeStruct
    rim_shape = shape((V, HB, channels, BLK), BF16)
    views = views.T
    offsets = jnp.swapaxes(offsets, 2, 3)

    band, band_t = pl.pallas_call(
        weights_kernel,
        out_shape=(
            shape((planes, channels, BLK), BF16), shape((BLK, planes * channels), BF16),
        ),
        in_specs=[SMEM, VMEM],
        out_specs=(VMEM, VMEM),
        scratch_shapes=[pltpu.VMEM((BLK, BLK), F32)],
        compiler_params=SMALL,
        name="band_weights",
    )(head_weight, reg_weight)

    pieces = {0: features}
    for r in range(2, frame_count, 2):
        pieces[r] = exchange(features, r)
    for r in range(0, frame_count, 2):
        pieces[r + 1] = exchange(pieces[r], 1)
    core, first, second = pl.pallas_call(
        pick_kernel,
        out_shape=(shape((V, nblk, channels, BLK), BF16), rim_shape, rim_shape),
        in_specs=[SMEM] + [VMEM] * (frame_count - 1),
        out_specs=(VMEM,) * 3,
        compiler_params=SMALL,
        name="pick_views",
    )(views, *[pieces[r] for r in range(1, frame_count)])
    first, second = swap_rims(first, second)

    depth, ref_grad, core_grad, grad_first, grad_second = pl.pallas_call(
        depth_kernel,
        out_shape=(
            shape((1, pixels), F32), shape((channels, pixels), F32),
            shape((V, nblk, channels, BLK), F32), rim_shape, rim_shape,
        ),
        in_specs=[SMEM] + [VMEM] * 4 + [pl.BlockSpec(memory_space=pltpu.HBM)] + [VMEM] * 3,
        out_specs=(VMEM,) * 5,
        scratch_shapes=[
            pltpu.VMEM((V, nblk + 2 * HB, channels, BLK), BF16),
            pltpu.VMEM((channels, pixels), F32),
            pltpu.VMEM((planes, V, channels, pixels), F32),
            pltpu.VMEM((planes, channels, pixels), F32),
            pltpu.VMEM((planes, channels, pixels), BF16),
            pltpu.VMEM((planes, BLK, BLK), BF16),
            pltpu.SemaphoreType.DMA((CHUNKS,)),
        ]
        + [pltpu.VMEM((nblk + 2 * HB, channels, BLK), F32)] * V,
        compiler_params=pltpu.CompilerParams(vmem_limit_bytes=30 << 20),
        cost_estimate=pl.CostEstimate(
            flops=4 * planes * V * channels * pixels * BLK, bytes_accessed=4 << 20,
            transcendentals=2 * planes * pixels,
        ),
        name="depth_window",
    )(offsets, features, core, first, second, pltpu.with_memory_space_constraint(kernels, pltpu.HBM), band, band_t, depth_cot)

    grad_first, grad_second = swap_rims(grad_first, grad_second)
    half = shape((frame_count // 2, channels, pixels), BF16)
    near, far = pl.pallas_call(
        merge_kernel,
        out_shape=(half, half),
        in_specs=[SMEM] + [VMEM] * 3,
        out_specs=(VMEM, VMEM),
        scratch_shapes=[pltpu.VMEM((V, HB, channels, BLK), F32)] * 2,
        compiler_params=SMALL,
        name="merge_rims",
    )(views, core_grad, grad_first, grad_second)
    received = exchange(far, 1)
    own, *sent = pl.pallas_call(
        pair_kernel,
        out_shape=(shape((channels, pixels), F32),)
        + (shape((1, channels, pixels), BF16),) * (frame_count // 2 - 1),
        in_specs=[VMEM, VMEM],
        out_specs=(VMEM,) * (frame_count // 2),
        compiler_params=SMALL,
        name="add_pair",
    )(near, received)
    total = (own + ref_grad)[None]
    for i, piece in enumerate(sent):
        total = total + exchange(piece, 2 * i + 2).astype(F32)
    return depth, total


def solution(mesh):
    return jax.shard_map(
        per_device,
        mesh=mesh,
        in_specs=(
            P("frame", None, "tile"),
            P(),
            P("frame", None, None, "tile"),
            P(),
            P(),
            P(),
            P("frame", "tile"),
        ),
        out_specs=(P("frame", "tile"), P("frame", None, "tile")),
        check_vma=False,
    )
```

time: 71.7 us -> 48.4 us (0.68)
  the two profiles are of different devices: /device:TPU:0 before, /device:TPU:16 now
where the time goes in v2:
time: 48.4 us; the launch traced here: 48.3 us
  waiting for transfers between devices  18.1 us (37%)
  Pallas kernels  15.2 us (31%)
  starting transfers between devices  12.7 us (26%)
  between operations  0.77 us (2%)
  local copies, waits for them, and re-layouts  0.71 us (1%)
  other arithmetic  0.69 us (1%)
    pallas_call x1, Pallas kernels, per_device(): pl.pallas_call(depth_kernel, out_shape=(shape((1, pixels), F32), shape((c...  12.8 us
    ppermute x11, waiting for transfers between devices, exchange(): return lax.ppermute(x, 'frame', [(i, i ^ distance) for i in range(count)])  10.6 us
    ppermute x4, waiting for transfers between devices, swap_rims(): lax.ppermute(rim, 'tile', pairs + [(b, a) for a, b in pairs])  7.55 us
    ppermute x11, starting transfers between devices, exchange(): return lax.ppermute(x, 'frame', [(i, i ^ distance) for i in range(count)])  7.19 us
    ppermute x4, starting transfers between devices, swap_rims(): lax.ppermute(rim, 'tile', pairs + [(b, a) for a, b in pairs])  5.54 us
  transfers between devices with their start and end apart: 15, of which 11 were waited for; matrix products, arithmetic and copies ran while one was open for 0% of the time, Pallas kernels for 2%

profile of v2, /device:TPU:16, one launch (start us, length us, event | category | flops | bytes accessed | tf_op | source)
XLA Modules:
  0.0 48.3 jit_solution(10463188347549517113)
XLA Ops:
  0.6 1.6 %collective-permute-start.3 = (bf16[1,32,1024]{2,1,0:T(8,128)(2,1)}, bf16[1,32,1024]{2,1,0:T(8,128)(2,1)S(1)}, u32[]{:S(2)}, u32[]{:S(2)}) collective-permute-start(bf16[1,32,1024]{2,1,0:T(8,128)(2,1)} %feat.1), channel_id=1, source_target_pairs={{0,16},{4,20},{8,24},{12,28},{16,0},{20,4},{24,8},{28,12},{1,17},{... | collective-permute-start | bytes 196616 | tf_op jit(solution)/shard_map/ppermute | solution.py:273
  2.2 1.5 %collective-permute-start.1 = (bf16[1,32,1024]{2,1,0:T(8,128)(2,1)}, bf16[1,32,1024]{2,1,0:T(8,128)(2,1)S(1)}, u32[]{:S(2)}, u32[]{:S(2)}) collective-permute-start(bf16[1,32,1024]{2,1,0:T(8,128)(2,1)} %feat.1), channel_id=1, source_target_pairs={{0,8},{4,12},{8,0},{12,4},{16,24},{20,28},{24,16},{28,20},{1,9},{5... | collective-permute-start | bytes 196616 | tf_op jit(solution)/shard_map/ppermute | solution.py:273
  4.2 1.0 %collective-permute-done.3.refs_3_ = bf16[1,32,1024]{2,1,0:T(8,128)(2,1)S(1)} collective-permute-done((bf16[1,32,1024]{2,1,0:T(8,128)(2,1)}, bf16[1,32,1024]{2,1,0:T(8,128)(2,1)S(1)}, u32[]{:S(2)}, u32[]{:S(2)}) %collective-permute-start.3) | collective-permute-done | bytes 65568 | tf_op jit(solution)/shard_map/ppermute | solution.py:273
  5.2 2.0 %collective-permute-done.1.refs_1_ = bf16[1,32,1024]{2,1,0:T(8,128)(2,1)S(1)} collective-permute-done((bf16[1,32,1024]{2,1,0:T(8,128)(2,1)}, bf16[1,32,1024]{2,1,0:T(8,128)(2,1)S(1)}, u32[]{:S(2)}, u32[]{:S(2)}) %collective-permute-start.1) | collective-permute-done | bytes 65568 | tf_op jit(solution)/shard_map/ppermute | solution.py:273
  7.1 1.9 %collective-permute-done.5.refs_5_ = bf16[1,32,1024]{2,1,0:T(8,128)(2,1)S(1)} collective-permute-done((bf16[1,32,1024]{2,1,0:T(8,128)(2,1)}, bf16[1,32,1024]{2,1,0:T(8,128)(2,1)S(1)}, u32[]{:S(2)}, u32[]{:S(2)}) %collective-permute-start.5) | collective-permute-done | bytes 65568 | tf_op jit(solution)/shard_map/ppermute | solution.py:273
  9.1 1.2 %collective-permute-done.6.refs_6_ = bf16[1,32,1024]{2,1,0:T(8,128)(2,1)S(1)} collective-permute-done((bf16[1,32,1024]{2,1,0:T(8,128)(2,1)S(1)}, bf16[1,32,1024]{2,1,0:T(8,128)(2,1)S(1)}, u32[]{:S(2)}, u32[]{:S(2)}) %collective-permute-start.6) | collective-permute-done | bytes 65568 | tf_op jit(solution)/shard_map/ppermute | solution.py:273
  10.3 0.7 %copy-done = s32[8,4]{0,1:T(4,128)S(1)} copy-done((s32[8,4]{0,1:T(4,128)S(1)}, s32[8,4]{0,1:T(4,128)}, u32[]{:S(2)}) %copy-start) | copy-done | bytes 152
  11.0 0.8 %pick_views.1 = (bf16[4,8,32,128]{3,2,1,0:T(8,128)(2,1)S(1)}, bf16[4,2,32,128]{3,2,1,0:T(8,128)(2,1)S(1)}, bf16[4,2,32,128]{3,2,1,0:T(8,128)(2,1)S(1)}) custom-call(s32[4,8]{1,0:T(4,128)S(1)} %bitcast.8, bf16[1,32,1024]{2,1,0:T(8,128)(2,1)S(1)} %collective-permute-done.refs_0_, bf16[1,32,1024]{2,1,0:T(8,128)(2,1)S(1)} %collective-permute-done.1.refs_1_, ...), custom_call_target="tpu_custom_call" | custom-call | tf_op jit(solution)/shard_map/pick_views/pallas_call | solution.py:313
  11.8 1.6 %collective-permute-start.7 = (bf16[4,2,32,128]{3,2,1,0:T(8,128)(2,1)S(1)}, bf16[4,2,32,128]{3,2,1,0:T(8,128)(2,1)S(1)}, u32[]{:S(2)}, u32[]{:S(2)}) collective-permute-start(bf16[4,2,32,128]{3,2,1,0:T(8,128)(2,1)S(1)} %get-tuple-element.19), channel_id=1, source_target_pairs={{0,1},{2,3},{1,0},{3,2},{4,5},{6,7},{5,4},{7,6},{8,9},{10,11},{9,8... | collective-permute-start | bytes 196616 | tf_op jit(solution)/shard_map/ppermute | solution.py:281
  13.5 1.9 %collective-permute-start.8 = (bf16[4,2,32,128]{3,2,1,0:T(8,128)(2,1)S(1)}, bf16[4,2,32,128]{3,2,1,0:T(8,128)(2,1)S(1)}, u32[]{:S(2)}, u32[]{:S(2)}) collective-permute-start(bf16[4,2,32,128]{3,2,1,0:T(8,128)(2,1)S(1)} %get-tuple-element.20), channel_id=1, source_target_pairs={{1,2},{2,1},{5,6},{6,5},{9,10},{10,9},{13,14},{14,13},{17,18},{18,... | collective-permute-start | bytes 196616 | tf_op jit(solution)/shard_map/ppermute | solution.py:281
  15.4 0.9 %band_weights.1 = (bf16[32,32,128]{2,1,0:T(8,128)(2,1)S(1)}, bf16[128,1024]{1,0:T(8,128)(2,1)S(1)}) custom-call(f32[8]{0:T(128)S(1)} %copy-done.3, bf16[3,8,32]{2,1,0:T(8,128)(2,1)S(1)} %copy-done.2), custom_call_target="tpu_custom_call" | custom-call | tf_op jit(solution)/shard_map/band_weights/pallas_call | solution.py:296
  16.3 3.3 %collective-permute-done.8.second = bf16[4,2,32,128]{3,2,1,0:T(8,128)(2,1)S(1)} collective-permute-done((bf16[4,2,32,128]{3,2,1,0:T(8,128)(2,1)S(1)}, bf16[4,2,32,128]{3,2,1,0:T(8,128)(2,1)S(1)}, u32[]{:S(2)}, u32[]{:S(2)}) %collective-permute-start.8) | collective-permute-done | bytes 65568 | tf_op jit(solution)/shard_map/ppermute | solution.py:281
  19.6 12.8 %depth_window.1 = (f32[1,1024]{1,0:T(1,128)}, f32[32,1024]{1,0:T(8,128)S(1)}, f32[4,8,32,128]{3,2,1,0:T(8,128)S(1)}, bf16[4,2,32,128]{3,2,1,0:T(8,128)(2,1)S(1)}, bf16[4,2,32,128]{3,2,1,0:T(8,128)(2,1)S(1)}) custom-call(s32[1,4,8,32]{3,2,1,0:T(8,128)S(1)} %bitcast.10, bf16[1,32,1024]{2,1,0:T(8,128)(2,1)S(1)} %copy-done.4, ...), custom_call_target="tpu_custom_call" | custom-call | flops 2147483648 | bytes 4194304 | tf_op jit(solution)/shard_map/depth_window/pallas_call | solution.py:323
  32.5 1.9 %collective-permute-start.10 = (bf16[4,2,32,128]{3,2,1,0:T(8,128)(2,1)S(1)}, bf16[4,2,32,128]{3,2,1,0:T(8,128)(2,1)S(1)}, u32[]{:S(2)}, u32[]{:S(2)}) collective-permute-start(bf16[4,2,32,128]{3,2,1,0:T(8,128)(2,1)S(1)} %get-tuple-element.26), channel_id=1, source_target_pairs={{1,2},{2,1},{5,6},{6,5},{9,10},{10,9},{13,14},{14,13},{17,18},{18,... | collective-permute-start | bytes 196616 | tf_op jit(solution)/shard_map/ppermute | solution.py:281
  34.4 2.3 %collective-permute-done.9.first = bf16[4,2,32,128]{3,2,1,0:T(8,128)(2,1)S(1)} collective-permute-done((bf16[4,2,32,128]{3,2,1,0:T(8,128)(2,1)S(1)}, bf16[4,2,32,128]{3,2,1,0:T(8,128)(2,1)S(1)}, u32[]{:S(2)}, u32[]{:S(2)}) %collective-permute-start.9) | collective-permute-done | bytes 65568 | tf_op jit(solution)/shard_map/ppermute | solution.py:281
  36.8 1.9 %collective-permute-done.10.second = bf16[4,2,32,128]{3,2,1,0:T(8,128)(2,1)S(1)} collective-permute-done((bf16[4,2,32,128]{3,2,1,0:T(8,128)(2,1)S(1)}, bf16[4,2,32,128]{3,2,1,0:T(8,128)(2,1)S(1)}, u32[]{:S(2)}, u32[]{:S(2)}) %collective-permute-start.10) | collective-permute-done | bytes 65568 | tf_op jit(solution)/shard_map/ppermute | solution.py:281
  38.7 0.7 %merge_rims.1 = (bf16[4,32,1024]{2,1,0:T(8,128)(2,1)S(1)}, bf16[4,32,1024]{2,1,0:T(8,128)(2,1)S(1)}) custom-call(s32[4,8]{1,0:T(4,128)S(1)} %bitcast.9, f32[4,8,32,128]{3,2,1,0:T(8,128)S(1)} %get-tuple-element.24.core, bf16[4,2,32,128]{3,2,1,0:T(8,128)(2,1)S(1)} %collective-permute-done.9.first, bf16[4,2,32,128]{3,2,1,0:T(8,128)(2,1)S(1)} %collective-permute-done.10.second), custom_call_target="tpu_custom_call" | custom-call | tf_op jit(solution)/shard_map/merge_rims/pallas_call | solution.py:351
  39.5 1.5 %collective-permute-done.11.received = bf16[4,32,1024]{2,1,0:T(8,128)(2,1)S(1)} collective-permute-done((bf16[4,32,1024]{2,1,0:T(8,128)(2,1)S(1)}, bf16[4,32,1024]{2,1,0:T(8,128)(2,1)S(1)}, u32[]{:S(2)}, u32[]{:S(2)}) %collective-permute-start.11) | collective-permute-done | bytes 262176 | tf_op jit(solution)/shard_map/ppermute | solution.py:273
  41.7 0.7 %collective-permute-start.13 = (bf16[1,32,1024]{2,1,0:T(8,128)(2,1)S(1)}, bf16[1,32,1024]{2,1,0:T(8,128)(2,1)S(1)}, u32[]{:S(2)}, u32[]{:S(2)}) collective-permute-start(bf16[1,32,1024]{2,1,0:T(8,128)(2,1)S(1)} %get-tuple-element.32), channel_id=1, source_target_pairs={{0,16},{4,20},{8,24},{12,28},{16,0},{20,4},{24,8},{28,12},{1,17},{... | collective-permute-start | bytes 196616 | tf_op jit(solution)/shard_map/ppermute | solution.py:273
  42.4 2.2 %collective-permute-start.14 = (bf16[1,32,1024]{2,1,0:T(8,128)(2,1)S(1)}, bf16[1,32,1024]{2,1,0:T(8,128)(2,1)S(1)}, u32[]{:S(2)}, u32[]{:S(2)}) collective-permute-start(bf16[1,32,1024]{2,1,0:T(8,128)(2,1)S(1)} %get-tuple-element.33), channel_id=1, source_target_pairs={{0,24},{4,28},{8,16},{12,20},{16,8},{20,12},{24,0},{28,4},{1,25},{... | collective-permute-start | bytes 196616 | tf_op jit(solution)/shard_map/ppermute | solution.py:273
  44.6 0.9 %collective-permute-done.12 = bf16[1,32,1024]{2,1,0:T(8,128)(2,1)S(1)} collective-permute-done((bf16[1,32,1024]{2,1,0:T(8,128)(2,1)S(1)}, bf16[1,32,1024]{2,1,0:T(8,128)(2,1)S(1)}, u32[]{:S(2)}, u32[]{:S(2)}) %collective-permute-start.12) | collective-permute-done | bytes 65568 | tf_op jit(solution)/shard_map/ppermute | solution.py:273
  45.6 1.1 %collective-permute-done.13 = bf16[1,32,1024]{2,1,0:T(8,128)(2,1)S(1)} collective-permute-done((bf16[1,32,1024]{2,1,0:T(8,128)(2,1)S(1)}, bf16[1,32,1024]{2,1,0:T(8,128)(2,1)S(1)}, u32[]{:S(2)}, u32[]{:S(2)}) %collective-permute-start.13) | collective-permute-done | bytes 65568 | tf_op jit(solution)/shard_map/ppermute | solution.py:273
  46.6 0.9 %collective-permute-done.14 = bf16[1,32,1024]{2,1,0:T(8,128)(2,1)S(1)} collective-permute-done((bf16[1,32,1024]{2,1,0:T(8,128)(2,1)S(1)}, bf16[1,32,1024]{2,1,0:T(8,128)(2,1)S(1)}, u32[]{:S(2)}, u32[]{:S(2)}) %collective-permute-start.14) | collective-permute-done | bytes 65568 | tf_op jit(solution)/shard_map/ppermute | solution.py:273
  47.6 0.7 %fusion.1 = f32[1,32,1024]{2,1,0:T(8,128)} fusion(bf16[1,32,1024]{2,1,0:T(8,128)(2,1)S(1)} %collective-permute-done.14, bf16[1,32,1024]{2,1,0:T(8,128)(2,1)S(1)} %collective-permute-done.13, bf16[1,32,1024]{2,1,0:T(8,128)(2,1)S(1)} %collective-permute-done.12, f32[32,1024]{1,0:T(8,128)S(1)} %get-tuple-element.29, f32[32,1024]{1,0:T(8,128)S(1)} %get-tuple-element.30), kind=kLoop, calls=%fused_computation.2 | loop fusion | flops 229376 | bytes 589824 | tf_op jit(solution)/shard_map/add | solution.py:372
  (26 shorter events, 1.3 us)
Async XLA Ops:
  0.6 4.5 %collective-permute-start.3 = (bf16[1,32,1024]{2,1,0:T(8,128)(2,1)}, bf16[1,32,1024]{2,1,0:T(8,128)(2,1)S(1)}, u32[]{:S(2)}, u32[]{:S(2)}) collective-permute-start(bf16[1,32,1024]{2,1,0:T(8,128)(2,1)} %feat.1), channel_id=1, source_target_pairs={{0,16},{4,20},{8,24},{12,28},{16,0},{20,4},{24,8},{28,12},{1,17},{... | collective-permute-start | bytes 196616 | tf_op jit(solution)/shard_map/ppermute | solution.py:273
  2.2 4.9 %collective-permute-start.1 = (bf16[1,32,1024]{2,1,0:T(8,128)(2,1)}, bf16[1,32,1024]{2,1,0:T(8,128)(2,1)S(1)}, u32[]{:S(2)}, u32[]{:S(2)}) collective-permute-start(bf16[1,32,1024]{2,1,0:T(8,128)(2,1)} %feat.1), channel_id=1, source_target_pairs={{0,8},{4,12},{8,0},{12,4},{16,24},{20,28},{24,16},{28,20},{1,9},{5... | collective-permute-start | bytes 196616 | tf_op jit(solution)/shard_map/ppermute | solution.py:273
  3.7 5.4 %collective-permute-start.5 = (bf16[1,32,1024]{2,1,0:T(8,128)(2,1)}, bf16[1,32,1024]{2,1,0:T(8,128)(2,1)S(1)}, u32[]{:S(2)}, u32[]{:S(2)}) collective-permute-start(bf16[1,32,1024]{2,1,0:T(8,128)(2,1)} %feat.1), channel_id=1, source_target_pairs={{0,24},{4,28},{8,16},{12,20},{16,8},{20,12},{24,0},{28,4},{1,25},{... | collective-permute-start | bytes 196616 | tf_op jit(solution)/shard_map/ppermute | solution.py:273
  4.2 4.9 %collective-permute-start = (bf16[1,32,1024]{2,1,0:T(8,128)(2,1)}, bf16[1,32,1024]{2,1,0:T(8,128)(2,1)S(1)}, u32[]{:S(2)}, u32[]{:S(2)}) collective-permute-start(bf16[1,32,1024]{2,1,0:T(8,128)(2,1)} %feat.1), channel_id=1, source_target_pairs={{0,4},{4,0},{8,12},{12,8},{16,20},{20,16},{24,28},{28,24},{1,5},{5... | collective-permute-start | bytes 196616 | tf_op jit(solution)/shard_map/ppermute | solution.py:273
  5.2 3.9 %collective-permute-start.4 = (bf16[1,32,1024]{2,1,0:T(8,128)(2,1)S(1)}, bf16[1,32,1024]{2,1,0:T(8,128)(2,1)S(1)}, u32[]{:S(2)}, u32[]{:S(2)}) collective-permute-start(bf16[1,32,1024]{2,1,0:T(8,128)(2,1)S(1)} %collective-permute-done.3.refs_3_), channel_id=1, source_target_pairs={{0,4},{4,0},{8,12},{12,8},{16,20},{20,16},{24,28},{28,24},{1,5},{5... | collective-permute-start | bytes 196616 | tf_op jit(solution)/shard_map/ppermute | solution.py:273
  7.1 2.0 %collective-permute-start.2 = (bf16[1,32,1024]{2,1,0:T(8,128)(2,1)S(1)}, bf16[1,32,1024]{2,1,0:T(8,128)(2,1)S(1)}, u32[]{:S(2)}, u32[]{:S(2)}) collective-permute-start(bf16[1,32,1024]{2,1,0:T(8,128)(2,1)S(1)} %collective-permute-done.1.refs_1_), channel_id=1, source_target_pairs={{0,4},{4,0},{8,12},{12,8},{16,20},{20,16},{24,28},{28,24},{1,5},{5... | collective-permute-start | bytes 196616 | tf_op jit(solution)/shard_map/ppermute | solution.py:273
  9.1 1.3 %collective-permute-start.6 = (bf16[1,32,1024]{2,1,0:T(8,128)(2,1)S(1)}, bf16[1,32,1024]{2,1,0:T(8,128)(2,1)S(1)}, u32[]{:S(2)}, u32[]{:S(2)}) collective-permute-start(bf16[1,32,1024]{2,1,0:T(8,128)(2,1)S(1)} %collective-permute-done.5.refs_5_), channel_id=1, source_target_pairs={{0,4},{4,0},{8,12},{12,8},{16,20},{20,16},{24,28},{28,24},{1,5},{5... | collective-permute-start | bytes 196616 | tf_op jit(solution)/shard_map/ppermute | solution.py:273
  10.3 0.7 %copy-start = (s32[8,4]{0,1:T(4,128)S(1)}, s32[8,4]{0,1:T(4,128)}, u32[]{:S(2)}) copy-start(s32[8,4]{0,1:T(4,128)} %param.8) | copy-start | bytes 388
  11.0 4.4 %copy-start.2 = (bf16[3,8,32]{2,1,0:T(8,128)(2,1)S(1)}, bf16[3,8,32]{2,1,0:T(8,128)(2,1)}, u32[]{:S(2)}) copy-start(bf16[3,8,32]{2,1,0:T(8,128)(2,1)} %reg.1) | copy-start | bytes 4612
  11.0 8.6 %copy-start.4 = (bf16[1,32,1024]{2,1,0:T(8,128)(2,1)S(1)}, bf16[1,32,1024]{2,1,0:T(8,128)(2,1)}, u32[]{:S(2)}) copy-start(bf16[1,32,1024]{2,1,0:T(8,128)(2,1)} %feat.1) | copy-start | bytes 196612
  11.0 8.6 %copy-start.5 = (s32[1,4,32,8]{2,3,1,0:T(8,128)S(1)}, s32[1,4,32,8]{2,3,1,0:T(8,128)}, u32[]{:S(2)}) copy-start(s32[1,4,32,8]{2,3,1,0:T(8,128)} %param.9) | copy-start | bytes 12292
  11.8 3.6 %copy-start.3 = (f32[8]{0:T(128)S(1)}, f32[8]{0:T(128)}, u32[]{:S(2)}) copy-start(f32[8]{0:T(128)} %head.1) | copy-start | bytes 100
  11.8 4.5 %collective-permute-start.7 = (bf16[4,2,32,128]{3,2,1,0:T(8,128)(2,1)S(1)}, bf16[4,2,32,128]{3,2,1,0:T(8,128)(2,1)S(1)}, u32[]{:S(2)}, u32[]{:S(2)}) collective-permute-start(bf16[4,2,32,128]{3,2,1,0:T(8,128)(2,1)S(1)} %get-tuple-element.19), channel_id=1, source_target_pairs={{0,1},{2,3},{1,0},{3,2},{4,5},{6,7},{5,4},{7,6},{8,9},{10,11},{9,8... | collective-permute-start | bytes 196616 | tf_op jit(solution)/shard_map/ppermute | solution.py:281
  13.5 6.1 %collective-permute-start.8 = (bf16[4,2,32,128]{3,2,1,0:T(8,128)(2,1)S(1)}, bf16[4,2,32,128]{3,2,1,0:T(8,128)(2,1)S(1)}, u32[]{:S(2)}, u32[]{:S(2)}) collective-permute-start(bf16[4,2,32,128]{3,2,1,0:T(8,128)(2,1)S(1)} %get-tuple-element.20), channel_id=1, source_target_pairs={{1,2},{2,1},{5,6},{6,5},{9,10},{10,9},{13,14},{14,13},{17,18},{18,... | collective-permute-start | bytes 196616 | tf_op jit(solution)/shard_map/ppermute | solution.py:281
  16.3 3.3 %copy-start.6 = (f32[1,1024]{1,0:T(1,128)S(1)}, f32[1,1024]{1,0:T(1,128)}, u32[]{:S(2)}) copy-start(f32[1,1024]{1,0:T(1,128)} %cot.1) | copy-start | bytes 12292
  32.4 6.3 %copy-start.1 = (s32[8,4]{0,1:T(4,128)S(1)}, s32[8,4]{0,1:T(4,128)}, u32[]{:S(2)}) copy-start(s32[8,4]{0,1:T(4,128)} %param.8) | copy-start | bytes 388
  32.4 4.3 %collective-permute-start.9 = (bf16[4,2,32,128]{3,2,1,0:T(8,128)(2,1)S(1)}, bf16[4,2,32,128]{3,2,1,0:T(8,128)(2,1)S(1)}, u32[]{:S(2)}, u32[]{:S(2)}) collective-permute-start(bf16[4,2,32,128]{3,2,1,0:T(8,128)(2,1)S(1)} %get-tuple-element.25), channel_id=1, source_target_pairs={{0,1},{2,3},{1,0},{3,2},{4,5},{6,7},{5,4},{7,6},{8,9},{10,11},{9,8... | collective-permute-start | bytes 196616 | tf_op jit(solution)/shard_map/ppermute | solution.py:281
  32.5 6.2 %collective-permute-start.10 = (bf16[4,2,32,128]{3,2,1,0:T(8,128)(2,1)S(1)}, bf16[4,2,32,128]{3,2,1,0:T(8,128)(2,1)S(1)}, u32[]{:S(2)}, u32[]{:S(2)}) collective-permute-start(bf16[4,2,32,128]{3,2,1,0:T(8,128)(2,1)S(1)} %get-tuple-element.26), channel_id=1, source_target_pairs={{1,2},{2,1},{5,6},{6,5},{9,10},{10,9},{13,14},{14,13},{17,18},{18,... | collective-permute-start | bytes 196616 | tf_op jit(solution)/shard_map/ppermute | solution.py:281
  39.4 1.6 %collective-permute-start.11 = (bf16[4,32,1024]{2,1,0:T(8,128)(2,1)S(1)}, bf16[4,32,1024]{2,1,0:T(8,128)(2,1)S(1)}, u32[]{:S(2)}, u32[]{:S(2)}) collective-permute-start(bf16[4,32,1024]{2,1,0:T(8,128)(2,1)S(1)} %get-tuple-element.28), channel_id=1, source_target_pairs={{0,4},{4,0},{8,12},{12,8},{16,20},{20,16},{24,28},{28,24},{1,5},{5... | collective-permute-start | bytes 786440 | tf_op jit(solution)/shard_map/ppermute | solution.py:273
  41.1 4.5 %collective-permute-start.12 = (bf16[1,32,1024]{2,1,0:T(8,128)(2,1)S(1)}, bf16[1,32,1024]{2,1,0:T(8,128)(2,1)S(1)}, u32[]{:S(2)}, u32[]{:S(2)}) collective-permute-start(bf16[1,32,1024]{2,1,0:T(8,128)(2,1)S(1)} %get-tuple-element.31), channel_id=1, source_target_pairs={{0,8},{4,12},{8,0},{12,4},{16,24},{20,28},{24,16},{28,20},{1,9},{5... | collective-permute-start | bytes 196616 | tf_op jit(solution)/shard_map/ppermute | solution.py:273
  41.7 5.0 %collective-permute-start.13 = (bf16[1,32,1024]{2,1,0:T(8,128)(2,1)S(1)}, bf16[1,32,1024]{2,1,0:T(8,128)(2,1)S(1)}, u32[]{:S(2)}, u32[]{:S(2)}) collective-permute-start(bf16[1,32,1024]{2,1,0:T(8,128)(2,1)S(1)} %get-tuple-element.32), channel_id=1, source_target_pairs={{0,16},{4,20},{8,24},{12,28},{16,0},{20,4},{24,8},{28,12},{1,17},{... | collective-permute-start | bytes 196616 | tf_op jit(solution)/shard_map/ppermute | solution.py:273
  42.4 5.2 %collective-permute-start.14 = (bf16[1,32,1024]{2,1,0:T(8,128)(2,1)S(1)}, bf16[1,32,1024]{2,1,0:T(8,128)(2,1)S(1)}, u32[]{:S(2)}, u32[]{:S(2)}) collective-permute-start(bf16[1,32,1024]{2,1,0:T(8,128)(2,1)S(1)} %get-tuple-element.33), channel_id=1, source_target_pairs={{0,24},{4,28},{8,16},{12,20},{16,8},{20,12},{24,0},{28,4},{1,25},{... | collective-permute-start | bytes 196616 | tf_op jit(solution)/shard_map/ppermute | solution.py:273

commit v3 on v2

v3 whole, which is shorter than its diff:
```python
import jax
import jax.numpy as jnp
from jax import lax
from jax.experimental import pallas as pl
from jax.experimental.pallas import tpu as pltpu
from jax.sharding import PartitionSpec as P


V = 4
HB = 2
BLK = 128
CHUNKS = 4
UNROLL = 8
F32 = jnp.float32
BF16 = jnp.bfloat16
VMEM = pl.BlockSpec(memory_space=pltpu.VMEM)
SMEM = pl.BlockSpec(memory_space=pltpu.SMEM)
SMALL = pltpu.CompilerParams(vmem_limit_bytes=4 << 20)


def split3(w):
    high = w.astype(BF16).astype(F32)
    mid = (w - high).astype(BF16).astype(F32)
    return high, mid, w - high - mid


def weights_kernel(head, reg, band, band_t, rows):
    tap_count, hidden_count, channels = reg.shape
    planes = band.shape[0]
    rows[...] = jnp.zeros_like(rows)
    for t in range(tap_count):
        row = head[0] * reg[t, 0:1, :].astype(F32)
        for r in range(1, hidden_count):
            row = row + head[r] * reg[t, r : r + 1, :].astype(F32)
        rows[t : t + 1, 0:channels] = row
    columns = rows[...].T
    lane = lax.broadcasted_iota(jnp.int32, (channels, BLK), 1)
    part = lane // planes
    score = lane % planes
    weights = []
    for t in range(tap_count):
        high, mid, low = split3(
            jnp.broadcast_to(columns[0:channels, t : t + 1], (channels, BLK))
        )
        weights.append(jnp.where(part < 2, high, jnp.where(part == 2, mid, low)))
    for d in range(planes):
        tile = jnp.zeros((channels, BLK), F32)
        for t in range(tap_count):
            tile = jnp.where(score == d - t + 1, weights[t], tile)
        band[d] = tile.astype(BF16)
    per_tile = BLK // channels
    for k in range(planes // per_tile):
        tile = band[k * per_tile : (k + 1) * per_tile].reshape(BLK, BLK)
        band_t[:, k * BLK : (k + 1) * BLK] = tile.astype(F32).T.astype(BF16)


def stage_kernel(features, views, features_out, views_out, sems):
    copies = [
        pltpu.make_async_copy(features, features_out, sems.at[0]),
        pltpu.make_async_copy(views, views_out, sems.at[1]),
    ]
    for copy in copies:
        copy.start()
    for copy in copies:
        copy.wait()


def side():
    return (lax.axis_index("frame") + lax.axis_index("tile")) % 2


def at_end():
    tile = lax.axis_index("tile")
    return jnp.where(side() == 0, tile == 0, tile == lax.axis_size("tile") - 1)


def halve_kernel(mine, partner, out):
    half = out.shape[1]

    def copy(start):
        for g, tile in enumerate((mine, partner)):
            for q in range(half):
                at = (start + q) * BLK
                out[g, q] = tile[0, :, at : at + BLK]

    pl.when(side() == 0)(lambda: copy(0))
    pl.when(side() == 1)(lambda: copy(half))


def rim_kernel(*refs):
    pieces, (outer, inner) = refs[:-2], refs[-2:]
    half = pieces[0].shape[1]
    left, right = slice(0, HB), slice(half - HB, half)

    def copy(out, part):
        for i, piece in enumerate(pieces):
            out[2 * i : 2 * i + 2] = piece[:, part]

    @pl.when(side() == 0)
    def _():
        copy(outer, left)
        copy(inner, right)

    @pl.when(side() == 1)
    def _():
        copy(outer, right)
        copy(inner, left)


def depth_kernel(views, offsets, offsets_partner, outer, inner, kernels, band, band_t, cot, cot_partner, *refs):
    (
        depth, depth_partner, core_grad, grad_outer, grad_inner,
        src, base, shifted, means, volume, ref_grad, sums, matrices, arrived,
    ) = refs[-14 - 2 * V : -2 * V]
    pieces, grads = refs[: -14 - 2 * V], refs[-2 * V :]
    slots, half = core_grad.shape[:2]
    channels, pixels = base.shape
    planes = kernels.shape[0]
    span = half + 2 * HB
    share = 1.0 / (V + 1)
    chunk = planes // CHUNKS
    me = lax.axis_index("frame")
    right_half = side()
    first_block = right_half * half
    where = (offsets, offsets_partner)
    columns = [(g, b) for g in range(2) for b in range(half)]

    def load(k):
        part = pl.ds(k * chunk, chunk)
        return pltpu.make_async_copy(kernels.at[part], matrices.at[part], arrived.at[k])

    for k in range(CHUNKS):
        load(k).start()

    def rims(near, far):
        for r in range(slots):
            src[r * span + near : r * span + near + HB] = outer[r]
            src[r * span + far : r * span + far + HB] = inner[r ^ 1]

    pl.when(right_half == 0)(lambda: rims(0, HB + half))
    pl.when(right_half == 1)(lambda: rims(HB + half, 0))

    @pl.when(at_end())
    def _():
        near = jnp.where(right_half == 0, 0, HB + half)
        for r in range(slots):
            for q in range(HB):
                src[r * span + q + near] = jnp.zeros((channels, BLK), BF16)

    for r in range(slots):
        src[r * span + HB : r * span + HB + half] = pieces[r // 2][r % 2]
    for k, (g, b) in enumerate(columns):
        base[:, k * BLK : (k + 1) * BLK] = pieces[0][g, b].astype(F32)
    for grad in grads:
        grad[...] = jnp.zeros_like(grad)
    ref_grad[...] = jnp.zeros_like(ref_grad)
    sums[...] = jnp.zeros_like(sums)
    slot_of = [[views[j, me ^ g] ^ me for j in range(V)] for g in range(2)]

    def rows_of(k, j):
        start = (k * V + j) * channels
        return slice(start, start + channels)

    def block_of(d, g, b, j):
        return where[g][0, j, first_block + b, d] + (b + HB)

    def forward(d):
        picked = []
        for g, b in columns:
            for j in range(V):
                picked.append(src[slot_of[g][j] * span + block_of(d, g, b, j)])
        warped = jnp.dot(
            jnp.concatenate(picked, axis=0), matrices[d], preferred_element_type=F32
        )
        for k in range(len(columns)):
            lanes = slice(k * BLK, (k + 1) * BLK)
            first = base[:, lanes]
            ys = [warped[rows_of(k, j)] - first for j in range(V)]
            for j in range(V):
                shifted[d, j, :, lanes] = ys[j]
            total = (ys[0] + ys[1]) + (ys[2] + ys[3])
            mean = total * share
            squares = (ys[0] * ys[0] + ys[1] * ys[1]) + (ys[2] * ys[2] + ys[3] * ys[3])
            variance = (squares - total * mean) * share
            volume[d, :, lanes] = variance.astype(BF16)
            means[d, :, lanes] = mean + (total - (V + 1) * mean) * share

    def forward_chunk(k, carry):
        load(k).wait()
        for i in range(chunk):
            forward(k * chunk + i)
        return carry

    lax.fori_loop(0, CHUNKS, forward_chunk, 0)

    wide = BLK * (2 if half % 2 == 0 else 1)
    groups = [slice(i, i + wide) for i in range(0, pixels, wide)]
    values = (
        lax.broadcasted_iota(jnp.int32, (planes, wide), 0).astype(F32) + 1.0
    ) / planes
    raws = []
    for lanes in groups:
        parts = jnp.dot(
            band_t[...], volume[:, :, lanes].reshape(planes * channels, wide),
            preferred_element_type=F32,
        )
        raws.append(
            parts[0:planes]
            + (parts[2 * planes : 3 * planes] + parts[3 * planes : 4 * planes])
        )
    stacks = []
    per_frame = half * BLK // wide
    for i, raw in enumerate(raws):
        given, out = ((cot, depth), (cot_partner, depth_partner))[i // per_frame]
        at = (i % per_frame) * wide
        slope_in = given[0:1, pl.ds(pl.multiple_of(first_block * BLK + at, BLK), wide)]
        tanh = jnp.tanh(raw)
        weights = jnp.exp(4.0 * tanh)
        norm = jnp.sum(weights, axis=0, keepdims=True)
        result = jnp.sum(weights * values, axis=0, keepdims=True) / norm
        out[0:1, at : at + wide] = result
        slope = (slope_in / norm) * (values - result) * weights
        draw = slope * (4.0 * (1.0 - tanh * tanh))
        high = draw.astype(BF16)
        low = (draw - high.astype(F32)).astype(BF16)
        stacks.append(jnp.concatenate([high, low, high, high], axis=0))
    for lanes, stack in zip(groups, stacks):
        dvolume = jnp.dot(
            band[...].reshape(planes * channels, BLK), stack, preferred_element_type=F32
        )
        volume[:, :, lanes] = dvolume.astype(BF16).reshape(planes, channels, wide)

    def backward(d, carry):
        rows = []
        for k in range(len(columns)):
            lanes = slice(k * BLK, (k + 1) * BLK)
            dvar = volume[d, :, lanes].astype(F32)
            mean = means[d, :, lanes]
            ref_grad[:, lanes] -= dvar * mean
            for j in range(V):
                rows.append((dvar * (shifted[d, j, :, lanes] - mean)).astype(BF16))
        dpicked = lax.dot_general(
            jnp.concatenate(rows, axis=0), matrices[d],
            (((1,), (1,)), ((), ())), preferred_element_type=F32,
        )
        for k, (g, b) in enumerate(columns):
            for j in range(V):
                grads[g * V + j][block_of(d, g, b, j)] += dpicked[rows_of(k, j)]
        return carry

    lax.fori_loop(0, planes, backward, 0, unroll=UNROLL)

    scale = 2.0 * share
    for k, (g, b) in enumerate(columns):
        sums[g, HB + b] = ref_grad[:, k * BLK : (k + 1) * BLK]
    for g in range(2):
        for j in range(V):
            sums[slot_of[g][j]] += grads[g * V + j][...]
    core_grad[...] = sums[:, HB : HB + half] * scale

    def give(left, right):
        left[...] = (sums[:, 0:HB] * scale).astype(BF16)
        right[...] = (sums[:, HB + half :] * scale).astype(BF16)

    pl.when(right_half == 0)(lambda: give(grad_outer, grad_inner))
    pl.when(right_half == 1)(lambda: give(grad_inner, grad_outer))


def merge_kernel(core, outer, inner, own, *sent):
    slots, half = core.shape[:2]

    def merge(near, far, beyond):
        for r in range(slots):
            out = own if r < 2 else sent[r // 2 - 1]
            for q in range(half):
                tile = core[r, q]
                if beyond and near <= q < near + HB:
                    tile = tile + outer[r, q - near].astype(F32)
                if far <= q < far + HB:
                    tile = tile + inner[r ^ 1, q - far].astype(F32)
                out[r % 2, q] = tile.astype(out.dtype)

    for i, ends in enumerate(((0, half - HB), (half - HB, 0))):
        here = side() == i
        pl.when(here & at_end())(lambda ends=ends: merge(*ends, False))
        pl.when(here & jnp.logical_not(at_end()))(lambda ends=ends: merge(*ends, True))


def sum_kernel(own, *refs):
    received, (mine, partner) = refs[:-2], refs[-2:]
    for g, out in enumerate((mine, partner)):
        total = own[g]
        for piece in received:
            total = total + piece[g].astype(F32)
        out[...] = total


def join_kernel(mine, partner, depth_mine, depth_partner, grad, depth):
    half = mine.shape[0]

    def join(at, tile, part):
        for q in range(half):
            grad[0, :, (at + q) * BLK : (at + q + 1) * BLK] = tile[q]
        depth[:, at * BLK : (at + half) * BLK] = part[...]

    @pl.when(side() == 0)
    def _():
        join(0, mine, depth_mine)
        join(half, partner, depth_partner)

    @pl.when(side() == 1)
    def _():
        join(0, partner, depth_partner)
        join(half, mine, depth_mine)


def exchange(x, distance):
    count = lax.axis_size("frame")
    return lax.ppermute(x, "frame", [(i, i ^ distance) for i in range(count)])


def swap_outer(x):
    count, tiles = lax.axis_size("frame"), lax.axis_size("tile")
    pairs = [
        (f * tiles + t, f * tiles + t + 1)
        for f in range(count)
        for t in range(tiles - 1)
        if (f + t) % 2 == 1
    ]
    ends = [(f, 0) for f in range(count) if f % 2 == 0]
    ends += [(f, tiles - 1) for f in range(count) if (f + tiles - 1) % 2 == 1]
    if count >= 4:
        pairs += [(f * tiles + t, (f ^ 2) * tiles + t) for f, t in ends if f & 2 == 0]
    return lax.ppermute(x, ("frame", "tile"), pairs + [(b, a) for a, b in pairs])


def small_call(kernel, ins, outs, scratch=()):
    return pl.pallas_call(
        kernel, out_shape=outs, in_specs=ins, out_specs=jax.tree.map(lambda _: VMEM, outs),
        scratch_shapes=scratch, compiler_params=SMALL,
    )


def per_device(features, views, offsets, kernels, reg_weight, head_weight, depth_cot):
    local_frames, channels, pixels = features.shape
    frames = lax.axis_size("frame")
    half = pixels // BLK // 2
    planes = kernels.shape[0]
    assert local_frames == 1 and frames & (frames - 1) == 0
    assert pixels == 2 * half * BLK and half >= HB
    shape = jax.ShapeDtypeStruct
    rim_shape = shape((frames, HB, channels, BLK), BF16)
    pair_shape = shape((2, half, channels, BLK), BF16)
    half_shape = shape((half, channels, BLK), F32)
    views = views.T
    offsets = jnp.swapaxes(offsets, 2, 3)

    band, band_t = small_call(
        weights_kernel, [SMEM, VMEM],
        (shape((planes, channels, BLK), BF16), shape((BLK, planes * channels), BF16)),
        [pltpu.VMEM((BLK, BLK), F32)],
    )(head_weight, reg_weight)

    features_partner = exchange(features, 1)
    staged, views = pl.pallas_call(
        stage_kernel,
        out_shape=(shape(features.shape, features.dtype), shape(views.shape, views.dtype)),
        in_specs=[pl.BlockSpec(memory_space=pltpu.HBM)] * 2,
        out_specs=(VMEM, VMEM),
        scratch_shapes=[pltpu.SemaphoreType.DMA((2,))],
        compiler_params=SMALL,
        name="stage_arguments",
    )(*(pltpu.with_memory_space_constraint(x, pltpu.HBM) for x in (features, views)))
    offsets_partner = exchange(offsets, 1)
    cot_partner = exchange(depth_cot, 1)
    pieces = [small_call(halve_kernel, [VMEM] * 2, pair_shape)(staged, features_partner)]
    for r in range(2, frames, 2):
        pieces.append(exchange(pieces[0], r))
    outer, inner = small_call(rim_kernel, [VMEM] * (frames // 2), (rim_shape, rim_shape))(*pieces)
    inner = exchange(inner, 1)
    outer = swap_outer(outer)

    span = half + 2 * HB
    depth_half = shape((1, half * BLK), F32)
    depth, depth_partner, core_grad, outer, inner = pl.pallas_call(
        depth_kernel,
        out_shape=(
            depth_half, depth_half, shape((frames, half, channels, BLK), F32), rim_shape, rim_shape,
        ),
        in_specs=[SMEM] * 3
        + [VMEM] * 2
        + [pl.BlockSpec(memory_space=pltpu.HBM)]
        + [VMEM] * (4 + frames // 2),
        out_specs=(VMEM,) * 5,
        scratch_shapes=[
            pltpu.VMEM((frames * span, channels, BLK), BF16),
            pltpu.VMEM((channels, pixels), F32),
            pltpu.VMEM((planes, V, channels, pixels), F32),
            pltpu.VMEM((planes, channels, pixels), F32),
            pltpu.VMEM((planes, channels, pixels), BF16),
            pltpu.VMEM((channels, pixels), F32),
            pltpu.VMEM((frames, span, channels, BLK), F32),
            pltpu.VMEM((planes, BLK, BLK), BF16),
            pltpu.SemaphoreType.DMA((CHUNKS,)),
        ]
        + [pltpu.VMEM((span, channels, BLK), F32)] * (2 * V),
        compiler_params=pltpu.CompilerParams(vmem_limit_bytes=34 << 20),
        cost_estimate=pl.CostEstimate(
            flops=4 * planes * V * channels * pixels * BLK, bytes_accessed=4 << 20,
            transcendentals=2 * planes * pixels,
        ),
        name="depth_window",
    )(
        views, offsets, offsets_partner, outer, inner,
        pltpu.with_memory_space_constraint(kernels, pltpu.HBM), band, band_t,
        depth_cot, cot_partner, *pieces,
    )

    inner = exchange(inner, 1)
    outer = swap_outer(outer)
    depth_partner = exchange(depth_partner, 1)
    own, *sent = small_call(
        merge_kernel, [VMEM] * 3,
        (shape(pair_shape.shape, F32),) + (pair_shape,) * (frames // 2 - 1),
    )(core_grad, outer, inner)
    received = []
    for r, piece in zip(range(2, frames, 2), sent):
        received.append(exchange(piece, r))
    mine, partner = small_call(
        sum_kernel, [VMEM] * (frames // 2), (half_shape, half_shape)
    )(own, *received)
    grad, depth = small_call(
        join_kernel, [VMEM] * 4,
        (shape(features.shape, F32), shape(depth_cot.shape, F32)),
    )(mine, exchange(partner, 1), depth, depth_partner)
    return depth, grad


def solution(mesh):
    return jax.shard_map(
        per_device,
        mesh=mesh,
        in_specs=(
            P("frame", None, "tile"),
            P(),
            P("frame", None, None, "tile"),
            P(),
            P(),
            P(),
            P("frame", "tile"),
        ),
        out_specs=(P("frame", "tile"), P("frame", None, "tile")),
        check_vma=False,
    )
```

time: 48.4 us -> 43.1 us (0.89)
  the two profiles are of different devices: /device:TPU:16 before, /device:TPU:0 now
where the time goes in v3:
time: 43.1 us; the launch traced here: 42.9 us
  waiting for transfers between devices  15.8 us (37%)
  Pallas kernels  14.9 us (35%)
  starting transfers between devices  11.4 us (26%)
  between operations  0.73 us (2%)
    pallas_call x1, Pallas kernels, per_device(): pl.pallas_call(depth_kernel, out_shape=(depth_half, depth_half, shape((fr...  12.4 us
    ppermute x13, starting transfers between devices, exchange(): return lax.ppermute(x, 'frame', [(i, i ^ distance) for i in range(count)])  9.75 us
    ppermute x13, waiting for transfers between devices, exchange(): return lax.ppermute(x, 'frame', [(i, i ^ distance) for i in range(count)])  9.09 us
    ppermute x2, waiting for transfers between devices, swap_outer(): lax.ppermute(x, ('frame', 'tile'), pairs + [(b, a) for a, b in pairs])  6.69 us
    ppermute x2, starting transfers between devices, swap_outer(): lax.ppermute(x, ('frame', 'tile'), pairs + [(b, a) for a, b in pairs])  1.67 us
    pallas_call x1, Pallas kernels, per_device(): small_call(weights_kernel, [SMEM, VMEM], (shape((planes, channels, BLK),...  0.86 us
  transfers between devices with their start and end apart: 15, of which 11 were waited for; matrix products, arithmetic and copies ran while one was open for 0% of the time, Pallas kernels for 4%

profile of v3, /device:TPU:0, one launch (start us, length us, event | category | flops | bytes accessed | tf_op | source)
XLA Modules:
  0.0 42.9 jit_solution(6423702487543773020)
XLA Ops:
  0.6 0.6 %collective-permute-start.1 = (bf16[1,32,1024]{2,1,0:T(8,128)(2,1)}, bf16[1,32,1024]{2,1,0:T(8,128)(2,1)S(1)}, u32[]{:S(2)}, u32[]{:S(2)}) collective-permute-start(bf16[1,32,1024]{2,1,0:T(8,128)(2,1)} %features.1), channel_id=1, source_target_pairs={{0,4},{4,0},{8,12},{12,8},{16,20},{20,16},{24,28},{28,24},{1,5},{5... | collective-permute-start | bytes 196616 | tf_op jit(solution)/shard_map/ppermute | solution.py:319
  1.2 0.9 %stage_arguments.1 = (bf16[1,32,1024]{2,1,0:T(8,128)(2,1)S(1)}, s32[4,8]{1,0:T(4,128)S(1)}) custom-call(bf16[1,32,1024]{2,1,0:T(8,128)(2,1)} %features.1, s32[4,8]{1,0:T(4,128)} %bitcast.4), custom_call_target="tpu_custom_call" | custom-call | tf_op jit(solution)/shard_map/stage_arguments/pallas_call | solution.py:365
  2.1 0.2 collective-permute-done.1.partner
  2.3 3.8 %collective-permute-start.4 = (bf16[2,4,32,128]{3,2,1,0:T(8,128)(2,1)S(1)}, bf16[2,4,32,128]{3,2,1,0:T(8,128)(2,1)S(1)}, u32[]{:S(2)}, u32[]{:S(2)}) collective-permute-start(bf16[2,4,32,128]{3,2,1,0:T(8,128)(2,1)S(1)} %shard_map.86.refs_0_), channel_id=1, source_target_pairs={{0,24},{4,28},{8,16},{12,20},{16,8},{20,12},{24,0},{28,4},{1,25},{... | collective-permute-start | bytes 196616 | tf_op jit(solution)/shard_map/ppermute | solution.py:319
  6.2 0.5 %collective-permute-start.3 = (bf16[2,4,32,128]{3,2,1,0:T(8,128)(2,1)S(1)}, bf16[2,4,32,128]{3,2,1,0:T(8,128)(2,1)S(1)}, u32[]{:S(2)}, u32[]{:S(2)}) collective-permute-start(bf16[2,4,32,128]{3,2,1,0:T(8,128)(2,1)S(1)} %shard_map.86.refs_0_), channel_id=1, source_target_pairs={{0,16},{4,20},{8,24},{12,28},{16,0},{20,4},{24,8},{28,12},{1,17},{... | collective-permute-start | bytes 196616 | tf_op jit(solution)/shard_map/ppermute | solution.py:319
  6.8 1.8 %collective-permute-done.4.refs_3_ = bf16[2,4,32,128]{3,2,1,0:T(8,128)(2,1)S(1)} collective-permute-done((bf16[2,4,32,128]{3,2,1,0:T(8,128)(2,1)S(1)}, bf16[2,4,32,128]{3,2,1,0:T(8,128)(2,1)S(1)}, u32[]{:S(2)}, u32[]{:S(2)}) %collective-permute-start.4) | collective-permute-done | bytes 65568 | tf_op jit(solution)/shard_map/ppermute | solution.py:319
  8.6 1.9 %collective-permute-done.3.refs_2_ = bf16[2,4,32,128]{3,2,1,0:T(8,128)(2,1)S(1)} collective-permute-done((bf16[2,4,32,128]{3,2,1,0:T(8,128)(2,1)S(1)}, bf16[2,4,32,128]{3,2,1,0:T(8,128)(2,1)S(1)}, u32[]{:S(2)}, u32[]{:S(2)}) %collective-permute-start.3) | collective-permute-done | bytes 65568 | tf_op jit(solution)/shard_map/ppermute | solution.py:319
  10.5 0.5 %collective-permute-done.2.refs_1_ = bf16[2,4,32,128]{3,2,1,0:T(8,128)(2,1)S(1)} collective-permute-done((bf16[2,4,32,128]{3,2,1,0:T(8,128)(2,1)S(1)}, bf16[2,4,32,128]{3,2,1,0:T(8,128)(2,1)S(1)}, u32[]{:S(2)}, u32[]{:S(2)}) %collective-permute-start.2) | collective-permute-done | bytes 65568 | tf_op jit(solution)/shard_map/ppermute | solution.py:319
  11.0 0.8 %collective-permute-start.5 = (bf16[8,2,32,128]{3,2,1,0:T(8,128)(2,1)S(1)}, bf16[8,2,32,128]{3,2,1,0:T(8,128)(2,1)S(1)}, u32[]{:S(2)}, u32[]{:S(2)}) collective-permute-start(bf16[8,2,32,128]{3,2,1,0:T(8,128)(2,1)S(1)} %get-tuple-element.23), channel_id=1, source_target_pairs={{1,2},{4,5},{6,7},{9,10},{12,13},{14,15},{17,18},{20,21},{22,23},{... | collective-permute-start | bytes 393224 | tf_op jit(solution)/shard_map/ppermute | solution.py:334
  11.9 0.5 %collective-permute-start.7 = (f32[1,1024]{1,0:T(1,128)S(1)}, f32[1,1024]{1,0:T(1,128)S(1)}, u32[]{:S(2)}, u32[]{:S(2)}) collective-permute-start(f32[1,1024]{1,0:T(1,128)S(1)} %copy-done.3), channel_id=1, source_target_pairs={{0,4},{4,0},{8,12},{12,8},{16,20},{20,16},{24,28},{28,24},{1,5},{5... | collective-permute-start | bytes 12296 | tf_op jit(solution)/shard_map/ppermute | solution.py:319
  12.5 0.9 %shard_map.88 = (bf16[32,32,128]{2,1,0:T(8,128)(2,1)S(1)}, bf16[128,1024]{1,0:T(8,128)(2,1)S(1)}) custom-call(f32[8]{0:T(128)S(1)} %copy-done.1, bf16[3,8,32]{2,1,0:T(8,128)(2,1)S(1)} %copy-done), custom_call_target="tpu_custom_call" | custom-call | tf_op jit(solution)/shard_map/pallas_call | solution.py:358
  13.5 2.5 %collective-permute-done.5.outer = bf16[8,2,32,128]{3,2,1,0:T(8,128)(2,1)S(1)} collective-permute-done((bf16[8,2,32,128]{3,2,1,0:T(8,128)(2,1)S(1)}, bf16[8,2,32,128]{3,2,1,0:T(8,128)(2,1)S(1)}, u32[]{:S(2)}, u32[]{:S(2)}) %collective-permute-start.5) | collective-permute-done | bytes 131104 | tf_op jit(solution)/shard_map/ppermute | solution.py:334
  16.0 12.4 %depth_window.1 = (f32[1,512]{1,0:T(1,128)S(1)}, f32[1,512]{1,0:T(1,128)S(1)}, f32[8,4,32,128]{3,2,1,0:T(8,128)S(1)}, bf16[8,2,32,128]{3,2,1,0:T(8,128)(2,1)S(1)}, bf16[8,2,32,128]{3,2,1,0:T(8,128)(2,1)S(1)}) custom-call(s32[4,8]{1,0:T(4,128)S(1)} %get-tuple-element.21.views, s32[1,4,8,32]{3,2,1,0:T(8,128)S(1)} %bitcast.3, ...), custom_call_target="tpu_custom_call" | custom-call | flops 2147483648 | bytes 4194304 | tf_op jit(solution)/shard_map/depth_window/pallas_call | solution.py:385
  28.4 0.8 %collective-permute-start.8 = (bf16[8,2,32,128]{3,2,1,0:T(8,128)(2,1)S(1)}, bf16[8,2,32,128]{3,2,1,0:T(8,128)(2,1)S(1)}, u32[]{:S(2)}, u32[]{:S(2)}) collective-permute-start(bf16[8,2,32,128]{3,2,1,0:T(8,128)(2,1)S(1)} %get-tuple-element.28), channel_id=1, source_target_pairs={{1,2},{4,5},{6,7},{9,10},{12,13},{14,15},{17,18},{20,21},{22,23},{... | collective-permute-start | bytes 393224 | tf_op jit(solution)/shard_map/ppermute | solution.py:334
  29.2 4.2 %collective-permute-done.8.outer = bf16[8,2,32,128]{3,2,1,0:T(8,128)(2,1)S(1)} collective-permute-done((bf16[8,2,32,128]{3,2,1,0:T(8,128)(2,1)S(1)}, bf16[8,2,32,128]{3,2,1,0:T(8,128)(2,1)S(1)}, u32[]{:S(2)}, u32[]{:S(2)}) %collective-permute-start.8) | collective-permute-done | bytes 131104 | tf_op jit(solution)/shard_map/ppermute | solution.py:334
  33.5 0.8 %collective-permute-start.10 = (bf16[2,4,32,128]{3,2,1,0:T(8,128)(2,1)S(1)}, bf16[2,4,32,128]{3,2,1,0:T(8,128)(2,1)S(1)}, u32[]{:S(2)}, u32[]{:S(2)}) collective-permute-start(bf16[2,4,32,128]{3,2,1,0:T(8,128)(2,1)S(1)} %get-tuple-element.31), channel_id=1, source_target_pairs={{0,8},{4,12},{8,0},{12,4},{16,24},{20,28},{24,16},{28,20},{1,9},{5... | collective-permute-start | bytes 196616 | tf_op jit(solution)/shard_map/ppermute | solution.py:319
  34.3 1.3 %collective-permute-start.11 = (bf16[2,4,32,128]{3,2,1,0:T(8,128)(2,1)S(1)}, bf16[2,4,32,128]{3,2,1,0:T(8,128)(2,1)S(1)}, u32[]{:S(2)}, u32[]{:S(2)}) collective-permute-start(bf16[2,4,32,128]{3,2,1,0:T(8,128)(2,1)S(1)} %get-tuple-element.32), channel_id=1, source_target_pairs={{0,16},{4,20},{8,24},{12,28},{16,0},{20,4},{24,8},{28,12},{1,17},{... | collective-permute-start | bytes 196616 | tf_op jit(solution)/shard_map/ppermute | solution.py:319
  35.6 1.4 %collective-permute-start.12 = (bf16[2,4,32,128]{3,2,1,0:T(8,128)(2,1)S(1)}, bf16[2,4,32,128]{3,2,1,0:T(8,128)(2,1)S(1)}, u32[]{:S(2)}, u32[]{:S(2)}) collective-permute-start(bf16[2,4,32,128]{3,2,1,0:T(8,128)(2,1)S(1)} %get-tuple-element.33), channel_id=1, source_target_pairs={{0,24},{4,28},{8,16},{12,20},{16,8},{20,12},{24,0},{28,4},{1,25},{... | collective-permute-start | bytes 196616 | tf_op jit(solution)/shard_map/ppermute | solution.py:319
  37.1 0.8 %collective-permute-done.10.refs_0_ = bf16[2,4,32,128]{3,2,1,0:T(8,128)(2,1)S(1)} collective-permute-done((bf16[2,4,32,128]{3,2,1,0:T(8,128)(2,1)S(1)}, bf16[2,4,32,128]{3,2,1,0:T(8,128)(2,1)S(1)}, u32[]{:S(2)}, u32[]{:S(2)}) %collective-permute-start.10) | collective-permute-done | bytes 65568 | tf_op jit(solution)/shard_map/ppermute | solution.py:319
  37.9 0.8 %collective-permute-done.11.refs_1_ = bf16[2,4,32,128]{3,2,1,0:T(8,128)(2,1)S(1)} collective-permute-done((bf16[2,4,32,128]{3,2,1,0:T(8,128)(2,1)S(1)}, bf16[2,4,32,128]{3,2,1,0:T(8,128)(2,1)S(1)}, u32[]{:S(2)}, u32[]{:S(2)}) %collective-permute-start.11) | collective-permute-done | bytes 65568 | tf_op jit(solution)/shard_map/ppermute | solution.py:319
  38.6 2.2 %collective-permute-done.12.refs_2_ = bf16[2,4,32,128]{3,2,1,0:T(8,128)(2,1)S(1)} collective-permute-done((bf16[2,4,32,128]{3,2,1,0:T(8,128)(2,1)S(1)}, bf16[2,4,32,128]{3,2,1,0:T(8,128)(2,1)S(1)}, u32[]{:S(2)}, u32[]{:S(2)}) %collective-permute-start.12) | collective-permute-done | bytes 65568 | tf_op jit(solution)/shard_map/ppermute | solution.py:319
  40.9 0.5 %collective-permute-start.14 = (f32[1,512]{1,0:T(1,128)S(1)}, f32[1,512]{1,0:T(1,128)S(1)}, u32[]{:S(2)}, u32[]{:S(2)}) collective-permute-start(f32[1,512]{1,0:T(1,128)S(1)} %get-tuple-element.37), channel_id=1, source_target_pairs={{0,4},{4,0},{8,12},{12,8},{16,20},{20,16},{24,28},{28,24},{1,5},{5... | collective-permute-start | bytes 6152 | tf_op jit(solution)/shard_map/ppermute | solution.py:319
  41.4 0.8 %collective-permute-done.14.depth_partner = f32[1,512]{1,0:T(1,128)S(1)} collective-permute-done((f32[1,512]{1,0:T(1,128)S(1)}, f32[1,512]{1,0:T(1,128)S(1)}, u32[]{:S(2)}, u32[]{:S(2)}) %collective-permute-start.14) | collective-permute-done | bytes 2080 | tf_op jit(solution)/shard_map/ppermute | solution.py:319
  42.2 0.7 %shard_map.91 = (f32[1,32,1024]{2,1,0:T(8,128)}, f32[1,1024]{1,0:T(1,128)}) custom-call(f32[4,32,128]{2,1,0:T(8,128)S(1)} %get-tuple-element.34.mine, f32[4,32,128]{2,1,0:T(8,128)S(1)} %collective-permute-done.13.partner, f32[1,512]{1,0:T(1,128)S(1)} %get-tuple-element.36.depth_mine, f32[1,512]{1,0:T(1,128)S(1)} %collective-permute-done.14.depth_partner), custom_call_target="tpu_custom_call" | custom-call | tf_op jit(solution)/shard_map/pallas_call | solution.py:432
  (22 shorter events, 0.7 us)
Async XLA Ops:
  0.6 1.7 %collective-permute-start.1 = (bf16[1,32,1024]{2,1,0:T(8,128)(2,1)}, bf16[1,32,1024]{2,1,0:T(8,128)(2,1)S(1)}, u32[]{:S(2)}, u32[]{:S(2)}) collective-permute-start(bf16[1,32,1024]{2,1,0:T(8,128)(2,1)} %features.1), channel_id=1, source_target_pairs={{0,4},{4,0},{8,12},{12,8},{16,20},{20,16},{24,28},{28,24},{1,5},{5... | collective-permute-start | bytes 196616 | tf_op jit(solution)/shard_map/ppermute | solution.py:319
  2.3 9.5 %copy-start.3 = (f32[1,1024]{1,0:T(1,128)S(1)}, f32[1,1024]{1,0:T(1,128)}, u32[]{:S(2)}) copy-start(f32[1,1024]{1,0:T(1,128)} %cot.1) | copy-start | bytes 12292
  2.3 10.0 %copy-start.2 = (s32[1,4,32,8]{2,3,1,0:T(8,128)S(1)}, s32[1,4,32,8]{2,3,1,0:T(8,128)}, u32[]{:S(2)}) copy-start(s32[1,4,32,8]{2,3,1,0:T(8,128)} %param.9) | copy-start | bytes 12292
  2.3 6.3 %collective-permute-start.4 = (bf16[2,4,32,128]{3,2,1,0:T(8,128)(2,1)S(1)}, bf16[2,4,32,128]{3,2,1,0:T(8,128)(2,1)S(1)}, u32[]{:S(2)}, u32[]{:S(2)}) collective-permute-start(bf16[2,4,32,128]{3,2,1,0:T(8,128)(2,1)S(1)} %shard_map.86.refs_0_), channel_id=1, source_target_pairs={{0,24},{4,28},{8,16},{12,20},{16,8},{20,12},{24,0},{28,4},{1,25},{... | collective-permute-start | bytes 196616 | tf_op jit(solution)/shard_map/ppermute | solution.py:319
  6.2 4.3 %collective-permute-start.3 = (bf16[2,4,32,128]{3,2,1,0:T(8,128)(2,1)S(1)}, bf16[2,4,32,128]{3,2,1,0:T(8,128)(2,1)S(1)}, u32[]{:S(2)}, u32[]{:S(2)}) collective-permute-start(bf16[2,4,32,128]{3,2,1,0:T(8,128)(2,1)S(1)} %shard_map.86.refs_0_), channel_id=1, source_target_pairs={{0,16},{4,20},{8,24},{12,28},{16,0},{20,4},{24,8},{28,12},{1,17},{... | collective-permute-start | bytes 196616 | tf_op jit(solution)/shard_map/ppermute | solution.py:319
  6.7 4.3 %collective-permute-start.2 = (bf16[2,4,32,128]{3,2,1,0:T(8,128)(2,1)S(1)}, bf16[2,4,32,128]{3,2,1,0:T(8,128)(2,1)S(1)}, u32[]{:S(2)}, u32[]{:S(2)}) collective-permute-start(bf16[2,4,32,128]{3,2,1,0:T(8,128)(2,1)S(1)} %shard_map.86.refs_0_), channel_id=1, source_target_pairs={{0,8},{4,12},{8,0},{12,4},{16,24},{20,28},{24,16},{28,20},{1,9},{5... | collective-permute-start | bytes 196616 | tf_op jit(solution)/shard_map/ppermute | solution.py:319
  11.0 1.5 %copy-start = (bf16[3,8,32]{2,1,0:T(8,128)(2,1)S(1)}, bf16[3,8,32]{2,1,0:T(8,128)(2,1)}, u32[]{:S(2)}) copy-start(bf16[3,8,32]{2,1,0:T(8,128)(2,1)} %reg.1) | copy-start | bytes 4612
  11.0 5.0 %collective-permute-start.5 = (bf16[8,2,32,128]{3,2,1,0:T(8,128)(2,1)S(1)}, bf16[8,2,32,128]{3,2,1,0:T(8,128)(2,1)S(1)}, u32[]{:S(2)}, u32[]{:S(2)}) collective-permute-start(bf16[8,2,32,128]{3,2,1,0:T(8,128)(2,1)S(1)} %get-tuple-element.23), channel_id=1, source_target_pairs={{1,2},{4,5},{6,7},{9,10},{12,13},{14,15},{17,18},{20,21},{22,23},{... | collective-permute-start | bytes 393224 | tf_op jit(solution)/shard_map/ppermute | solution.py:334
  11.8 0.7 %copy-start.1 = (f32[8]{0:T(128)S(1)}, f32[8]{0:T(128)}, u32[]{:S(2)}) copy-start(f32[8]{0:T(128)} %head.1) | copy-start | bytes 100
  11.8 4.2 %collective-permute-start.6 = (bf16[8,2,32,128]{3,2,1,0:T(8,128)(2,1)S(1)}, bf16[8,2,32,128]{3,2,1,0:T(8,128)(2,1)S(1)}, u32[]{:S(2)}, u32[]{:S(2)}) collective-permute-start(bf16[8,2,32,128]{3,2,1,0:T(8,128)(2,1)S(1)} %get-tuple-element.24), channel_id=1, source_target_pairs={{0,4},{4,0},{8,12},{12,8},{16,20},{20,16},{24,28},{28,24},{1,5},{5... | collective-permute-start | bytes 393224 | tf_op jit(solution)/shard_map/ppermute | solution.py:319
  11.9 1.5 %collective-permute-start.7 = (f32[1,1024]{1,0:T(1,128)S(1)}, f32[1,1024]{1,0:T(1,128)S(1)}, u32[]{:S(2)}, u32[]{:S(2)}) collective-permute-start(f32[1,1024]{1,0:T(1,128)S(1)} %copy-done.3), channel_id=1, source_target_pairs={{0,4},{4,0},{8,12},{12,8},{16,20},{20,16},{24,28},{28,24},{1,5},{5... | collective-permute-start | bytes 12296 | tf_op jit(solution)/shard_map/ppermute | solution.py:319
  12.4 1.2 %collective-permute-start = (s32[1,4,8,32]{3,2,1,0:T(8,128)S(1)}, s32[1,4,8,32]{3,2,1,0:T(8,128)S(1)}, u32[]{:S(2)}, u32[]{:S(2)}) collective-permute-start(s32[1,4,8,32]{3,2,1,0:T(8,128)S(1)} %bitcast.2), channel_id=1, source_target_pairs={{0,4},{4,0},{8,12},{12,8},{16,20},{20,16},{24,28},{28,24},{1,5},{5... | collective-permute-start | bytes 12296 | tf_op jit(solution)/shard_map/ppermute | solution.py:319
  28.4 5.0 %collective-permute-start.8 = (bf16[8,2,32,128]{3,2,1,0:T(8,128)(2,1)S(1)}, bf16[8,2,32,128]{3,2,1,0:T(8,128)(2,1)S(1)}, u32[]{:S(2)}, u32[]{:S(2)}) collective-permute-start(bf16[8,2,32,128]{3,2,1,0:T(8,128)(2,1)S(1)} %get-tuple-element.28), channel_id=1, source_target_pairs={{1,2},{4,5},{6,7},{9,10},{12,13},{14,15},{17,18},{20,21},{22,23},{... | collective-permute-start | bytes 393224 | tf_op jit(solution)/shard_map/ppermute | solution.py:334
  29.2 4.2 %collective-permute-start.9 = (bf16[8,2,32,128]{3,2,1,0:T(8,128)(2,1)S(1)}, bf16[8,2,32,128]{3,2,1,0:T(8,128)(2,1)S(1)}, u32[]{:S(2)}, u32[]{:S(2)}) collective-permute-start(bf16[8,2,32,128]{3,2,1,0:T(8,128)(2,1)S(1)} %get-tuple-element.29), channel_id=1, source_target_pairs={{0,4},{4,0},{8,12},{12,8},{16,20},{20,16},{24,28},{28,24},{1,5},{5... | collective-permute-start | bytes 393224 | tf_op jit(solution)/shard_map/ppermute | solution.py:319
  33.5 4.3 %collective-permute-start.10 = (bf16[2,4,32,128]{3,2,1,0:T(8,128)(2,1)S(1)}, bf16[2,4,32,128]{3,2,1,0:T(8,128)(2,1)S(1)}, u32[]{:S(2)}, u32[]{:S(2)}) collective-permute-start(bf16[2,4,32,128]{3,2,1,0:T(8,128)(2,1)S(1)} %get-tuple-element.31), channel_id=1, source_target_pairs={{0,8},{4,12},{8,0},{12,4},{16,24},{20,28},{24,16},{28,20},{1,9},{5... | collective-permute-start | bytes 196616 | tf_op jit(solution)/shard_map/ppermute | solution.py:319
  34.3 4.3 %collective-permute-start.11 = (bf16[2,4,32,128]{3,2,1,0:T(8,128)(2,1)S(1)}, bf16[2,4,32,128]{3,2,1,0:T(8,128)(2,1)S(1)}, u32[]{:S(2)}, u32[]{:S(2)}) collective-permute-start(bf16[2,4,32,128]{3,2,1,0:T(8,128)(2,1)S(1)} %get-tuple-element.32), channel_id=1, source_target_pairs={{0,16},{4,20},{8,24},{12,28},{16,0},{20,4},{24,8},{28,12},{1,17},{... | collective-permute-start | bytes 196616 | tf_op jit(solution)/shard_map/ppermute | solution.py:319
  35.6 5.2 %collective-permute-start.12 = (bf16[2,4,32,128]{3,2,1,0:T(8,128)(2,1)S(1)}, bf16[2,4,32,128]{3,2,1,0:T(8,128)(2,1)S(1)}, u32[]{:S(2)}, u32[]{:S(2)}) collective-permute-start(bf16[2,4,32,128]{3,2,1,0:T(8,128)(2,1)S(1)} %get-tuple-element.33), channel_id=1, source_target_pairs={{0,24},{4,28},{8,16},{12,20},{16,8},{20,12},{24,0},{28,4},{1,25},{... | collective-permute-start | bytes 196616 | tf_op jit(solution)/shard_map/ppermute | solution.py:319
  40.8 1.4 %collective-permute-start.13 = (f32[4,32,128]{2,1,0:T(8,128)S(1)}, f32[4,32,128]{2,1,0:T(8,128)S(1)}, u32[]{:S(2)}, u32[]{:S(2)}) collective-permute-start(f32[4,32,128]{2,1,0:T(8,128)S(1)} %get-tuple-element.35), channel_id=1, source_target_pairs={{0,4},{4,0},{8,12},{12,8},{16,20},{20,16},{24,28},{28,24},{1,5},{5... | collective-permute-start | bytes 196616 | tf_op jit(solution)/shard_map/ppermute | solution.py:319
  40.9 1.3 %collective-permute-start.14 = (f32[1,512]{1,0:T(1,128)S(1)}, f32[1,512]{1,0:T(1,128)S(1)}, u32[]{:S(2)}, u32[]{:S(2)}) collective-permute-start(f32[1,512]{1,0:T(1,128)S(1)} %get-tuple-element.37), channel_id=1, source_target_pairs={{0,4},{4,0},{8,12},{12,8},{16,20},{20,16},{24,28},{28,24},{1,5},{5... | collective-permute-start | bytes 6152 | tf_op jit(solution)/shard_map/ppermute | solution.py:319

commit v4 on v3

v4 whole, which is shorter than its diff:
```python
import jax
import jax.numpy as jnp
from jax import lax
from jax.experimental import pallas as pl
from jax.experimental.pallas import tpu as pltpu
from jax.sharding import PartitionSpec as P


V = 4
HB = 2
BLK = 128
FORWARD = 32
BACKWARD = 32
F32 = jnp.float32
BF16 = jnp.bfloat16
VMEM = pl.BlockSpec(memory_space=pltpu.VMEM)
SMEM = pl.BlockSpec(memory_space=pltpu.SMEM)
SMALL = pltpu.CompilerParams(vmem_limit_bytes=4 << 20)


def split3(w):
    high = w.astype(BF16).astype(F32)
    mid = (w - high).astype(BF16).astype(F32)
    return high, mid, w - high - mid


def weights_kernel(head, reg, kernels, band, band_t, matrices, rows, arrived):
    tap_count, hidden_count, channels = reg.shape
    planes = band.shape[0]
    load = pltpu.make_async_copy(kernels, matrices, arrived)
    load.start()
    rows[...] = jnp.zeros_like(rows)
    for t in range(tap_count):
        row = head[0] * reg[t, 0:1, :].astype(F32)
        for r in range(1, hidden_count):
            row = row + head[r] * reg[t, r : r + 1, :].astype(F32)
        rows[t : t + 1, 0:channels] = row
    columns = rows[...].T
    lane = lax.broadcasted_iota(jnp.int32, (channels, BLK), 1)
    part = lane // planes
    score = lane % planes
    weights = []
    for t in range(tap_count):
        high, mid, low = split3(
            jnp.broadcast_to(columns[0:channels, t : t + 1], (channels, BLK))
        )
        weights.append(jnp.where(part < 2, high, jnp.where(part == 2, mid, low)))
    for d in range(planes):
        tile = jnp.zeros((channels, BLK), F32)
        for t in range(tap_count):
            tile = jnp.where(score == d - t + 1, weights[t], tile)
        band[d] = tile.astype(BF16)
    per_tile = BLK // channels
    for k in range(planes // per_tile):
        tile = band[k * per_tile : (k + 1) * per_tile].reshape(BLK, BLK)
        band_t[:, k * BLK : (k + 1) * BLK] = tile.astype(F32).T.astype(BF16)
    load.wait()


def stage_kernel(*refs):
    count = len(refs) // 2
    sems = refs[-1]
    copies = [
        pltpu.make_async_copy(refs[i], refs[count + i], sems.at[i]) for i in range(count)
    ]
    for copy in copies:
        copy.start()
    for copy in copies:
        copy.wait()


def table_kernel(mine, partner, out):
    planes = mine.shape[3]
    half = mine.shape[2] // 2

    def fill(start):
        for g, offsets in enumerate((mine, partner)):
            for j in range(V):
                for b in range(half):
                    row = offsets[0, j, start + b : start + b + 1, :]
                    out[g * V + j : g * V + j + 1, b * planes : (b + 1) * planes] = row

    pl.when(side() == 0)(lambda: fill(0))
    pl.when(side() == 1)(lambda: fill(half))


def side():
    return (lax.axis_index("frame") + lax.axis_index("tile")) % 2


def at_end():
    tile = lax.axis_index("tile")
    return jnp.where(side() == 0, tile == 0, tile == lax.axis_size("tile") - 1)


def halve_kernel(mine, partner, out):
    half = out.shape[1]

    def copy(start):
        for g, tile in enumerate((mine, partner)):
            for q in range(half):
                at = (start + q) * BLK
                out[g, q] = tile[0, :, at : at + BLK]

    pl.when(side() == 0)(lambda: copy(0))
    pl.when(side() == 1)(lambda: copy(half))


def rim_kernel(*refs):
    pieces, (outer, inner) = refs[:-2], refs[-2:]
    half = pieces[0].shape[1]
    left, right = slice(0, HB), slice(half - HB, half)

    def copy(out, part):
        for i, piece in enumerate(pieces):
            out[2 * i : 2 * i + 2] = piece[:, part]

    @pl.when(side() == 0)
    def _():
        copy(outer, left)
        copy(inner, right)

    @pl.when(side() == 1)
    def _():
        copy(outer, right)
        copy(inner, left)


class Work:
    def __init__(self, views, table, matrices, half, far):
        self.table, self.matrices = table, matrices
        self.half, self.slots = half, lax.axis_size("frame")
        self.planes = matrices.shape[0]
        self.span = half + 2 * HB
        self.me, self.side = lax.axis_index("frame"), side()
        blocks = half - HB if far else HB
        self.first = jnp.where((self.side == 0) == far, HB if far else half - HB, 0)
        self.columns = [(g, b) for g in range(2) for b in range(blocks)]
        self.slot_of = [[views[j, self.me ^ g] ^ self.me for j in range(V)] for g in range(2)]

    def lanes(self, k):
        return slice(k * BLK, (k + 1) * BLK)

    def rows_of(self, k, i, channels):
        start = (k * (V // 2) + i) * channels
        return slice(start, start + channels)

    def block_of(self, d, g, b, j):
        at = self.first + b
        return self.table[g * V + j, at * self.planes + d] + (at + HB)

    def pair_matrix(self, d):
        matrix = self.matrices[d]
        upper = jnp.concatenate([matrix, matrix], axis=1)
        return jnp.concatenate([upper, jnp.concatenate([matrix, -matrix], axis=1)], axis=0)

    def gather(self, src, base, pieces, outer, inner):
        half, span = self.half, self.span
        for r in range(self.slots):
            src[r * span + HB : r * span + HB + half] = pieces[r // 2][r % 2]

        def rims(near, far):
            for r in range(self.slots):
                if outer is not None:
                    src[r * span + near : r * span + near + HB] = outer[r]
                src[r * span + far : r * span + far + HB] = inner[r ^ 1]

        pl.when(self.side == 0)(lambda: rims(0, HB + half))
        pl.when(self.side == 1)(lambda: rims(HB + half, 0))
        if outer is not None:

            @pl.when(at_end())
            def _():
                near = jnp.where(self.side == 0, 0, HB + half)
                for r in range(self.slots):
                    for q in range(HB):
                        src[r * span + q + near] = jnp.zeros_like(src[0])

        for k, (g, b) in enumerate(self.columns):
            base[:, self.lanes(k)] = 2.0 * pieces[0][g, self.first + b].astype(F32)

    def forward(self, src, base, shifted, means, volume):
        pairs, share = V // 2, 1.0 / (V + 1)
        channels = base.shape[0]

        def plane(d, carry):
            picked = []
            for g, b in self.columns:
                for i in range(pairs):
                    tiles = [
                        src[self.slot_of[g][j] * self.span + self.block_of(d, g, b, j)]
                        for j in (2 * i, 2 * i + 1)
                    ]
                    picked.append(jnp.concatenate(tiles, axis=1))
            warped = jnp.dot(
                jnp.concatenate(picked, axis=0), self.pair_matrix(d), preferred_element_type=F32
            )
            for k in range(len(self.columns)):
                lanes = self.lanes(k)
                rows = [self.rows_of(k, i, channels) for i in range(pairs)]
                twice_first = base[:, lanes]
                plus = [warped[rows[i], 0:BLK] - twice_first for i in range(pairs)]
                minus = [warped[rows[i], BLK:] for i in range(pairs)]
                for i in range(pairs):
                    shifted[d, 2 * i, :, lanes] = plus[i]
                    shifted[d, 2 * i + 1, :, lanes] = minus[i]
                total = sum(plus[1:], plus[0])
                twice_mean = total * (2.0 * share)
                squares = sum(x * x for x in plus) + sum(x * x for x in minus)
                variance = (squares - total * twice_mean) * (0.5 * share)
                volume[d, :, lanes] = variance.astype(BF16)
                centred = total - (0.5 / share) * twice_mean
                means[d, :, lanes] = twice_mean + centred * (2.0 * share)
            return carry

        lax.fori_loop(0, self.planes, plane, 0, unroll=FORWARD)

    def backward(self, shifted, means, dvolume, ref_grad, grads, sums):
        pairs = V // 2
        channels = ref_grad.shape[0]
        for grad in grads:
            grad[...] = jnp.zeros_like(grad)
        ref_grad[...] = jnp.zeros_like(ref_grad)

        def plane(d, carry):
            rows = []
            for k in range(len(self.columns)):
                lanes = self.lanes(k)
                dvar = dvolume[d, :, lanes].astype(F32)
                twice_mean = means[d, :, lanes]
                ref_grad[:, lanes] -= dvar * twice_mean
                for i in range(pairs):
                    plus = dvar * (shifted[d, 2 * i, :, lanes] - twice_mean)
                    minus = dvar * shifted[d, 2 * i + 1, :, lanes]
                    rows.append(
                        jnp.concatenate([plus.astype(BF16), minus.astype(BF16)], axis=1)
                    )
            dpicked = lax.dot_general(
                jnp.concatenate(rows, axis=0), self.pair_matrix(d),
                (((1,), (1,)), ((), ())), preferred_element_type=F32,
            )
            for k, (g, b) in enumerate(self.columns):
                for i in range(pairs):
                    for j, part in ((2 * i, slice(0, BLK)), (2 * i + 1, slice(BLK, None))):
                        grads[g * V + j][self.block_of(d, g, b, j)] += dpicked[
                            self.rows_of(k, i, channels), part
                        ]
            return carry

        lax.fori_loop(0, self.planes, plane, 0, unroll=BACKWARD)
        for k, (g, b) in enumerate(self.columns):
            sums[g * self.span + HB + self.first + b] += ref_grad[:, self.lanes(k)]
        for g in range(2):
            for j in range(V):
                sums[pl.ds(self.slot_of[g][j] * self.span, self.span)] += grads[g * V + j][...]

    def give(self, sums, out, outer):
        end = HB + self.half

        def copy(start):
            for r in range(self.slots):
                at = r * self.span + start
                out[r] = (sums[at : at + HB] * (1.0 / (V + 1))).astype(BF16)

        pl.when(self.side == 0)(lambda: copy(0 if outer else end))
        pl.when(self.side == 1)(lambda: copy(end if outer else 0))


def forward_kernel(views, table, inner, matrices, *refs):
    pieces, (shifted, means, volume, src, base) = refs[:-5], refs[-5:]
    work = Work(views, table, matrices, pieces[0].shape[1], True)
    work.gather(src, base, pieces, None, inner)
    work.forward(src, base, shifted, means, volume)


def depth_kernel(
    views, table, outer, inner, matrices, band, band_t, cot, cot_partner,
    far_volume, *refs,
):
    (
        depth, depth_partner, far_dvolume, grad_outer, sums,
        src, base, shifted, means, volume, ref_grad,
    ) = refs[-11 - 2 * V : -2 * V]
    pieces, grads = refs[: -11 - 2 * V], refs[-2 * V :]
    half = pieces[0].shape[1]
    planes = matrices.shape[0]
    channels = base.shape[0]
    near = Work(views, table, matrices, half, False)
    far = Work(views, table, matrices, half, True)
    near.gather(src, base, pieces, outer, inner)
    near.forward(src, base, shifted, means, volume)

    groups = []
    for work, given, taken in ((near, volume, volume), (far, far_volume, far_dvolume)):
        wide = len(work.columns) // 2 * BLK
        for g in range(2):
            groups.append((work, given, taken, slice(g * wide, (g + 1) * wide), wide, g))
    raws = []
    for work, given, _, lanes, wide, g in groups:
        parts = jnp.dot(
            band_t[...], given[:, :, lanes].reshape(planes * channels, wide),
            preferred_element_type=F32,
        )
        raws.append(
            parts[0:planes]
            + (parts[2 * planes : 3 * planes] + parts[3 * planes : 4 * planes])
        )
    stacks = []
    for (work, _, _, _, wide, g), raw in zip(groups, raws):
        values = (
            lax.broadcasted_iota(jnp.int32, (planes, wide), 0).astype(F32) + 1.0
        ) / planes
        start = pl.multiple_of(work.first * BLK, BLK)
        start_all = pl.multiple_of((work.side * half + work.first) * BLK, BLK)
        slope_in = (cot, cot_partner)[g][0:1, pl.ds(start_all, wide)]
        tanh = jnp.tanh(raw)
        weights = jnp.exp(4.0 * tanh)
        norm = jnp.sum(weights, axis=0, keepdims=True)
        result = jnp.sum(weights * values, axis=0, keepdims=True) / norm
        (depth, depth_partner)[g][0:1, pl.ds(start, wide)] = result
        slope = (slope_in / norm) * (values - result) * weights
        draw = slope * (4.0 * (1.0 - tanh * tanh))
        high = draw.astype(BF16)
        low = (draw - high.astype(F32)).astype(BF16)
        stacks.append(jnp.concatenate([high, low, high, high], axis=0))
    for (_, _, taken, lanes, wide, _), stack in zip(groups, stacks):
        dvolume = jnp.dot(
            band[...].reshape(planes * channels, BLK), stack, preferred_element_type=F32
        )
        taken[:, :, lanes] = dvolume.astype(BF16).reshape(planes, channels, wide)

    sums[...] = jnp.zeros_like(sums)
    near.backward(shifted, means, volume, ref_grad, grads, sums)
    near.give(sums, grad_outer, True)


def backward_kernel(
    views, table, matrices, shifted, means, dvolume, sums_in,
    core_grad, grad_inner, sums, ref_grad, *grads,
):
    half = core_grad.shape[1]
    work = Work(views, table, matrices, half, True)
    sums[...] = sums_in[...]
    work.backward(shifted, means, dvolume, ref_grad, grads, sums)
    for r in range(work.slots):
        at = r * work.span + HB
        core_grad[r] = sums[at : at + half] * (1.0 / (V + 1))
    work.give(sums, grad_inner, False)


def merge_kernel(core, outer, inner, own, *sent):
    slots, half = core.shape[:2]

    def merge(near, far, beyond):
        for r in range(slots):
            out = own if r < 2 else sent[r // 2 - 1]
            for q in range(half):
                tile = core[r, q]
                if beyond and near <= q < near + HB:
                    tile = tile + outer[r, q - near].astype(F32)
                if far <= q < far + HB:
                    tile = tile + inner[r ^ 1, q - far].astype(F32)
                out[r % 2, q] = tile.astype(out.dtype)

    for i, ends in enumerate(((0, half - HB), (half - HB, 0))):
        here = side() == i
        pl.when(here & at_end())(lambda ends=ends: merge(*ends, False))
        pl.when(here & jnp.logical_not(at_end()))(lambda ends=ends: merge(*ends, True))


def sum_kernel(own, *refs):
    received, (mine, partner) = refs[:-2], refs[-2:]
    for g, out in enumerate((mine, partner)):
        total = own[g]
        for piece in received:
            total = total + piece[g].astype(F32)
        out[...] = total.astype(out.dtype)


def join_kernel(mine, partner, depth_mine, depth_partner, grad, depth):
    half = mine.shape[0]

    def join(at, tile, part):
        for q in range(half):
            grad[0, :, (at + q) * BLK : (at + q + 1) * BLK] = tile[q].astype(F32)
        depth[:, at * BLK : (at + half) * BLK] = part[...]

    @pl.when(side() == 0)
    def _():
        join(0, mine, depth_mine)
        join(half, partner, depth_partner)

    @pl.when(side() == 1)
    def _():
        join(0, partner, depth_partner)
        join(half, mine, depth_mine)


def exchange(x, distance):
    count = lax.axis_size("frame")
    return lax.ppermute(x, "frame", [(i, i ^ distance) for i in range(count)])


def swap_outer(x):
    count, tiles = lax.axis_size("frame"), lax.axis_size("tile")
    pairs = [
        (f * tiles + t, f * tiles + t + 1)
        for f in range(count)
        for t in range(tiles - 1)
        if (f + t) % 2 == 1
    ]
    ends = [(f, 0) for f in range(count) if f % 2 == 0]
    ends += [(f, tiles - 1) for f in range(count) if (f + tiles - 1) % 2 == 1]
    if count >= 4:
        pairs += [(f * tiles + t, (f ^ 2) * tiles + t) for f, t in ends if f & 2 == 0]
    return lax.ppermute(x, ("frame", "tile"), pairs + [(b, a) for a, b in pairs])


def small_call(kernel, ins, outs, scratch=()):
    return pl.pallas_call(
        kernel, out_shape=outs, in_specs=ins, out_specs=jax.tree.map(lambda _: VMEM, outs),
        scratch_shapes=scratch, compiler_params=SMALL,
    )


def per_device(features, views, offsets, kernels, reg_weight, head_weight, depth_cot):
    local_frames, channels, pixels = features.shape
    frames = lax.axis_size("frame")
    half = pixels // BLK // 2
    planes = kernels.shape[0]
    assert local_frames == 1 and frames & (frames - 1) == 0
    assert pixels == 2 * half * BLK and half >= HB
    shape = jax.ShapeDtypeStruct
    rim_shape = shape((frames, HB, channels, BLK), BF16)
    pair_shape = shape((2, half, channels, BLK), BF16)
    half_shape = shape((half, channels, BLK), F32)
    views = views.T
    offsets = jnp.swapaxes(offsets, 2, 3)

    features_partner = exchange(features, 1)
    arguments = (features, views, reg_weight, head_weight, offsets, depth_cot)
    staged, views, reg_weight, head_weight, offsets_mine, cot_mine = pl.pallas_call(
        stage_kernel,
        out_shape=tuple(shape(x.shape, x.dtype) for x in arguments),
        in_specs=[pl.BlockSpec(memory_space=pltpu.HBM)] * len(arguments),
        out_specs=(VMEM,) * len(arguments),
        scratch_shapes=[pltpu.SemaphoreType.DMA((len(arguments),))],
        compiler_params=SMALL,
        name="stage_arguments",
    )(*(pltpu.with_memory_space_constraint(x, pltpu.HBM) for x in arguments))
    prepare = small_call(
        weights_kernel, [SMEM, VMEM, pl.BlockSpec(memory_space=pltpu.HBM)],
        (
            shape((planes, channels, BLK), BF16), shape((BLK, planes * channels), BF16),
            shape(kernels.shape, BF16),
        ),
        [pltpu.VMEM((BLK, BLK), F32), pltpu.SemaphoreType.DMA(())],
    )
    band, band_t, matrices = prepare(head_weight, reg_weight, pltpu.with_memory_space_constraint(kernels, pltpu.HBM))

    offsets_partner = exchange(offsets, 1)
    table = small_call(
        table_kernel, [VMEM] * 2, shape((2 * V, half * planes), jnp.int32)
    )(offsets_mine, offsets_partner)
    cot_partner = exchange(depth_cot, 1)
    pieces = [small_call(halve_kernel, [VMEM] * 2, pair_shape)(staged, features_partner)]
    for r in range(2, frames, 2):
        pieces.append(exchange(pieces[0], r))
    outer, inner = small_call(rim_kernel, [VMEM] * (frames // 2), (rim_shape, rim_shape))(*pieces)
    inner = exchange(inner, 1)
    outer = swap_outer(outer)

    span = half + 2 * HB
    assert V % 2 == 0 and planes % FORWARD == 0
    near_pixels, far_pixels = 2 * HB * BLK, 2 * (half - HB) * BLK
    depth_half = shape((1, half * BLK), F32)
    sums_shape = shape((frames * span, channels, BLK), F32)
    sources = pltpu.VMEM((frames * span, channels, BLK), BF16)
    accumulators = [pltpu.VMEM((span, channels, BLK), F32)] * (2 * V)

    def big_call(kernel, smem, vmem, outs, scratch, limit, part):
        return pl.pallas_call(
            kernel, out_shape=outs, in_specs=[SMEM] * smem + [VMEM] * vmem,
            out_specs=jax.tree.map(lambda _: VMEM, outs), scratch_shapes=scratch,
            compiler_params=pltpu.CompilerParams(vmem_limit_bytes=limit << 20),
            cost_estimate=pl.CostEstimate(
                flops=int(part * planes * V * channels * pixels * BLK),
                bytes_accessed=4 << 20, transcendentals=2 * planes * pixels,
            ),
        )

    shifted, means, volume = big_call(
        forward_kernel, 2, 2 + frames // 2,
        (
            shape((planes, V, channels, far_pixels), F32),
            shape((planes, channels, far_pixels), F32),
            shape((planes, channels, far_pixels), BF16),
        ),
        [sources, pltpu.VMEM((channels, far_pixels), F32)], 4, 1,
    )(views, table, inner, matrices, *pieces)
    depth, depth_partner, dvolume, outer, sums = big_call(
        depth_kernel, 2, 8 + frames // 2,
        (
            depth_half, depth_half, shape((planes, channels, far_pixels), BF16), rim_shape,
            sums_shape,
        ),
        [
            sources,
            pltpu.VMEM((channels, near_pixels), F32),
            pltpu.VMEM((planes, V, channels, near_pixels), F32),
            pltpu.VMEM((planes, channels, near_pixels), F32),
            pltpu.VMEM((planes, channels, near_pixels), BF16),
            pltpu.VMEM((channels, near_pixels), F32),
        ]
        + accumulators, 20, 2,
    )(
        views, table, outer, inner, matrices, band, band_t, cot_mine,
        cot_partner, volume, *pieces,
    )
    outer = swap_outer(outer)
    core_grad, inner = big_call(
        backward_kernel, 2, 5,
        (shape((frames, half, channels, BLK), F32), rim_shape),
        [
            pltpu.VMEM(sums_shape.shape, F32), pltpu.VMEM((channels, far_pixels), F32),
        ]
        + accumulators, 6, 1,
    )(views, table, matrices, shifted, means, dvolume, sums)
    inner = exchange(inner, 1)
    depth_partner = exchange(depth_partner, 1)
    own, *sent = small_call(
        merge_kernel, [VMEM] * 3,
        (shape(pair_shape.shape, F32),) + (pair_shape,) * (frames // 2 - 1),
    )(core_grad, outer, inner)
    received = []
    for r, piece in zip(range(2, frames, 2), sent):
        received.append(exchange(piece, r))
    mine, partner = small_call(
        sum_kernel, [VMEM] * (frames // 2), (half_shape, shape(half_shape.shape, BF16))
    )(own, *received)
    grad, depth = small_call(
        join_kernel, [VMEM] * 4,
        (shape(features.shape, F32), shape(depth_cot.shape, F32)),
    )(mine, exchange(partner, 1), depth, depth_partner)
    return depth, grad


def solution(mesh):
    return jax.shard_map(
        per_device,
        mesh=mesh,
        in_specs=(
            P("frame", None, "tile"),
            P(),
            P("frame", None, None, "tile"),
            P(),
            P(),
            P(),
            P("frame", "tile"),
        ),
        out_specs=(P("frame", "tile"), P("frame", None, "tile")),
        check_vma=False,
    )
```

time: 43.1 us -> 41.6 us (0.965)
  waiting for transfers between devices: 15.8 us -> 13.1 us
  starting transfers between devices: 11.4 us -> 12.4 us
    ppermute x2, waiting for transfers between devices: 6.69 us -> 3.98 us  [swap_outer(): lax.ppermute(x, ('frame', 'tile'), pairs + [(b, a) for a, b in pairs])]
    ppermute x13, starting transfers between devices: 9.75 us -> 10.7 us  [exchange(): return lax.ppermute(x, 'frame', [(i, i ^ distance) for i in range(count)])]
    pallas_call x4 -> x7, Pallas kernels: 14.1 us -> 14.4 us  [the longest x1 5.47 us: per_device(): big_call(depth_kernel, 2, 8 + frames // 2, (depth_half, depth_half, shape...]
  transfers between devices with their start and end apart: 15 -> 15, of which waited for: 11 -> 10; matrix products, arithmetic and copies ran while one was open for 0% -> 0% of each run, Pallas kernels for 4% -> 14%
where the time goes in v4:
time: 41.6 us; the launch traced here: 41.4 us
  Pallas kernels  15.2 us (37%)
  waiting for transfers between devices  13.1 us (31%)
  starting transfers between devices  12.4 us (30%)
  between operations  0.76 us (2%)
    ppermute x13, starting transfers between devices, exchange(): return lax.ppermute(x, 'frame', [(i, i ^ distance) for i in range(count)])  10.7 us
    ppermute x13, waiting for transfers between devices, exchange(): return lax.ppermute(x, 'frame', [(i, i ^ distance) for i in range(count)])  9.08 us
    pallas_call x1, Pallas kernels, per_device(): big_call(depth_kernel, 2, 8 + frames // 2, (depth_half, depth_half, shape...  5.47 us
    ppermute x2, waiting for transfers between devices, swap_outer(): lax.ppermute(x, ('frame', 'tile'), pairs + [(b, a) for a, b in pairs])  3.98 us
    pallas_call x1, Pallas kernels, per_device(): big_call(backward_kernel, 2, 5, (shape((frames, half, channels, BLK), F32...  3.21 us
    pallas_call x1, Pallas kernels, per_device(): big_call(forward_kernel, 2, 2 + frames // 2, (shape((planes, V, channels,...  2.93 us
    pallas_call x1, Pallas kernels, per_device(): prepare(head_weight, reg_weight, pltpu.with_memory_space_constraint(kerne...  1.78 us
    ppermute x2, starting transfers between devices, swap_outer(): lax.ppermute(x, ('frame', 'tile'), pairs + [(b, a) for a, b in pairs])  1.64 us
  transfers between devices with their start and end apart: 15, of which 10 were waited for; matrix products, arithmetic and copies ran while one was open for 0% of the time, Pallas kernels for 14%

profile of v4, /device:TPU:0, one launch (start us, length us, event | category | flops | bytes accessed | tf_op | source)
XLA Modules:
  0.0 41.4 jit_solution(1292060675178955631)
XLA Ops:
  0.6 0.6 %collective-permute-start.1 = (bf16[1,32,1024]{2,1,0:T(8,128)(2,1)}, bf16[1,32,1024]{2,1,0:T(8,128)(2,1)S(1)}, u32[]{:S(2)}, u32[]{:S(2)}) collective-permute-start(bf16[1,32,1024]{2,1,0:T(8,128)(2,1)} %refs_0_.1), channel_id=1, source_target_pairs={{0,4},{4,0},{8,12},{12,8},{16,20},{20,16},{24,28},{28,24},{1,5},{5... | collective-permute-start | bytes 196616 | tf_op jit(solution)/shard_map/ppermute | solution.py:401
  1.2 0.9 %stage_arguments.1 = (bf16[1,32,1024]{2,1,0:T(8,128)(2,1)S(1)}, s32[4,8]{1,0:T(4,128)S(1)}, bf16[3,8,32]{2,1,0:T(8,128)(2,1)S(1)}, f32[8]{0:T(128)S(1)}, s32[1,4...) custom-call(bf16[1,32,1024]{2,1,0:T(8,128)(2,1)} %refs_0_.1, s32[4,8]{1,0:T(4,128)} %bitcast.4, bf16[3,8,32]{2,1,0:T(8,128)(2,1)} %refs_2_.1, ...), custom_call_target="tpu_custom_call" | custom-call | tf_op jit(solution)/shard_map/stage_arguments/pallas_call | solution.py:442
  2.3 3.8 %collective-permute-start.4 = (bf16[2,4,32,128]{3,2,1,0:T(8,128)(2,1)S(1)}, bf16[2,4,32,128]{3,2,1,0:T(8,128)(2,1)S(1)}, u32[]{:S(2)}, u32[]{:S(2)}) collective-permute-start(bf16[2,4,32,128]{3,2,1,0:T(8,128)(2,1)S(1)} %shard_map.88.refs_0_), channel_id=1, source_target_pairs={{0,24},{4,28},{8,16},{12,20},{16,8},{20,12},{24,0},{28,4},{1,25},{... | collective-permute-start | bytes 196616 | tf_op jit(solution)/shard_map/ppermute | solution.py:401
  6.2 0.5 %collective-permute-start.3 = (bf16[2,4,32,128]{3,2,1,0:T(8,128)(2,1)S(1)}, bf16[2,4,32,128]{3,2,1,0:T(8,128)(2,1)S(1)}, u32[]{:S(2)}, u32[]{:S(2)}) collective-permute-start(bf16[2,4,32,128]{3,2,1,0:T(8,128)(2,1)S(1)} %shard_map.88.refs_0_), channel_id=1, source_target_pairs={{0,16},{4,20},{8,24},{12,28},{16,0},{20,4},{24,8},{28,12},{1,17},{... | collective-permute-start | bytes 196616 | tf_op jit(solution)/shard_map/ppermute | solution.py:401
  6.8 1.8 %collective-permute-done.4.refs_3_ = bf16[2,4,32,128]{3,2,1,0:T(8,128)(2,1)S(1)} collective-permute-done((bf16[2,4,32,128]{3,2,1,0:T(8,128)(2,1)S(1)}, bf16[2,4,32,128]{3,2,1,0:T(8,128)(2,1)S(1)}, u32[]{:S(2)}, u32[]{:S(2)}) %collective-permute-start.4) | collective-permute-done | bytes 65568 | tf_op jit(solution)/shard_map/ppermute | solution.py:401
  8.6 1.9 %collective-permute-done.3.refs_2_ = bf16[2,4,32,128]{3,2,1,0:T(8,128)(2,1)S(1)} collective-permute-done((bf16[2,4,32,128]{3,2,1,0:T(8,128)(2,1)S(1)}, bf16[2,4,32,128]{3,2,1,0:T(8,128)(2,1)S(1)}, u32[]{:S(2)}, u32[]{:S(2)}) %collective-permute-start.3) | collective-permute-done | bytes 65568 | tf_op jit(solution)/shard_map/ppermute | solution.py:401
  10.4 0.5 %collective-permute-done.2.refs_1_ = bf16[2,4,32,128]{3,2,1,0:T(8,128)(2,1)S(1)} collective-permute-done((bf16[2,4,32,128]{3,2,1,0:T(8,128)(2,1)S(1)}, bf16[2,4,32,128]{3,2,1,0:T(8,128)(2,1)S(1)}, u32[]{:S(2)}, u32[]{:S(2)}) %collective-permute-start.2) | collective-permute-done | bytes 65568 | tf_op jit(solution)/shard_map/ppermute | solution.py:401
  11.1 0.8 %collective-permute-start.6 = (bf16[8,2,32,128]{3,2,1,0:T(8,128)(2,1)S(1)}, bf16[8,2,32,128]{3,2,1,0:T(8,128)(2,1)S(1)}, u32[]{:S(2)}, u32[]{:S(2)}) collective-permute-start(bf16[8,2,32,128]{3,2,1,0:T(8,128)(2,1)S(1)} %get-tuple-element.40), channel_id=1, source_target_pairs={{1,2},{4,5},{6,7},{9,10},{12,13},{14,15},{17,18},{20,21},{22,23},{... | collective-permute-start | bytes 393224 | tf_op jit(solution)/shard_map/ppermute | solution.py:416
  11.9 0.9 %collective-permute-start = (s32[1,4,8,32]{3,2,1,0:T(8,128)}, s32[1,4,8,32]{3,2,1,0:T(8,128)S(1)}, u32[]{:S(2)}, u32[]{:S(2)}) collective-permute-start(s32[1,4,8,32]{3,2,1,0:T(8,128)} %bitcast.3), channel_id=1, source_target_pairs={{0,4},{4,0},{8,12},{12,8},{16,20},{20,16},{24,28},{28,24},{1,5},{5... | collective-permute-start | bytes 12296 | tf_op jit(solution)/shard_map/ppermute | solution.py:401
  12.8 1.8 %shard_map.87 = (bf16[32,32,128]{2,1,0:T(8,128)(2,1)S(1)}, bf16[128,1024]{1,0:T(8,128)(2,1)S(1)}, bf16[32,128,128]{2,1,0:T(8,128)(2,1)S(1)}) custom-call(f32[8]{0:T(128)S(1)} %get-tuple-element.33.head, bf16[3,8,32]{2,1,0:T(8,128)(2,1)S(1)} %get-tuple-element.34.reg, bf16[32,128,128]{2,1,0:T(8,128)(2,1)} %kernels.1), custom_call_target="tpu_custom_call" | custom-call | tf_op jit(solution)/shard_map/pallas_call | solution.py:459
  14.8 2.9 %shard_map.90 = (f32[32,4,32,512]{3,2,1,0:T(8,128)S(1)}, f32[32,32,512]{2,1,0:T(8,128)S(1)}, bf16[32,32,512]{2,1,0:T(8,128)(2,1)S(1)}) custom-call(s32[4,8]{1,0:T(4,128)S(1)} %get-tuple-element.31.views, s32[8,128]{1,0:T(8,128)S(1)} %shard_map.86.table, bf16[8,2,32,128]{3,2,1,0:T(8,128)(2,1)S(1)} %collective-permute-done.5.inner, ...), custom_call_target="tpu_custom_call" | custom-call | flops 536870912 | bytes 4194304 | tf_op jit(solution)/shard_map/pallas_call | solution.py:492
  17.7 5.5 %shard_map.91 = (f32[1,512]{1,0:T(1,128)S(1)}, f32[1,512]{1,0:T(1,128)S(1)}, bf16[32,32,512]{2,1,0:T(8,128)(2,1)S(1)}, bf16[8,2,32,128]{3,2,1,0:T(8,128)(2,1)S(1)}, f32[64,32,128]{2,1,0:T(8,128)S(1)}) custom-call(s32[4,8]{1,0:T(4,128)S(1)} %get-tuple-element.31.views, s32[8,128]{1,0:T(8,128)S(1)} %shard_map.86.table, ...), custom_call_target="tpu_custom_call" | custom-call | flops 1073741824 | bytes 4194304 | tf_op jit(solution)/shard_map/pallas_call | solution.py:501
  23.2 3.2 %shard_map.92 = (f32[8,4,32,128]{3,2,1,0:T(8,128)S(1)}, bf16[8,2,32,128]{3,2,1,0:T(8,128)(2,1)S(1)}) custom-call(s32[4,8]{1,0:T(4,128)S(1)} %get-tuple-element.31.views, s32[8,128]{1,0:T(8,128)S(1)} %shard_map.86.table, bf16[32,128,128]{2,1,0:T(8,128)(2,1)S(1)} %get-tuple-element.35.matrices, f32[32,4,32,512]{3,2,1,0:T(8,128)S(1)} %get-tuple-element.38.shifted, ...), custom_call_target="tpu_custom_call" | custom-call | flops 536870912 | bytes 4194304 | tf_op jit(solution)/shard_map/pallas_call | solution.py:521
  26.4 0.6 %collective-permute-start.9 = (bf16[8,2,32,128]{3,2,1,0:T(8,128)(2,1)S(1)}, bf16[8,2,32,128]{3,2,1,0:T(8,128)(2,1)S(1)}, u32[]{:S(2)}, u32[]{:S(2)}) collective-permute-start(bf16[8,2,32,128]{3,2,1,0:T(8,128)(2,1)S(1)} %get-tuple-element.49), channel_id=1, source_target_pairs={{0,4},{4,0},{8,12},{12,8},{16,20},{20,16},{24,28},{28,24},{1,5},{5... | collective-permute-start | bytes 393224 | tf_op jit(solution)/shard_map/ppermute | solution.py:401
  27.0 0.8 %collective-permute-start.8 = (bf16[8,2,32,128]{3,2,1,0:T(8,128)(2,1)S(1)}, bf16[8,2,32,128]{3,2,1,0:T(8,128)(2,1)S(1)}, u32[]{:S(2)}, u32[]{:S(2)}) collective-permute-start(bf16[8,2,32,128]{3,2,1,0:T(8,128)(2,1)S(1)} %get-tuple-element.48), channel_id=1, source_target_pairs={{1,2},{4,5},{6,7},{9,10},{12,13},{14,15},{17,18},{20,21},{22,23},{... | collective-permute-start | bytes 393224 | tf_op jit(solution)/shard_map/ppermute | solution.py:416
  28.0 4.0 %collective-permute-done.8.outer = bf16[8,2,32,128]{3,2,1,0:T(8,128)(2,1)S(1)} collective-permute-done((bf16[8,2,32,128]{3,2,1,0:T(8,128)(2,1)S(1)}, bf16[8,2,32,128]{3,2,1,0:T(8,128)(2,1)S(1)}, u32[]{:S(2)}, u32[]{:S(2)}) %collective-permute-start.8) | collective-permute-done | bytes 131104 | tf_op jit(solution)/shard_map/ppermute | solution.py:416
  32.0 0.9 %collective-permute-start.10 = (bf16[2,4,32,128]{3,2,1,0:T(8,128)(2,1)S(1)}, bf16[2,4,32,128]{3,2,1,0:T(8,128)(2,1)S(1)}, u32[]{:S(2)}, u32[]{:S(2)}) collective-permute-start(bf16[2,4,32,128]{3,2,1,0:T(8,128)(2,1)S(1)} %get-tuple-element.51), channel_id=1, source_target_pairs={{0,8},{4,12},{8,0},{12,4},{16,24},{20,28},{24,16},{28,20},{1,9},{5... | collective-permute-start | bytes 196616 | tf_op jit(solution)/shard_map/ppermute | solution.py:401
  32.9 1.3 %collective-permute-start.11 = (bf16[2,4,32,128]{3,2,1,0:T(8,128)(2,1)S(1)}, bf16[2,4,32,128]{3,2,1,0:T(8,128)(2,1)S(1)}, u32[]{:S(2)}, u32[]{:S(2)}) collective-permute-start(bf16[2,4,32,128]{3,2,1,0:T(8,128)(2,1)S(1)} %get-tuple-element.52), channel_id=1, source_target_pairs={{0,16},{4,20},{8,24},{12,28},{16,0},{20,4},{24,8},{28,12},{1,17},{... | collective-permute-start | bytes 196616 | tf_op jit(solution)/shard_map/ppermute | solution.py:401
  34.1 1.4 %collective-permute-start.12 = (bf16[2,4,32,128]{3,2,1,0:T(8,128)(2,1)S(1)}, bf16[2,4,32,128]{3,2,1,0:T(8,128)(2,1)S(1)}, u32[]{:S(2)}, u32[]{:S(2)}) collective-permute-start(bf16[2,4,32,128]{3,2,1,0:T(8,128)(2,1)S(1)} %get-tuple-element.53), channel_id=1, source_target_pairs={{0,24},{4,28},{8,16},{12,20},{16,8},{20,12},{24,0},{28,4},{1,25},{... | collective-permute-start | bytes 196616 | tf_op jit(solution)/shard_map/ppermute | solution.py:401
  35.6 1.4 %collective-permute-done.10.refs_0_ = bf16[2,4,32,128]{3,2,1,0:T(8,128)(2,1)S(1)} collective-permute-done((bf16[2,4,32,128]{3,2,1,0:T(8,128)(2,1)S(1)}, bf16[2,4,32,128]{3,2,1,0:T(8,128)(2,1)S(1)}, u32[]{:S(2)}, u32[]{:S(2)}) %collective-permute-start.10) | collective-permute-done | bytes 65568 | tf_op jit(solution)/shard_map/ppermute | solution.py:401
  37.0 0.8 %collective-permute-done.11.refs_1_ = bf16[2,4,32,128]{3,2,1,0:T(8,128)(2,1)S(1)} collective-permute-done((bf16[2,4,32,128]{3,2,1,0:T(8,128)(2,1)S(1)}, bf16[2,4,32,128]{3,2,1,0:T(8,128)(2,1)S(1)}, u32[]{:S(2)}, u32[]{:S(2)}) %collective-permute-start.11) | collective-permute-done | bytes 65568 | tf_op jit(solution)/shard_map/ppermute | solution.py:401
  37.8 1.5 %collective-permute-done.12.refs_2_ = bf16[2,4,32,128]{3,2,1,0:T(8,128)(2,1)S(1)} collective-permute-done((bf16[2,4,32,128]{3,2,1,0:T(8,128)(2,1)S(1)}, bf16[2,4,32,128]{3,2,1,0:T(8,128)(2,1)S(1)}, u32[]{:S(2)}, u32[]{:S(2)}) %collective-permute-start.12) | collective-permute-done | bytes 65568 | tf_op jit(solution)/shard_map/ppermute | solution.py:401
  39.9 0.8 %collective-permute-done.14.depth_partner = f32[1,512]{1,0:T(1,128)S(1)} collective-permute-done((f32[1,512]{1,0:T(1,128)S(1)}, f32[1,512]{1,0:T(1,128)S(1)}, u32[]{:S(2)}, u32[]{:S(2)}) %collective-permute-start.14) | collective-permute-done | bytes 2080 | tf_op jit(solution)/shard_map/ppermute | solution.py:401
  40.7 0.7 %shard_map.95 = (f32[1,32,1024]{2,1,0:T(8,128)}, f32[1,1024]{1,0:T(1,128)}) custom-call(f32[4,32,128]{2,1,0:T(8,128)S(1)} %get-tuple-element.54.mine, bf16[4,32,128]{2,1,0:T(8,128)(2,1)S(1)} %collective-permute-done.13.partner, f32[1,512]{1,0:T(1,128)S(1)} %get-tuple-element.56.depth_mine, f32[1,512]{1,0:T(1,128)S(1)} %collective-permute-done.14.depth_partner), custom_call_target="tpu_custom_call" | custom-call | tf_op jit(solution)/shard_map/pallas_call | solution.py:541
  (17 shorter events, 1.4 us)
Async XLA Ops:
  0.6 1.7 %collective-permute-start.1 = (bf16[1,32,1024]{2,1,0:T(8,128)(2,1)}, bf16[1,32,1024]{2,1,0:T(8,128)(2,1)S(1)}, u32[]{:S(2)}, u32[]{:S(2)}) collective-permute-start(bf16[1,32,1024]{2,1,0:T(8,128)(2,1)} %refs_0_.1), channel_id=1, source_target_pairs={{0,4},{4,0},{8,12},{12,8},{16,20},{20,16},{24,28},{28,24},{1,5},{5... | collective-permute-start | bytes 196616 | tf_op jit(solution)/shard_map/ppermute | solution.py:401
  2.3 6.3 %collective-permute-start.4 = (bf16[2,4,32,128]{3,2,1,0:T(8,128)(2,1)S(1)}, bf16[2,4,32,128]{3,2,1,0:T(8,128)(2,1)S(1)}, u32[]{:S(2)}, u32[]{:S(2)}) collective-permute-start(bf16[2,4,32,128]{3,2,1,0:T(8,128)(2,1)S(1)} %shard_map.88.refs_0_), channel_id=1, source_target_pairs={{0,24},{4,28},{8,16},{12,20},{16,8},{20,12},{24,0},{28,4},{1,25},{... | collective-permute-start | bytes 196616 | tf_op jit(solution)/shard_map/ppermute | solution.py:401
  6.2 4.3 %collective-permute-start.3 = (bf16[2,4,32,128]{3,2,1,0:T(8,128)(2,1)S(1)}, bf16[2,4,32,128]{3,2,1,0:T(8,128)(2,1)S(1)}, u32[]{:S(2)}, u32[]{:S(2)}) collective-permute-start(bf16[2,4,32,128]{3,2,1,0:T(8,128)(2,1)S(1)} %shard_map.88.refs_0_), channel_id=1, source_target_pairs={{0,16},{4,20},{8,24},{12,28},{16,0},{20,4},{24,8},{28,12},{1,17},{... | collective-permute-start | bytes 196616 | tf_op jit(solution)/shard_map/ppermute | solution.py:401
  6.7 4.3 %collective-permute-start.2 = (bf16[2,4,32,128]{3,2,1,0:T(8,128)(2,1)S(1)}, bf16[2,4,32,128]{3,2,1,0:T(8,128)(2,1)S(1)}, u32[]{:S(2)}, u32[]{:S(2)}) collective-permute-start(bf16[2,4,32,128]{3,2,1,0:T(8,128)(2,1)S(1)} %shard_map.88.refs_0_), channel_id=1, source_target_pairs={{0,8},{4,12},{8,0},{12,4},{16,24},{20,28},{24,16},{28,20},{1,9},{5... | collective-permute-start | bytes 196616 | tf_op jit(solution)/shard_map/ppermute | solution.py:401
  11.0 3.8 %collective-permute-start.5 = (bf16[8,2,32,128]{3,2,1,0:T(8,128)(2,1)S(1)}, bf16[8,2,32,128]{3,2,1,0:T(8,128)(2,1)S(1)}, u32[]{:S(2)}, u32[]{:S(2)}) collective-permute-start(bf16[8,2,32,128]{3,2,1,0:T(8,128)(2,1)S(1)} %get-tuple-element.37), channel_id=1, source_target_pairs={{0,4},{4,0},{8,12},{12,8},{16,20},{20,16},{24,28},{28,24},{1,5},{5... | collective-permute-start | bytes 393224 | tf_op jit(solution)/shard_map/ppermute | solution.py:401
  11.1 6.7 %collective-permute-start.6 = (bf16[8,2,32,128]{3,2,1,0:T(8,128)(2,1)S(1)}, bf16[8,2,32,128]{3,2,1,0:T(8,128)(2,1)S(1)}, u32[]{:S(2)}, u32[]{:S(2)}) collective-permute-start(bf16[8,2,32,128]{3,2,1,0:T(8,128)(2,1)S(1)} %get-tuple-element.40), channel_id=1, source_target_pairs={{1,2},{4,5},{6,7},{9,10},{12,13},{14,15},{17,18},{20,21},{22,23},{... | collective-permute-start | bytes 393224 | tf_op jit(solution)/shard_map/ppermute | solution.py:416
  11.9 2.7 %collective-permute-start = (s32[1,4,8,32]{3,2,1,0:T(8,128)}, s32[1,4,8,32]{3,2,1,0:T(8,128)S(1)}, u32[]{:S(2)}, u32[]{:S(2)}) collective-permute-start(s32[1,4,8,32]{3,2,1,0:T(8,128)} %bitcast.3), channel_id=1, source_target_pairs={{0,4},{4,0},{8,12},{12,8},{16,20},{20,16},{24,28},{28,24},{1,5},{5... | collective-permute-start | bytes 12296 | tf_op jit(solution)/shard_map/ppermute | solution.py:401
  12.8 4.9 %collective-permute-start.7 = (f32[1,1024]{1,0:T(1,128)}, f32[1,1024]{1,0:T(1,128)S(1)}, u32[]{:S(2)}, u32[]{:S(2)}) collective-permute-start(f32[1,1024]{1,0:T(1,128)} %refs_5_.1), channel_id=1, source_target_pairs={{0,4},{4,0},{8,12},{12,8},{16,20},{20,16},{24,28},{28,24},{1,5},{5... | collective-permute-start | bytes 12296 | tf_op jit(solution)/shard_map/ppermute | solution.py:401
  26.4 1.6 %collective-permute-start.9 = (bf16[8,2,32,128]{3,2,1,0:T(8,128)(2,1)S(1)}, bf16[8,2,32,128]{3,2,1,0:T(8,128)(2,1)S(1)}, u32[]{:S(2)}, u32[]{:S(2)}) collective-permute-start(bf16[8,2,32,128]{3,2,1,0:T(8,128)(2,1)S(1)} %get-tuple-element.49), channel_id=1, source_target_pairs={{0,4},{4,0},{8,12},{12,8},{16,20},{20,16},{24,28},{28,24},{1,5},{5... | collective-permute-start | bytes 393224 | tf_op jit(solution)/shard_map/ppermute | solution.py:401
  27.0 5.0 %collective-permute-start.8 = (bf16[8,2,32,128]{3,2,1,0:T(8,128)(2,1)S(1)}, bf16[8,2,32,128]{3,2,1,0:T(8,128)(2,1)S(1)}, u32[]{:S(2)}, u32[]{:S(2)}) collective-permute-start(bf16[8,2,32,128]{3,2,1,0:T(8,128)(2,1)S(1)} %get-tuple-element.48), channel_id=1, source_target_pairs={{1,2},{4,5},{6,7},{9,10},{12,13},{14,15},{17,18},{20,21},{22,23},{... | collective-permute-start | bytes 393224 | tf_op jit(solution)/shard_map/ppermute | solution.py:416
  32.0 5.0 %collective-permute-start.10 = (bf16[2,4,32,128]{3,2,1,0:T(8,128)(2,1)S(1)}, bf16[2,4,32,128]{3,2,1,0:T(8,128)(2,1)S(1)}, u32[]{:S(2)}, u32[]{:S(2)}) collective-permute-start(bf16[2,4,32,128]{3,2,1,0:T(8,128)(2,1)S(1)} %get-tuple-element.51), channel_id=1, source_target_pairs={{0,8},{4,12},{8,0},{12,4},{16,24},{20,28},{24,16},{28,20},{1,9},{5... | collective-permute-start | bytes 196616 | tf_op jit(solution)/shard_map/ppermute | solution.py:401
  32.9 4.9 %collective-permute-start.11 = (bf16[2,4,32,128]{3,2,1,0:T(8,128)(2,1)S(1)}, bf16[2,4,32,128]{3,2,1,0:T(8,128)(2,1)S(1)}, u32[]{:S(2)}, u32[]{:S(2)}) collective-permute-start(bf16[2,4,32,128]{3,2,1,0:T(8,128)(2,1)S(1)} %get-tuple-element.52), channel_id=1, source_target_pairs={{0,16},{4,20},{8,24},{12,28},{16,0},{20,4},{24,8},{28,12},{1,17},{... | collective-permute-start | bytes 196616 | tf_op jit(solution)/shard_map/ppermute | solution.py:401
  34.1 5.2 %collective-permute-start.12 = (bf16[2,4,32,128]{3,2,1,0:T(8,128)(2,1)S(1)}, bf16[2,4,32,128]{3,2,1,0:T(8,128)(2,1)S(1)}, u32[]{:S(2)}, u32[]{:S(2)}) collective-permute-start(bf16[2,4,32,128]{3,2,1,0:T(8,128)(2,1)S(1)} %get-tuple-element.53), channel_id=1, source_target_pairs={{0,24},{4,28},{8,16},{12,20},{16,8},{20,12},{24,0},{28,4},{1,25},{... | collective-permute-start | bytes 196616 | tf_op jit(solution)/shard_map/ppermute | solution.py:401
  39.3 1.4 %collective-permute-start.13 = (bf16[4,32,128]{2,1,0:T(8,128)(2,1)S(1)}, bf16[4,32,128]{2,1,0:T(8,128)(2,1)S(1)}, u32[]{:S(2)}, u32[]{:S(2)}) collective-permute-start(bf16[4,32,128]{2,1,0:T(8,128)(2,1)S(1)} %get-tuple-element.55), channel_id=1, source_target_pairs={{0,4},{4,0},{8,12},{12,8},{16,20},{20,16},{24,28},{28,24},{1,5},{5... | collective-permute-start | bytes 98312 | tf_op jit(solution)/shard_map/ppermute | solution.py:401
  39.4 1.3 %collective-permute-start.14 = (f32[1,512]{1,0:T(1,128)S(1)}, f32[1,512]{1,0:T(1,128)S(1)}, u32[]{:S(2)}, u32[]{:S(2)}) collective-permute-start(f32[1,512]{1,0:T(1,128)S(1)} %get-tuple-element.57), channel_id=1, source_target_pairs={{0,4},{4,0},{8,12},{12,8},{16,20},{20,16},{24,28},{28,24},{1,5},{5... | collective-permute-start | bytes 6152 | tf_op jit(solution)/shard_map/ppermute | solution.py:401

commit v5 on v4

--- a/solution.py
+++ b/solution.py
@@ -215,6 +215,45 @@
 
         lax.fori_loop(0, self.planes, plane, 0, unroll=FORWARD)
 
+    def depths(self, band, band_t, cots, volume, dvolume, depths, first):
+        planes = self.planes
+        channels = volume.shape[1]
+        wide = len(self.columns) // 2 * BLK
+        groups = [slice(g * wide, (g + 1) * wide) for g in range(2)]
+        values = (
+            lax.broadcasted_iota(jnp.int32, (planes, wide), 0).astype(F32) + 1.0
+        ) / planes
+        raws = []
+        for lanes in groups:
+            parts = jnp.dot(
+                band_t[...], volume[:, :, lanes].reshape(planes * channels, wide),
+                preferred_element_type=F32,
+            )
+            raws.append(
+                parts[0:planes]
+                + (parts[2 * planes : 3 * planes] + parts[3 * planes : 4 * planes])
+            )
+        stacks = []
+        start = first * BLK
+        start_cot = pl.multiple_of((self.side * self.half + self.first) * BLK, BLK)
+        for g, raw in enumerate(raws):
+            slope_in = cots[g][0:1, pl.ds(start_cot, wide)]
+            tanh = jnp.tanh(raw)
+            weights = jnp.exp(4.0 * tanh)
+            norm = jnp.sum(weights, axis=0, keepdims=True)
+            result = jnp.sum(weights * values, axis=0, keepdims=True) / norm
+            depths[g][0:1, pl.ds(pl.multiple_of(start, BLK), wide)] = result
+            slope = (slope_in / norm) * (values - result) * weights
+            draw = slope * (4.0 * (1.0 - tanh * tanh))
+            high = draw.astype(BF16)
+            low = (draw - high.astype(F32)).astype(BF16)
+            stacks.append(jnp.concatenate([high, low, high, high], axis=0))
+        for lanes, stack in zip(groups, stacks):
+            cotangent = jnp.dot(
+                band[...].reshape(planes * channels, BLK), stack, preferred_element_type=F32
+            )
+            dvolume[:, :, lanes] = cotangent.astype(BF16).reshape(planes, channels, wide)
+
     def backward(self, shifted, means, dvolume, ref_grad, grads, sums):
         pairs = V // 2
         channels = ref_grad.shape[0]
@@ -266,69 +305,36 @@
         pl.when(self.side == 1)(lambda: copy(end if outer else 0))
 
 
-def forward_kernel(views, table, inner, matrices, *refs):
-    pieces, (shifted, means, volume, src, base) = refs[:-5], refs[-5:]
+def forward_kernel(views, table, inner, matrices, band, band_t, cot, cot_partner, *refs):
+    pieces, (shifted, means, dvolume, depth, depth_partner, src, base) = refs[:-7], refs[-7:]
     work = Work(views, table, matrices, pieces[0].shape[1], True)
     work.gather(src, base, pieces, None, inner)
-    work.forward(src, base, shifted, means, volume)
+    work.forward(src, base, shifted, means, dvolume)
+    work.depths(
+        band, band_t, (cot, cot_partner), dvolume, dvolume, (depth, depth_partner), 0
+    )
 
 
 def depth_kernel(
-    views, table, outer, inner, matrices, band, band_t, cot, cot_partner,
-    far_volume, *refs,
+    views, table, outer, inner, matrices, band, band_t, cot, cot_partner, far_depth,
+    far_depth_partner, *refs,
 ):
     (
-        depth, depth_partner, far_dvolume, grad_outer, sums,
+        depth, depth_partner, grad_outer, sums,
         src, base, shifted, means, volume, ref_grad,
-    ) = refs[-11 - 2 * V : -2 * V]
-    pieces, grads = refs[: -11 - 2 * V], refs[-2 * V :]
+    ) = refs[-10 - 2 * V : -2 * V]
+    pieces, grads = refs[: -10 - 2 * V], refs[-2 * V :]
     half = pieces[0].shape[1]
-    planes = matrices.shape[0]
-    channels = base.shape[0]
     near = Work(views, table, matrices, half, False)
-    far = Work(views, table, matrices, half, True)
     near.gather(src, base, pieces, outer, inner)
     near.forward(src, base, shifted, means, volume)
-
-    groups = []
-    for work, given, taken in ((near, volume, volume), (far, far_volume, far_dvolume)):
-        wide = len(work.columns) // 2 * BLK
-        for g in range(2):
-            groups.append((work, given, taken, slice(g * wide, (g + 1) * wide), wide, g))
-    raws = []
-    for work, given, _, lanes, wide, g in groups:
-        parts = jnp.dot(
-            band_t[...], given[:, :, lanes].reshape(planes * channels, wide),
-            preferred_element_type=F32,
-        )
-        raws.append(
-            parts[0:planes]
-            + (parts[2 * planes : 3 * planes] + parts[3 * planes : 4 * planes])
-        )
-    stacks = []
-    for (work, _, _, _, wide, g), raw in zip(groups, raws):
-        values = (
-            lax.broadcasted_iota(jnp.int32, (planes, wide), 0).astype(F32) + 1.0
-        ) / planes
-        start = pl.multiple_of(work.first * BLK, BLK)
-        start_all = pl.multiple_of((work.side * half + work.first) * BLK, BLK)
-        slope_in = (cot, cot_partner)[g][0:1, pl.ds(start_all, wide)]
-        tanh = jnp.tanh(raw)
-        weights = jnp.exp(4.0 * tanh)
-        norm = jnp.sum(weights, axis=0, keepdims=True)
-        result = jnp.sum(weights * values, axis=0, keepdims=True) / norm
-        (depth, depth_partner)[g][0:1, pl.ds(start, wide)] = result
-        slope = (slope_in / norm) * (values - result) * weights
-        draw = slope * (4.0 * (1.0 - tanh * tanh))
-        high = draw.astype(BF16)
-        low = (draw - high.astype(F32)).astype(BF16)
-        stacks.append(jnp.concatenate([high, low, high, high], axis=0))
-    for (_, _, taken, lanes, wide, _), stack in zip(groups, stacks):
-        dvolume = jnp.dot(
-            band[...].reshape(planes * channels, BLK), stack, preferred_element_type=F32
-        )
-        taken[:, :, lanes] = dvolume.astype(BF16).reshape(planes, channels, wide)
-
+    near.depths(
+        band, band_t, (cot, cot_partner), volume, volume, (depth, depth_partner), near.first
+    )
+    far_at = pl.multiple_of(jnp.where(near.side == 0, HB, 0) * BLK, BLK)
+    far_wide = far_depth.shape[1]
+    depth[0:1, pl.ds(far_at, far_wide)] = far_depth[...]
+    depth_partner[0:1, pl.ds(far_at, far_wide)] = far_depth_partner[...]
     sums[...] = jnp.zeros_like(sums)
     near.backward(shifted, means, volume, ref_grad, grads, sums)
     near.give(sums, grad_outer, True)
@@ -489,21 +495,20 @@
             ),
         )
 
-    shifted, means, volume = big_call(
-        forward_kernel, 2, 2 + frames // 2,
+    far_half = shape((1, far_pixels // 2), F32)
+    shifted, means, dvolume, *far_depths = big_call(
+        forward_kernel, 2, 6 + frames // 2,
         (
             shape((planes, V, channels, far_pixels), F32),
             shape((planes, channels, far_pixels), F32),
             shape((planes, channels, far_pixels), BF16),
+            far_half, far_half,
         ),
         [sources, pltpu.VMEM((channels, far_pixels), F32)], 4, 1,
-    )(views, table, inner, matrices, *pieces)
-    depth, depth_partner, dvolume, outer, sums = big_call(
-        depth_kernel, 2, 8 + frames // 2,
-        (
-            depth_half, depth_half, shape((planes, channels, far_pixels), BF16), rim_shape,
-            sums_shape,
-        ),
+    )(views, table, inner, matrices, band, band_t, cot_mine, cot_partner, *pieces)
+    depth, depth_partner, outer, sums = big_call(
+        depth_kernel, 2, 9 + frames // 2,
+        (depth_half, depth_half, rim_shape, sums_shape),
         [
             sources,
             pltpu.VMEM((channels, near_pixels), F32),
@@ -514,8 +519,8 @@
         ]
         + accumulators, 20, 2,
     )(
-        views, table, outer, inner, matrices, band, band_t, cot_mine,
-        cot_partner, volume, *pieces,
+        views, table, outer, inner, matrices, band, band_t, cot_mine, cot_partner,
+        *far_depths, *pieces,
     )
     outer = swap_outer(outer)
     core_grad, inner = big_call(

time: 41.6 us -> 41.6 us (level)
  transfers between devices with their start and end apart: 15 -> 15, of which waited for: 10 -> 10; matrix products, arithmetic and copies ran while one was open for 0% -> 0% of each run, Pallas kernels for 14% -> 15%
where the time goes in v5:
time: 41.6 us; the launch traced here: 41.4 us
  Pallas kernels  15.2 us (37%)
  waiting for transfers between devices  13.1 us (31%)
  starting transfers between devices  12.3 us (30%)
  between operations  0.76 us (2%)
    ppermute x13, starting transfers between devices, exchange(): return lax.ppermute(x, 'frame', [(i, i ^ distance) for i in range(count)])  10.7 us
    ppermute x13, waiting for transfers between devices, exchange(): return lax.ppermute(x, 'frame', [(i, i ^ distance) for i in range(count)])  9.11 us
    pallas_call x1, Pallas kernels, per_device(): big_call(depth_kernel, 2, 9 + frames // 2, (depth_half, depth_half, rim_s...  5.25 us
    ppermute x2, waiting for transfers between devices, swap_outer(): lax.ppermute(x, ('frame', 'tile'), pairs + [(b, a) for a, b in pairs])  3.98 us
    pallas_call x1, Pallas kernels, per_device(): big_call(forward_kernel, 2, 6 + frames // 2, (shape((planes, V, channels,...  3.5 us
    pallas_call x1, Pallas kernels, per_device(): big_call(backward_kernel, 2, 5, (shape((frames, half, channels, BLK), F32...  2.86 us
    pallas_call x1, Pallas kernels, per_device(): prepare(head_weight, reg_weight, pltpu.with_memory_space_constraint(kerne...  1.78 us
    ppermute x2, starting transfers between devices, swap_outer(): lax.ppermute(x, ('frame', 'tile'), pairs + [(b, a) for a, b in pairs])  1.62 us
  transfers between devices with their start and end apart: 15, of which 10 were waited for; matrix products, arithmetic and copies ran while one was open for 0% of the time, Pallas kernels for 15%

profile of v5, /device:TPU:0, one launch (start us, length us, event | category | flops | bytes accessed | tf_op | source)
XLA Modules:
  0.0 41.4 jit_solution(11743716590953631983)
XLA Ops:
  0.6 0.6 %collective-permute-start.1 = (bf16[1,32,1024]{2,1,0:T(8,128)(2,1)}, bf16[1,32,1024]{2,1,0:T(8,128)(2,1)S(1)}, u32[]{:S(2)}, u32[]{:S(2)}) collective-permute-start(bf16[1,32,1024]{2,1,0:T(8,128)(2,1)} %refs_0_.1), channel_id=1, source_target_pairs={{0,4},{4,0},{8,12},{12,8},{16,20},{20,16},{24,28},{28,24},{1,5},{5... | collective-permute-start | bytes 196616 | tf_op jit(solution)/shard_map/ppermute | solution.py:407
  1.2 0.9 %stage_arguments.1 = (bf16[1,32,1024]{2,1,0:T(8,128)(2,1)S(1)}, s32[4,8]{1,0:T(4,128)S(1)}, bf16[3,8,32]{2,1,0:T(8,128)(2,1)S(1)}, f32[8]{0:T(128)S(1)}, s32[1,4...) custom-call(bf16[1,32,1024]{2,1,0:T(8,128)(2,1)} %refs_0_.1, s32[4,8]{1,0:T(4,128)} %bitcast.4, bf16[3,8,32]{2,1,0:T(8,128)(2,1)} %refs_2_.1, ...), custom_call_target="tpu_custom_call" | custom-call | tf_op jit(solution)/shard_map/stage_arguments/pallas_call | solution.py:448
  2.3 3.8 %collective-permute-start.4 = (bf16[2,4,32,128]{3,2,1,0:T(8,128)(2,1)S(1)}, bf16[2,4,32,128]{3,2,1,0:T(8,128)(2,1)S(1)}, u32[]{:S(2)}, u32[]{:S(2)}) collective-permute-start(bf16[2,4,32,128]{3,2,1,0:T(8,128)(2,1)S(1)} %shard_map.88.refs_0_), channel_id=1, source_target_pairs={{0,24},{4,28},{8,16},{12,20},{16,8},{20,12},{24,0},{28,4},{1,25},{... | collective-permute-start | bytes 196616 | tf_op jit(solution)/shard_map/ppermute | solution.py:407
  6.2 0.5 %collective-permute-start.3 = (bf16[2,4,32,128]{3,2,1,0:T(8,128)(2,1)S(1)}, bf16[2,4,32,128]{3,2,1,0:T(8,128)(2,1)S(1)}, u32[]{:S(2)}, u32[]{:S(2)}) collective-permute-start(bf16[2,4,32,128]{3,2,1,0:T(8,128)(2,1)S(1)} %shard_map.88.refs_0_), channel_id=1, source_target_pairs={{0,16},{4,20},{8,24},{12,28},{16,0},{20,4},{24,8},{28,12},{1,17},{... | collective-permute-start | bytes 196616 | tf_op jit(solution)/shard_map/ppermute | solution.py:407
  6.8 1.8 %collective-permute-done.4.refs_3_ = bf16[2,4,32,128]{3,2,1,0:T(8,128)(2,1)S(1)} collective-permute-done((bf16[2,4,32,128]{3,2,1,0:T(8,128)(2,1)S(1)}, bf16[2,4,32,128]{3,2,1,0:T(8,128)(2,1)S(1)}, u32[]{:S(2)}, u32[]{:S(2)}) %collective-permute-start.4) | collective-permute-done | bytes 65568 | tf_op jit(solution)/shard_map/ppermute | solution.py:407
  8.6 1.9 %collective-permute-done.3.refs_2_ = bf16[2,4,32,128]{3,2,1,0:T(8,128)(2,1)S(1)} collective-permute-done((bf16[2,4,32,128]{3,2,1,0:T(8,128)(2,1)S(1)}, bf16[2,4,32,128]{3,2,1,0:T(8,128)(2,1)S(1)}, u32[]{:S(2)}, u32[]{:S(2)}) %collective-permute-start.3) | collective-permute-done | bytes 65568 | tf_op jit(solution)/shard_map/ppermute | solution.py:407
  10.4 0.5 %collective-permute-done.2.refs_1_ = bf16[2,4,32,128]{3,2,1,0:T(8,128)(2,1)S(1)} collective-permute-done((bf16[2,4,32,128]{3,2,1,0:T(8,128)(2,1)S(1)}, bf16[2,4,32,128]{3,2,1,0:T(8,128)(2,1)S(1)}, u32[]{:S(2)}, u32[]{:S(2)}) %collective-permute-start.2) | collective-permute-done | bytes 65568 | tf_op jit(solution)/shard_map/ppermute | solution.py:407
  11.1 0.8 %collective-permute-start.7 = (bf16[8,2,32,128]{3,2,1,0:T(8,128)(2,1)S(1)}, bf16[8,2,32,128]{3,2,1,0:T(8,128)(2,1)S(1)}, u32[]{:S(2)}, u32[]{:S(2)}) collective-permute-start(bf16[8,2,32,128]{3,2,1,0:T(8,128)(2,1)S(1)} %get-tuple-element.45), channel_id=1, source_target_pairs={{1,2},{4,5},{6,7},{9,10},{12,13},{14,15},{17,18},{20,21},{22,23},{... | collective-permute-start | bytes 393224 | tf_op jit(solution)/shard_map/ppermute | solution.py:422
  11.9 0.9 %collective-permute-start = (s32[1,4,8,32]{3,2,1,0:T(8,128)}, s32[1,4,8,32]{3,2,1,0:T(8,128)S(1)}, u32[]{:S(2)}, u32[]{:S(2)}) collective-permute-start(s32[1,4,8,32]{3,2,1,0:T(8,128)} %bitcast.3), channel_id=1, source_target_pairs={{0,4},{4,0},{8,12},{12,8},{16,20},{20,16},{24,28},{28,24},{1,5},{5... | collective-permute-start | bytes 12296 | tf_op jit(solution)/shard_map/ppermute | solution.py:407
  12.8 1.8 %shard_map.87 = (bf16[32,32,128]{2,1,0:T(8,128)(2,1)S(1)}, bf16[128,1024]{1,0:T(8,128)(2,1)S(1)}, bf16[32,128,128]{2,1,0:T(8,128)(2,1)S(1)}) custom-call(f32[8]{0:T(128)S(1)} %get-tuple-element.34.head, bf16[3,8,32]{2,1,0:T(8,128)(2,1)S(1)} %get-tuple-element.35.reg, bf16[32,128,128]{2,1,0:T(8,128)(2,1)} %kernels.1), custom_call_target="tpu_custom_call" | custom-call | tf_op jit(solution)/shard_map/pallas_call | solution.py:465
  14.8 3.5 %shard_map.90 = (f32[32,4,32,512]{3,2,1,0:T(8,128)S(1)}, f32[32,32,512]{2,1,0:T(8,128)S(1)}, bf16[32,32,512]{2,1,0:T(8,128)(2,1)S(1)}, f32[1,256]{1,0:T(1,128)S(1)}, f32[1,256]{1,0:T(1,128)S(1)}) custom-call(s32[4,8]{1,0:T(4,128)S(1)} %get-tuple-element.32.views, s32[8,128]{1,0:T(8,128)S(1)} %shard_map.86.table, ...), custom_call_target="tpu_custom_call" | custom-call | flops 536870912 | bytes 4194304 | tf_op jit(solution)/shard_map/pallas_call | solution.py:499
  18.3 5.2 %shard_map.91 = (f32[1,512]{1,0:T(1,128)S(1)}, f32[1,512]{1,0:T(1,128)S(1)}, bf16[8,2,32,128]{3,2,1,0:T(8,128)(2,1)S(1)}, f32[64,32,128]{2,1,0:T(8,128)S(1)}) custom-call(s32[4,8]{1,0:T(4,128)S(1)} %get-tuple-element.32.views, s32[8,128]{1,0:T(8,128)S(1)} %shard_map.86.table, bf16[8,2,32,128]{3,2,1,0:T(8,128)(2,1)S(1)} %collective-permute-done.7.outer, ...), custom_call_target="tpu_custom_call" | custom-call | flops 1073741824 | bytes 4194304 | tf_op jit(solution)/shard_map/pallas_call | solution.py:509
  23.5 2.9 %shard_map.92 = (f32[8,4,32,128]{3,2,1,0:T(8,128)S(1)}, bf16[8,2,32,128]{3,2,1,0:T(8,128)(2,1)S(1)}) custom-call(s32[4,8]{1,0:T(4,128)S(1)} %get-tuple-element.32.views, s32[8,128]{1,0:T(8,128)S(1)} %shard_map.86.table, bf16[32,128,128]{2,1,0:T(8,128)(2,1)S(1)} %get-tuple-element.36.matrices, f32[32,4,32,512]{3,2,1,0:T(8,128)S(1)} %get-tuple-element.42.shifted, ...), custom_call_target="tpu_custom_call" | custom-call | flops 536870912 | bytes 4194304 | tf_op jit(solution)/shard_map/pallas_call | solution.py:526
  26.4 0.5 %collective-permute-start.9 = (bf16[8,2,32,128]{3,2,1,0:T(8,128)(2,1)S(1)}, bf16[8,2,32,128]{3,2,1,0:T(8,128)(2,1)S(1)}, u32[]{:S(2)}, u32[]{:S(2)}) collective-permute-start(bf16[8,2,32,128]{3,2,1,0:T(8,128)(2,1)S(1)} %get-tuple-element.51), channel_id=1, source_target_pairs={{0,4},{4,0},{8,12},{12,8},{16,20},{20,16},{24,28},{28,24},{1,5},{5... | collective-permute-start | bytes 393224 | tf_op jit(solution)/shard_map/ppermute | solution.py:407
  26.9 0.8 %collective-permute-start.8 = (bf16[8,2,32,128]{3,2,1,0:T(8,128)(2,1)S(1)}, bf16[8,2,32,128]{3,2,1,0:T(8,128)(2,1)S(1)}, u32[]{:S(2)}, u32[]{:S(2)}) collective-permute-start(bf16[8,2,32,128]{3,2,1,0:T(8,128)(2,1)S(1)} %get-tuple-element.50), channel_id=1, source_target_pairs={{1,2},{4,5},{6,7},{9,10},{12,13},{14,15},{17,18},{20,21},{22,23},{... | collective-permute-start | bytes 393224 | tf_op jit(solution)/shard_map/ppermute | solution.py:422
  27.9 4.0 %collective-permute-done.8.outer = bf16[8,2,32,128]{3,2,1,0:T(8,128)(2,1)S(1)} collective-permute-done((bf16[8,2,32,128]{3,2,1,0:T(8,128)(2,1)S(1)}, bf16[8,2,32,128]{3,2,1,0:T(8,128)(2,1)S(1)}, u32[]{:S(2)}, u32[]{:S(2)}) %collective-permute-start.8) | collective-permute-done | bytes 131104 | tf_op jit(solution)/shard_map/ppermute | solution.py:422
  32.0 0.8 %collective-permute-start.10 = (bf16[2,4,32,128]{3,2,1,0:T(8,128)(2,1)S(1)}, bf16[2,4,32,128]{3,2,1,0:T(8,128)(2,1)S(1)}, u32[]{:S(2)}, u32[]{:S(2)}) collective-permute-start(bf16[2,4,32,128]{3,2,1,0:T(8,128)(2,1)S(1)} %get-tuple-element.53), channel_id=1, source_target_pairs={{0,8},{4,12},{8,0},{12,4},{16,24},{20,28},{24,16},{28,20},{1,9},{5... | collective-permute-start | bytes 196616 | tf_op jit(solution)/shard_map/ppermute | solution.py:407
  32.8 1.3 %collective-permute-start.11 = (bf16[2,4,32,128]{3,2,1,0:T(8,128)(2,1)S(1)}, bf16[2,4,32,128]{3,2,1,0:T(8,128)(2,1)S(1)}, u32[]{:S(2)}, u32[]{:S(2)}) collective-permute-start(bf16[2,4,32,128]{3,2,1,0:T(8,128)(2,1)S(1)} %get-tuple-element.54), channel_id=1, source_target_pairs={{0,16},{4,20},{8,24},{12,28},{16,0},{20,4},{24,8},{28,12},{1,17},{... | collective-permute-start | bytes 196616 | tf_op jit(solution)/shard_map/ppermute | solution.py:407
  34.1 1.4 %collective-permute-start.12 = (bf16[2,4,32,128]{3,2,1,0:T(8,128)(2,1)S(1)}, bf16[2,4,32,128]{3,2,1,0:T(8,128)(2,1)S(1)}, u32[]{:S(2)}, u32[]{:S(2)}) collective-permute-start(bf16[2,4,32,128]{3,2,1,0:T(8,128)(2,1)S(1)} %get-tuple-element.55), channel_id=1, source_target_pairs={{0,24},{4,28},{8,16},{12,20},{16,8},{20,12},{24,0},{28,4},{1,25},{... | collective-permute-start | bytes 196616 | tf_op jit(solution)/shard_map/ppermute | solution.py:407
  35.5 1.4 %collective-permute-done.10.refs_0_ = bf16[2,4,32,128]{3,2,1,0:T(8,128)(2,1)S(1)} collective-permute-done((bf16[2,4,32,128]{3,2,1,0:T(8,128)(2,1)S(1)}, bf16[2,4,32,128]{3,2,1,0:T(8,128)(2,1)S(1)}, u32[]{:S(2)}, u32[]{:S(2)}) %collective-permute-start.10) | collective-permute-done | bytes 65568 | tf_op jit(solution)/shard_map/ppermute | solution.py:407
  36.9 0.8 %collective-permute-done.11.refs_1_ = bf16[2,4,32,128]{3,2,1,0:T(8,128)(2,1)S(1)} collective-permute-done((bf16[2,4,32,128]{3,2,1,0:T(8,128)(2,1)S(1)}, bf16[2,4,32,128]{3,2,1,0:T(8,128)(2,1)S(1)}, u32[]{:S(2)}, u32[]{:S(2)}) %collective-permute-start.11) | collective-permute-done | bytes 65568 | tf_op jit(solution)/shard_map/ppermute | solution.py:407
  37.8 1.5 %collective-permute-done.12.refs_2_ = bf16[2,4,32,128]{3,2,1,0:T(8,128)(2,1)S(1)} collective-permute-done((bf16[2,4,32,128]{3,2,1,0:T(8,128)(2,1)S(1)}, bf16[2,4,32,128]{3,2,1,0:T(8,128)(2,1)S(1)}, u32[]{:S(2)}, u32[]{:S(2)}) %collective-permute-start.12) | collective-permute-done | bytes 65568 | tf_op jit(solution)/shard_map/ppermute | solution.py:407
  39.9 0.8 %collective-permute-done.14.depth_partner = f32[1,512]{1,0:T(1,128)S(1)} collective-permute-done((f32[1,512]{1,0:T(1,128)S(1)}, f32[1,512]{1,0:T(1,128)S(1)}, u32[]{:S(2)}, u32[]{:S(2)}) %collective-permute-start.14) | collective-permute-done | bytes 2080 | tf_op jit(solution)/shard_map/ppermute | solution.py:407
  40.7 0.7 %shard_map.95 = (f32[1,32,1024]{2,1,0:T(8,128)}, f32[1,1024]{1,0:T(1,128)}) custom-call(f32[4,32,128]{2,1,0:T(8,128)S(1)} %get-tuple-element.56.mine, bf16[4,32,128]{2,1,0:T(8,128)(2,1)S(1)} %collective-permute-done.13.partner, f32[1,512]{1,0:T(1,128)S(1)} %get-tuple-element.58.depth_mine, f32[1,512]{1,0:T(1,128)S(1)} %collective-permute-done.14.depth_partner), custom_call_target="tpu_custom_call" | custom-call | tf_op jit(solution)/shard_map/pallas_call | solution.py:546
  (17 shorter events, 1.4 us)
Async XLA Ops:
  0.6 1.7 %collective-permute-start.1 = (bf16[1,32,1024]{2,1,0:T(8,128)(2,1)}, bf16[1,32,1024]{2,1,0:T(8,128)(2,1)S(1)}, u32[]{:S(2)}, u32[]{:S(2)}) collective-permute-start(bf16[1,32,1024]{2,1,0:T(8,128)(2,1)} %refs_0_.1), channel_id=1, source_target_pairs={{0,4},{4,0},{8,12},{12,8},{16,20},{20,16},{24,28},{28,24},{1,5},{5... | collective-permute-start | bytes 196616 | tf_op jit(solution)/shard_map/ppermute | solution.py:407
  2.3 6.3 %collective-permute-start.4 = (bf16[2,4,32,128]{3,2,1,0:T(8,128)(2,1)S(1)}, bf16[2,4,32,128]{3,2,1,0:T(8,128)(2,1)S(1)}, u32[]{:S(2)}, u32[]{:S(2)}) collective-permute-start(bf16[2,4,32,128]{3,2,1,0:T(8,128)(2,1)S(1)} %shard_map.88.refs_0_), channel_id=1, source_target_pairs={{0,24},{4,28},{8,16},{12,20},{16,8},{20,12},{24,0},{28,4},{1,25},{... | collective-permute-start | bytes 196616 | tf_op jit(solution)/shard_map/ppermute | solution.py:407
  6.2 4.3 %collective-permute-start.3 = (bf16[2,4,32,128]{3,2,1,0:T(8,128)(2,1)S(1)}, bf16[2,4,32,128]{3,2,1,0:T(8,128)(2,1)S(1)}, u32[]{:S(2)}, u32[]{:S(2)}) collective-permute-start(bf16[2,4,32,128]{3,2,1,0:T(8,128)(2,1)S(1)} %shard_map.88.refs_0_), channel_id=1, source_target_pairs={{0,16},{4,20},{8,24},{12,28},{16,0},{20,4},{24,8},{28,12},{1,17},{... | collective-permute-start | bytes 196616 | tf_op jit(solution)/shard_map/ppermute | solution.py:407
  6.7 4.3 %collective-permute-start.2 = (bf16[2,4,32,128]{3,2,1,0:T(8,128)(2,1)S(1)}, bf16[2,4,32,128]{3,2,1,0:T(8,128)(2,1)S(1)}, u32[]{:S(2)}, u32[]{:S(2)}) collective-permute-start(bf16[2,4,32,128]{3,2,1,0:T(8,128)(2,1)S(1)} %shard_map.88.refs_0_), channel_id=1, source_target_pairs={{0,8},{4,12},{8,0},{12,4},{16,24},{20,28},{24,16},{28,20},{1,9},{5... | collective-permute-start | bytes 196616 | tf_op jit(solution)/shard_map/ppermute | solution.py:407
  11.0 3.8 %collective-permute-start.5 = (bf16[8,2,32,128]{3,2,1,0:T(8,128)(2,1)S(1)}, bf16[8,2,32,128]{3,2,1,0:T(8,128)(2,1)S(1)}, u32[]{:S(2)}, u32[]{:S(2)}) collective-permute-start(bf16[8,2,32,128]{3,2,1,0:T(8,128)(2,1)S(1)} %get-tuple-element.38), channel_id=1, source_target_pairs={{0,4},{4,0},{8,12},{12,8},{16,20},{20,16},{24,28},{28,24},{1,5},{5... | collective-permute-start | bytes 393224 | tf_op jit(solution)/shard_map/ppermute | solution.py:407
  11.1 7.2 %collective-permute-start.7 = (bf16[8,2,32,128]{3,2,1,0:T(8,128)(2,1)S(1)}, bf16[8,2,32,128]{3,2,1,0:T(8,128)(2,1)S(1)}, u32[]{:S(2)}, u32[]{:S(2)}) collective-permute-start(bf16[8,2,32,128]{3,2,1,0:T(8,128)(2,1)S(1)} %get-tuple-element.45), channel_id=1, source_target_pairs={{1,2},{4,5},{6,7},{9,10},{12,13},{14,15},{17,18},{20,21},{22,23},{... | collective-permute-start | bytes 393224 | tf_op jit(solution)/shard_map/ppermute | solution.py:422
  11.9 2.7 %collective-permute-start = (s32[1,4,8,32]{3,2,1,0:T(8,128)}, s32[1,4,8,32]{3,2,1,0:T(8,128)S(1)}, u32[]{:S(2)}, u32[]{:S(2)}) collective-permute-start(s32[1,4,8,32]{3,2,1,0:T(8,128)} %bitcast.3), channel_id=1, source_target_pairs={{0,4},{4,0},{8,12},{12,8},{16,20},{20,16},{24,28},{28,24},{1,5},{5... | collective-permute-start | bytes 12296 | tf_op jit(solution)/shard_map/ppermute | solution.py:407
  12.8 1.9 %collective-permute-start.6 = (f32[1,1024]{1,0:T(1,128)}, f32[1,1024]{1,0:T(1,128)S(1)}, u32[]{:S(2)}, u32[]{:S(2)}) collective-permute-start(f32[1,1024]{1,0:T(1,128)} %refs_5_.1), channel_id=1, source_target_pairs={{0,4},{4,0},{8,12},{12,8},{16,20},{20,16},{24,28},{28,24},{1,5},{5... | collective-permute-start | bytes 12296 | tf_op jit(solution)/shard_map/ppermute | solution.py:407
  26.4 1.5 %collective-permute-start.9 = (bf16[8,2,32,128]{3,2,1,0:T(8,128)(2,1)S(1)}, bf16[8,2,32,128]{3,2,1,0:T(8,128)(2,1)S(1)}, u32[]{:S(2)}, u32[]{:S(2)}) collective-permute-start(bf16[8,2,32,128]{3,2,1,0:T(8,128)(2,1)S(1)} %get-tuple-element.51), channel_id=1, source_target_pairs={{0,4},{4,0},{8,12},{12,8},{16,20},{20,16},{24,28},{28,24},{1,5},{5... | collective-permute-start | bytes 393224 | tf_op jit(solution)/shard_map/ppermute | solution.py:407
  26.9 5.0 %collective-permute-start.8 = (bf16[8,2,32,128]{3,2,1,0:T(8,128)(2,1)S(1)}, bf16[8,2,32,128]{3,2,1,0:T(8,128)(2,1)S(1)}, u32[]{:S(2)}, u32[]{:S(2)}) collective-permute-start(bf16[8,2,32,128]{3,2,1,0:T(8,128)(2,1)S(1)} %get-tuple-element.50), channel_id=1, source_target_pairs={{1,2},{4,5},{6,7},{9,10},{12,13},{14,15},{17,18},{20,21},{22,23},{... | collective-permute-start | bytes 393224 | tf_op jit(solution)/shard_map/ppermute | solution.py:422
  32.0 5.0 %collective-permute-start.10 = (bf16[2,4,32,128]{3,2,1,0:T(8,128)(2,1)S(1)}, bf16[2,4,32,128]{3,2,1,0:T(8,128)(2,1)S(1)}, u32[]{:S(2)}, u32[]{:S(2)}) collective-permute-start(bf16[2,4,32,128]{3,2,1,0:T(8,128)(2,1)S(1)} %get-tuple-element.53), channel_id=1, source_target_pairs={{0,8},{4,12},{8,0},{12,4},{16,24},{20,28},{24,16},{28,20},{1,9},{5... | collective-permute-start | bytes 196616 | tf_op jit(solution)/shard_map/ppermute | solution.py:407
  32.8 5.0 %collective-permute-start.11 = (bf16[2,4,32,128]{3,2,1,0:T(8,128)(2,1)S(1)}, bf16[2,4,32,128]{3,2,1,0:T(8,128)(2,1)S(1)}, u32[]{:S(2)}, u32[]{:S(2)}) collective-permute-start(bf16[2,4,32,128]{3,2,1,0:T(8,128)(2,1)S(1)} %get-tuple-element.54), channel_id=1, source_target_pairs={{0,16},{4,20},{8,24},{12,28},{16,0},{20,4},{24,8},{28,12},{1,17},{... | collective-permute-start | bytes 196616 | tf_op jit(solution)/shard_map/ppermute | solution.py:407
  34.1 5.2 %collective-permute-start.12 = (bf16[2,4,32,128]{3,2,1,0:T(8,128)(2,1)S(1)}, bf16[2,4,32,128]{3,2,1,0:T(8,128)(2,1)S(1)}, u32[]{:S(2)}, u32[]{:S(2)}) collective-permute-start(bf16[2,4,32,128]{3,2,1,0:T(8,128)(2,1)S(1)} %get-tuple-element.55), channel_id=1, source_target_pairs={{0,24},{4,28},{8,16},{12,20},{16,8},{20,12},{24,0},{28,4},{1,25},{... | collective-permute-start | bytes 196616 | tf_op jit(solution)/shard_map/ppermute | solution.py:407
  39.3 1.4 %collective-permute-start.13 = (bf16[4,32,128]{2,1,0:T(8,128)(2,1)S(1)}, bf16[4,32,128]{2,1,0:T(8,128)(2,1)S(1)}, u32[]{:S(2)}, u32[]{:S(2)}) collective-permute-start(bf16[4,32,128]{2,1,0:T(8,128)(2,1)S(1)} %get-tuple-element.57), channel_id=1, source_target_pairs={{0,4},{4,0},{8,12},{12,8},{16,20},{20,16},{24,28},{28,24},{1,5},{5... | collective-permute-start | bytes 98312 | tf_op jit(solution)/shard_map/ppermute | solution.py:407
  39.4 1.3 %collective-permute-start.14 = (f32[1,512]{1,0:T(1,128)S(1)}, f32[1,512]{1,0:T(1,128)S(1)}, u32[]{:S(2)}, u32[]{:S(2)}) collective-permute-start(f32[1,512]{1,0:T(1,128)S(1)} %get-tuple-element.59), channel_id=1, source_target_pairs={{0,4},{4,0},{8,12},{12,8},{16,20},{20,16},{24,28},{28,24},{1,5},{5... | collective-permute-start | bytes 6152 | tf_op jit(solution)/shard_map/ppermute | solution.py:407

commit v6 on v5

--- a/solution.py
+++ b/solution.py
@@ -271,19 +271,15 @@
                 for i in range(pairs):
                     plus = dvar * (shifted[d, 2 * i, :, lanes] - twice_mean)
                     minus = dvar * shifted[d, 2 * i + 1, :, lanes]
-                    rows.append(
-                        jnp.concatenate([plus.astype(BF16), minus.astype(BF16)], axis=1)
-                    )
+                    rows += [(plus + minus).astype(BF16), (plus - minus).astype(BF16)]
             dpicked = lax.dot_general(
-                jnp.concatenate(rows, axis=0), self.pair_matrix(d),
+                jnp.concatenate(rows, axis=0), self.matrices[d],
                 (((1,), (1,)), ((), ())), preferred_element_type=F32,
             )
             for k, (g, b) in enumerate(self.columns):
-                for i in range(pairs):
-                    for j, part in ((2 * i, slice(0, BLK)), (2 * i + 1, slice(BLK, None))):
-                        grads[g * V + j][self.block_of(d, g, b, j)] += dpicked[
-                            self.rows_of(k, i, channels), part
-                        ]
+                for j in range(V):
+                    start = (k * V + j) * channels
+                    grads[g * V + j][self.block_of(d, g, b, j)] += dpicked[start : start + channels]
             return carry
 
         lax.fori_loop(0, self.planes, plane, 0, unroll=BACKWARD)

time: 41.6 us -> 41.2 us (level)
  no operation moved by 1% of the time
where the time goes in v6:
time: 41.2 us; the launch traced here: 41 us
  Pallas kernels  14.9 us (36%)
  waiting for transfers between devices  13.1 us (32%)
  starting transfers between devices  12.4 us (30%)
  between operations  0.76 us (2%)
    ppermute x13, starting transfers between devices, exchange(): return lax.ppermute(x, 'frame', [(i, i ^ distance) for i in range(count)])  10.7 us
    ppermute x13, waiting for transfers between devices, exchange(): return lax.ppermute(x, 'frame', [(i, i ^ distance) for i in range(count)])  9.08 us
    pallas_call x1, Pallas kernels, per_device(): big_call(depth_kernel, 2, 9 + frames // 2, (depth_half, depth_half, rim_s...  4.92 us
    ppermute x2, waiting for transfers between devices, swap_outer(): lax.ppermute(x, ('frame', 'tile'), pairs + [(b, a) for a, b in pairs])  3.98 us
    pallas_call x1, Pallas kernels, per_device(): big_call(forward_kernel, 2, 6 + frames // 2, (shape((planes, V, channels,...  3.5 us
    pallas_call x1, Pallas kernels, per_device(): big_call(backward_kernel, 2, 5, (shape((frames, half, channels, BLK), F32...  2.87 us
    pallas_call x1, Pallas kernels, per_device(): prepare(head_weight, reg_weight, pltpu.with_memory_space_constraint(kerne...  1.78 us
    ppermute x2, starting transfers between devices, swap_outer(): lax.ppermute(x, ('frame', 'tile'), pairs + [(b, a) for a, b in pairs])  1.63 us
  transfers between devices with their start and end apart: 15, of which 10 were waited for; matrix products, arithmetic and copies ran while one was open for 0% of the time, Pallas kernels for 15%

profile of v6, /device:TPU:0, one launch (start us, length us, event | category | flops | bytes accessed | tf_op | source)
XLA Modules:
  0.0 41.0 jit_solution(11304248895195845646)
XLA Ops:
  0.6 0.6 %collective-permute-start.1 = (bf16[1,32,1024]{2,1,0:T(8,128)(2,1)}, bf16[1,32,1024]{2,1,0:T(8,128)(2,1)S(1)}, u32[]{:S(2)}, u32[]{:S(2)}) collective-permute-start(bf16[1,32,1024]{2,1,0:T(8,128)(2,1)} %refs_0_.1), channel_id=1, source_target_pairs={{0,4},{4,0},{8,12},{12,8},{16,20},{20,16},{24,28},{28,24},{1,5},{5... | collective-permute-start | bytes 196616 | tf_op jit(solution)/shard_map/ppermute | solution.py:403
  1.2 0.9 %stage_arguments.1 = (bf16[1,32,1024]{2,1,0:T(8,128)(2,1)S(1)}, s32[4,8]{1,0:T(4,128)S(1)}, bf16[3,8,32]{2,1,0:T(8,128)(2,1)S(1)}, f32[8]{0:T(128)S(1)}, s32[1,4...) custom-call(bf16[1,32,1024]{2,1,0:T(8,128)(2,1)} %refs_0_.1, s32[4,8]{1,0:T(4,128)} %bitcast.4, bf16[3,8,32]{2,1,0:T(8,128)(2,1)} %refs_2_.1, ...), custom_call_target="tpu_custom_call" | custom-call | tf_op jit(solution)/shard_map/stage_arguments/pallas_call | solution.py:444
  2.3 3.8 %collective-permute-start.4 = (bf16[2,4,32,128]{3,2,1,0:T(8,128)(2,1)S(1)}, bf16[2,4,32,128]{3,2,1,0:T(8,128)(2,1)S(1)}, u32[]{:S(2)}, u32[]{:S(2)}) collective-permute-start(bf16[2,4,32,128]{3,2,1,0:T(8,128)(2,1)S(1)} %shard_map.88.refs_0_), channel_id=1, source_target_pairs={{0,24},{4,28},{8,16},{12,20},{16,8},{20,12},{24,0},{28,4},{1,25},{... | collective-permute-start | bytes 196616 | tf_op jit(solution)/shard_map/ppermute | solution.py:403
  6.2 0.5 %collective-permute-start.3 = (bf16[2,4,32,128]{3,2,1,0:T(8,128)(2,1)S(1)}, bf16[2,4,32,128]{3,2,1,0:T(8,128)(2,1)S(1)}, u32[]{:S(2)}, u32[]{:S(2)}) collective-permute-start(bf16[2,4,32,128]{3,2,1,0:T(8,128)(2,1)S(1)} %shard_map.88.refs_0_), channel_id=1, source_target_pairs={{0,16},{4,20},{8,24},{12,28},{16,0},{20,4},{24,8},{28,12},{1,17},{... | collective-permute-start | bytes 196616 | tf_op jit(solution)/shard_map/ppermute | solution.py:403
  6.8 1.8 %collective-permute-done.4.refs_3_ = bf16[2,4,32,128]{3,2,1,0:T(8,128)(2,1)S(1)} collective-permute-done((bf16[2,4,32,128]{3,2,1,0:T(8,128)(2,1)S(1)}, bf16[2,4,32,128]{3,2,1,0:T(8,128)(2,1)S(1)}, u32[]{:S(2)}, u32[]{:S(2)}) %collective-permute-start.4) | collective-permute-done | bytes 65568 | tf_op jit(solution)/shard_map/ppermute | solution.py:403
  8.6 1.9 %collective-permute-done.3.refs_2_ = bf16[2,4,32,128]{3,2,1,0:T(8,128)(2,1)S(1)} collective-permute-done((bf16[2,4,32,128]{3,2,1,0:T(8,128)(2,1)S(1)}, bf16[2,4,32,128]{3,2,1,0:T(8,128)(2,1)S(1)}, u32[]{:S(2)}, u32[]{:S(2)}) %collective-permute-start.3) | collective-permute-done | bytes 65568 | tf_op jit(solution)/shard_map/ppermute | solution.py:403
  10.4 0.5 %collective-permute-done.2.refs_1_ = bf16[2,4,32,128]{3,2,1,0:T(8,128)(2,1)S(1)} collective-permute-done((bf16[2,4,32,128]{3,2,1,0:T(8,128)(2,1)S(1)}, bf16[2,4,32,128]{3,2,1,0:T(8,128)(2,1)S(1)}, u32[]{:S(2)}, u32[]{:S(2)}) %collective-permute-start.2) | collective-permute-done | bytes 65568 | tf_op jit(solution)/shard_map/ppermute | solution.py:403
  11.1 0.8 %collective-permute-start.7 = (bf16[8,2,32,128]{3,2,1,0:T(8,128)(2,1)S(1)}, bf16[8,2,32,128]{3,2,1,0:T(8,128)(2,1)S(1)}, u32[]{:S(2)}, u32[]{:S(2)}) collective-permute-start(bf16[8,2,32,128]{3,2,1,0:T(8,128)(2,1)S(1)} %get-tuple-element.45), channel_id=1, source_target_pairs={{1,2},{4,5},{6,7},{9,10},{12,13},{14,15},{17,18},{20,21},{22,23},{... | collective-permute-start | bytes 393224 | tf_op jit(solution)/shard_map/ppermute | solution.py:418
  11.9 0.9 %collective-permute-start = (s32[1,4,8,32]{3,2,1,0:T(8,128)}, s32[1,4,8,32]{3,2,1,0:T(8,128)S(1)}, u32[]{:S(2)}, u32[]{:S(2)}) collective-permute-start(s32[1,4,8,32]{3,2,1,0:T(8,128)} %bitcast.3), channel_id=1, source_target_pairs={{0,4},{4,0},{8,12},{12,8},{16,20},{20,16},{24,28},{28,24},{1,5},{5... | collective-permute-start | bytes 12296 | tf_op jit(solution)/shard_map/ppermute | solution.py:403
  12.8 1.8 %shard_map.87 = (bf16[32,32,128]{2,1,0:T(8,128)(2,1)S(1)}, bf16[128,1024]{1,0:T(8,128)(2,1)S(1)}, bf16[32,128,128]{2,1,0:T(8,128)(2,1)S(1)}) custom-call(f32[8]{0:T(128)S(1)} %get-tuple-element.34.head, bf16[3,8,32]{2,1,0:T(8,128)(2,1)S(1)} %get-tuple-element.35.reg, bf16[32,128,128]{2,1,0:T(8,128)(2,1)} %kernels.1), custom_call_target="tpu_custom_call" | custom-call | tf_op jit(solution)/shard_map/pallas_call | solution.py:461
  14.8 3.5 %shard_map.90 = (f32[32,4,32,512]{3,2,1,0:T(8,128)S(1)}, f32[32,32,512]{2,1,0:T(8,128)S(1)}, bf16[32,32,512]{2,1,0:T(8,128)(2,1)S(1)}, f32[1,256]{1,0:T(1,128)S(1)}, f32[1,256]{1,0:T(1,128)S(1)}) custom-call(s32[4,8]{1,0:T(4,128)S(1)} %get-tuple-element.32.views, s32[8,128]{1,0:T(8,128)S(1)} %shard_map.86.table, ...), custom_call_target="tpu_custom_call" | custom-call | flops 536870912 | bytes 4194304 | tf_op jit(solution)/shard_map/pallas_call | solution.py:495
  18.3 4.9 %shard_map.91 = (f32[1,512]{1,0:T(1,128)S(1)}, f32[1,512]{1,0:T(1,128)S(1)}, bf16[8,2,32,128]{3,2,1,0:T(8,128)(2,1)S(1)}, f32[64,32,128]{2,1,0:T(8,128)S(1)}) custom-call(s32[4,8]{1,0:T(4,128)S(1)} %get-tuple-element.32.views, s32[8,128]{1,0:T(8,128)S(1)} %shard_map.86.table, bf16[8,2,32,128]{3,2,1,0:T(8,128)(2,1)S(1)} %collective-permute-done.7.outer, ...), custom_call_target="tpu_custom_call" | custom-call | flops 1073741824 | bytes 4194304 | tf_op jit(solution)/shard_map/pallas_call | solution.py:505
  23.2 2.9 %shard_map.92 = (f32[8,4,32,128]{3,2,1,0:T(8,128)S(1)}, bf16[8,2,32,128]{3,2,1,0:T(8,128)(2,1)S(1)}) custom-call(s32[4,8]{1,0:T(4,128)S(1)} %get-tuple-element.32.views, s32[8,128]{1,0:T(8,128)S(1)} %shard_map.86.table, bf16[32,128,128]{2,1,0:T(8,128)(2,1)S(1)} %get-tuple-element.36.matrices, f32[32,4,32,512]{3,2,1,0:T(8,128)S(1)} %get-tuple-element.42.shifted, ...), custom_call_target="tpu_custom_call" | custom-call | flops 536870912 | bytes 4194304 | tf_op jit(solution)/shard_map/pallas_call | solution.py:522
  26.1 0.5 %collective-permute-start.9 = (bf16[8,2,32,128]{3,2,1,0:T(8,128)(2,1)S(1)}, bf16[8,2,32,128]{3,2,1,0:T(8,128)(2,1)S(1)}, u32[]{:S(2)}, u32[]{:S(2)}) collective-permute-start(bf16[8,2,32,128]{3,2,1,0:T(8,128)(2,1)S(1)} %get-tuple-element.51), channel_id=1, source_target_pairs={{0,4},{4,0},{8,12},{12,8},{16,20},{20,16},{24,28},{28,24},{1,5},{5... | collective-permute-start | bytes 393224 | tf_op jit(solution)/shard_map/ppermute | solution.py:403
  26.6 0.8 %collective-permute-start.8 = (bf16[8,2,32,128]{3,2,1,0:T(8,128)(2,1)S(1)}, bf16[8,2,32,128]{3,2,1,0:T(8,128)(2,1)S(1)}, u32[]{:S(2)}, u32[]{:S(2)}) collective-permute-start(bf16[8,2,32,128]{3,2,1,0:T(8,128)(2,1)S(1)} %get-tuple-element.50), channel_id=1, source_target_pairs={{1,2},{4,5},{6,7},{9,10},{12,13},{14,15},{17,18},{20,21},{22,23},{... | collective-permute-start | bytes 393224 | tf_op jit(solution)/shard_map/ppermute | solution.py:418
  27.6 4.0 %collective-permute-done.8.outer = bf16[8,2,32,128]{3,2,1,0:T(8,128)(2,1)S(1)} collective-permute-done((bf16[8,2,32,128]{3,2,1,0:T(8,128)(2,1)S(1)}, bf16[8,2,32,128]{3,2,1,0:T(8,128)(2,1)S(1)}, u32[]{:S(2)}, u32[]{:S(2)}) %collective-permute-start.8) | collective-permute-done | bytes 131104 | tf_op jit(solution)/shard_map/ppermute | solution.py:418
  31.7 0.8 %collective-permute-start.10 = (bf16[2,4,32,128]{3,2,1,0:T(8,128)(2,1)S(1)}, bf16[2,4,32,128]{3,2,1,0:T(8,128)(2,1)S(1)}, u32[]{:S(2)}, u32[]{:S(2)}) collective-permute-start(bf16[2,4,32,128]{3,2,1,0:T(8,128)(2,1)S(1)} %get-tuple-element.53), channel_id=1, source_target_pairs={{0,8},{4,12},{8,0},{12,4},{16,24},{20,28},{24,16},{28,20},{1,9},{5... | collective-permute-start | bytes 196616 | tf_op jit(solution)/shard_map/ppermute | solution.py:403
  32.5 1.3 %collective-permute-start.11 = (bf16[2,4,32,128]{3,2,1,0:T(8,128)(2,1)S(1)}, bf16[2,4,32,128]{3,2,1,0:T(8,128)(2,1)S(1)}, u32[]{:S(2)}, u32[]{:S(2)}) collective-permute-start(bf16[2,4,32,128]{3,2,1,0:T(8,128)(2,1)S(1)} %get-tuple-element.54), channel_id=1, source_target_pairs={{0,16},{4,20},{8,24},{12,28},{16,0},{20,4},{24,8},{28,12},{1,17},{... | collective-permute-start | bytes 196616 | tf_op jit(solution)/shard_map/ppermute | solution.py:403
  33.8 1.4 %collective-permute-start.12 = (bf16[2,4,32,128]{3,2,1,0:T(8,128)(2,1)S(1)}, bf16[2,4,32,128]{3,2,1,0:T(8,128)(2,1)S(1)}, u32[]{:S(2)}, u32[]{:S(2)}) collective-permute-start(bf16[2,4,32,128]{3,2,1,0:T(8,128)(2,1)S(1)} %get-tuple-element.55), channel_id=1, source_target_pairs={{0,24},{4,28},{8,16},{12,20},{16,8},{20,12},{24,0},{28,4},{1,25},{... | collective-permute-start | bytes 196616 | tf_op jit(solution)/shard_map/ppermute | solution.py:403
  35.2 1.4 %collective-permute-done.10.refs_0_ = bf16[2,4,32,128]{3,2,1,0:T(8,128)(2,1)S(1)} collective-permute-done((bf16[2,4,32,128]{3,2,1,0:T(8,128)(2,1)S(1)}, bf16[2,4,32,128]{3,2,1,0:T(8,128)(2,1)S(1)}, u32[]{:S(2)}, u32[]{:S(2)}) %collective-permute-start.10) | collective-permute-done | bytes 65568 | tf_op jit(solution)/shard_map/ppermute | solution.py:403
  36.7 0.8 %collective-permute-done.11.refs_1_ = bf16[2,4,32,128]{3,2,1,0:T(8,128)(2,1)S(1)} collective-permute-done((bf16[2,4,32,128]{3,2,1,0:T(8,128)(2,1)S(1)}, bf16[2,4,32,128]{3,2,1,0:T(8,128)(2,1)S(1)}, u32[]{:S(2)}, u32[]{:S(2)}) %collective-permute-start.11) | collective-permute-done | bytes 65568 | tf_op jit(solution)/shard_map/ppermute | solution.py:403
  37.5 1.5 %collective-permute-done.12.refs_2_ = bf16[2,4,32,128]{3,2,1,0:T(8,128)(2,1)S(1)} collective-permute-done((bf16[2,4,32,128]{3,2,1,0:T(8,128)(2,1)S(1)}, bf16[2,4,32,128]{3,2,1,0:T(8,128)(2,1)S(1)}, u32[]{:S(2)}, u32[]{:S(2)}) %collective-permute-start.12) | collective-permute-done | bytes 65568 | tf_op jit(solution)/shard_map/ppermute | solution.py:403
  39.5 0.8 %collective-permute-done.14.depth_partner = f32[1,512]{1,0:T(1,128)S(1)} collective-permute-done((f32[1,512]{1,0:T(1,128)S(1)}, f32[1,512]{1,0:T(1,128)S(1)}, u32[]{:S(2)}, u32[]{:S(2)}) %collective-permute-start.14) | collective-permute-done | bytes 2080 | tf_op jit(solution)/shard_map/ppermute | solution.py:403
  40.4 0.7 %shard_map.95 = (f32[1,32,1024]{2,1,0:T(8,128)}, f32[1,1024]{1,0:T(1,128)}) custom-call(f32[4,32,128]{2,1,0:T(8,128)S(1)} %get-tuple-element.56.mine, bf16[4,32,128]{2,1,0:T(8,128)(2,1)S(1)} %collective-permute-done.13.partner, f32[1,512]{1,0:T(1,128)S(1)} %get-tuple-element.58.depth_mine, f32[1,512]{1,0:T(1,128)S(1)} %collective-permute-done.14.depth_partner), custom_call_target="tpu_custom_call" | custom-call | tf_op jit(solution)/shard_map/pallas_call | solution.py:542
  (17 shorter events, 1.4 us)
Async XLA Ops:
  0.6 1.7 %collective-permute-start.1 = (bf16[1,32,1024]{2,1,0:T(8,128)(2,1)}, bf16[1,32,1024]{2,1,0:T(8,128)(2,1)S(1)}, u32[]{:S(2)}, u32[]{:S(2)}) collective-permute-start(bf16[1,32,1024]{2,1,0:T(8,128)(2,1)} %refs_0_.1), channel_id=1, source_target_pairs={{0,4},{4,0},{8,12},{12,8},{16,20},{20,16},{24,28},{28,24},{1,5},{5... | collective-permute-start | bytes 196616 | tf_op jit(solution)/shard_map/ppermute | solution.py:403
  2.3 6.3 %collective-permute-start.4 = (bf16[2,4,32,128]{3,2,1,0:T(8,128)(2,1)S(1)}, bf16[2,4,32,128]{3,2,1,0:T(8,128)(2,1)S(1)}, u32[]{:S(2)}, u32[]{:S(2)}) collective-permute-start(bf16[2,4,32,128]{3,2,1,0:T(8,128)(2,1)S(1)} %shard_map.88.refs_0_), channel_id=1, source_target_pairs={{0,24},{4,28},{8,16},{12,20},{16,8},{20,12},{24,0},{28,4},{1,25},{... | collective-permute-start | bytes 196616 | tf_op jit(solution)/shard_map/ppermute | solution.py:403
  6.2 4.3 %collective-permute-start.3 = (bf16[2,4,32,128]{3,2,1,0:T(8,128)(2,1)S(1)}, bf16[2,4,32,128]{3,2,1,0:T(8,128)(2,1)S(1)}, u32[]{:S(2)}, u32[]{:S(2)}) collective-permute-start(bf16[2,4,32,128]{3,2,1,0:T(8,128)(2,1)S(1)} %shard_map.88.refs_0_), channel_id=1, source_target_pairs={{0,16},{4,20},{8,24},{12,28},{16,0},{20,4},{24,8},{28,12},{1,17},{... | collective-permute-start | bytes 196616 | tf_op jit(solution)/shard_map/ppermute | solution.py:403
  6.7 4.3 %collective-permute-start.2 = (bf16[2,4,32,128]{3,2,1,0:T(8,128)(2,1)S(1)}, bf16[2,4,32,128]{3,2,1,0:T(8,128)(2,1)S(1)}, u32[]{:S(2)}, u32[]{:S(2)}) collective-permute-start(bf16[2,4,32,128]{3,2,1,0:T(8,128)(2,1)S(1)} %shard_map.88.refs_0_), channel_id=1, source_target_pairs={{0,8},{4,12},{8,0},{12,4},{16,24},{20,28},{24,16},{28,20},{1,9},{5... | collective-permute-start | bytes 196616 | tf_op jit(solution)/shard_map/ppermute | solution.py:403
  11.0 3.8 %collective-permute-start.5 = (bf16[8,2,32,128]{3,2,1,0:T(8,128)(2,1)S(1)}, bf16[8,2,32,128]{3,2,1,0:T(8,128)(2,1)S(1)}, u32[]{:S(2)}, u32[]{:S(2)}) collective-permute-start(bf16[8,2,32,128]{3,2,1,0:T(8,128)(2,1)S(1)} %get-tuple-element.38), channel_id=1, source_target_pairs={{0,4},{4,0},{8,12},{12,8},{16,20},{20,16},{24,28},{28,24},{1,5},{5... | collective-permute-start | bytes 393224 | tf_op jit(solution)/shard_map/ppermute | solution.py:403
  11.1 7.2 %collective-permute-start.7 = (bf16[8,2,32,128]{3,2,1,0:T(8,128)(2,1)S(1)}, bf16[8,2,32,128]{3,2,1,0:T(8,128)(2,1)S(1)}, u32[]{:S(2)}, u32[]{:S(2)}) collective-permute-start(bf16[8,2,32,128]{3,2,1,0:T(8,128)(2,1)S(1)} %get-tuple-element.45), channel_id=1, source_target_pairs={{1,2},{4,5},{6,7},{9,10},{12,13},{14,15},{17,18},{20,21},{22,23},{... | collective-permute-start | bytes 393224 | tf_op jit(solution)/shard_map/ppermute | solution.py:418
  11.9 2.7 %collective-permute-start = (s32[1,4,8,32]{3,2,1,0:T(8,128)}, s32[1,4,8,32]{3,2,1,0:T(8,128)S(1)}, u32[]{:S(2)}, u32[]{:S(2)}) collective-permute-start(s32[1,4,8,32]{3,2,1,0:T(8,128)} %bitcast.3), channel_id=1, source_target_pairs={{0,4},{4,0},{8,12},{12,8},{16,20},{20,16},{24,28},{28,24},{1,5},{5... | collective-permute-start | bytes 12296 | tf_op jit(solution)/shard_map/ppermute | solution.py:403
  12.8 1.9 %collective-permute-start.6 = (f32[1,1024]{1,0:T(1,128)}, f32[1,1024]{1,0:T(1,128)S(1)}, u32[]{:S(2)}, u32[]{:S(2)}) collective-permute-start(f32[1,1024]{1,0:T(1,128)} %refs_5_.1), channel_id=1, source_target_pairs={{0,4},{4,0},{8,12},{12,8},{16,20},{20,16},{24,28},{28,24},{1,5},{5... | collective-permute-start | bytes 12296 | tf_op jit(solution)/shard_map/ppermute | solution.py:403
  26.1 1.5 %collective-permute-start.9 = (bf16[8,2,32,128]{3,2,1,0:T(8,128)(2,1)S(1)}, bf16[8,2,32,128]{3,2,1,0:T(8,128)(2,1)S(1)}, u32[]{:S(2)}, u32[]{:S(2)}) collective-permute-start(bf16[8,2,32,128]{3,2,1,0:T(8,128)(2,1)S(1)} %get-tuple-element.51), channel_id=1, source_target_pairs={{0,4},{4,0},{8,12},{12,8},{16,20},{20,16},{24,28},{28,24},{1,5},{5... | collective-permute-start | bytes 393224 | tf_op jit(solution)/shard_map/ppermute | solution.py:403
  26.6 5.0 %collective-permute-start.8 = (bf16[8,2,32,128]{3,2,1,0:T(8,128)(2,1)S(1)}, bf16[8,2,32,128]{3,2,1,0:T(8,128)(2,1)S(1)}, u32[]{:S(2)}, u32[]{:S(2)}) collective-permute-start(bf16[8,2,32,128]{3,2,1,0:T(8,128)(2,1)S(1)} %get-tuple-element.50), channel_id=1, source_target_pairs={{1,2},{4,5},{6,7},{9,10},{12,13},{14,15},{17,18},{20,21},{22,23},{... | collective-permute-start | bytes 393224 | tf_op jit(solution)/shard_map/ppermute | solution.py:418
  31.7 5.0 %collective-permute-start.10 = (bf16[2,4,32,128]{3,2,1,0:T(8,128)(2,1)S(1)}, bf16[2,4,32,128]{3,2,1,0:T(8,128)(2,1)S(1)}, u32[]{:S(2)}, u32[]{:S(2)}) collective-permute-start(bf16[2,4,32,128]{3,2,1,0:T(8,128)(2,1)S(1)} %get-tuple-element.53), channel_id=1, source_target_pairs={{0,8},{4,12},{8,0},{12,4},{16,24},{20,28},{24,16},{28,20},{1,9},{5... | collective-permute-start | bytes 196616 | tf_op jit(solution)/shard_map/ppermute | solution.py:403
  32.5 5.0 %collective-permute-start.11 = (bf16[2,4,32,128]{3,2,1,0:T(8,128)(2,1)S(1)}, bf16[2,4,32,128]{3,2,1,0:T(8,128)(2,1)S(1)}, u32[]{:S(2)}, u32[]{:S(2)}) collective-permute-start(bf16[2,4,32,128]{3,2,1,0:T(8,128)(2,1)S(1)} %get-tuple-element.54), channel_id=1, source_target_pairs={{0,16},{4,20},{8,24},{12,28},{16,0},{20,4},{24,8},{28,12},{1,17},{... | collective-permute-start | bytes 196616 | tf_op jit(solution)/shard_map/ppermute | solution.py:403
  33.8 5.2 %collective-permute-start.12 = (bf16[2,4,32,128]{3,2,1,0:T(8,128)(2,1)S(1)}, bf16[2,4,32,128]{3,2,1,0:T(8,128)(2,1)S(1)}, u32[]{:S(2)}, u32[]{:S(2)}) collective-permute-start(bf16[2,4,32,128]{3,2,1,0:T(8,128)(2,1)S(1)} %get-tuple-element.55), channel_id=1, source_target_pairs={{0,24},{4,28},{8,16},{12,20},{16,8},{20,12},{24,0},{28,4},{1,25},{... | collective-permute-start | bytes 196616 | tf_op jit(solution)/shard_map/ppermute | solution.py:403
  39.0 1.4 %collective-permute-start.13 = (bf16[4,32,128]{2,1,0:T(8,128)(2,1)S(1)}, bf16[4,32,128]{2,1,0:T(8,128)(2,1)S(1)}, u32[]{:S(2)}, u32[]{:S(2)}) collective-permute-start(bf16[4,32,128]{2,1,0:T(8,128)(2,1)S(1)} %get-tuple-element.57), channel_id=1, source_target_pairs={{0,4},{4,0},{8,12},{12,8},{16,20},{20,16},{24,28},{28,24},{1,5},{5... | collective-permute-start | bytes 98312 | tf_op jit(solution)/shard_map/ppermute | solution.py:403
  39.1 1.3 %collective-permute-start.14 = (f32[1,512]{1,0:T(1,128)S(1)}, f32[1,512]{1,0:T(1,128)S(1)}, u32[]{:S(2)}, u32[]{:S(2)}) collective-permute-start(f32[1,512]{1,0:T(1,128)S(1)} %get-tuple-element.59), channel_id=1, source_target_pairs={{0,4},{4,0},{8,12},{12,8},{16,20},{20,16},{24,28},{28,24},{1,5},{5... | collective-permute-start | bytes 6152 | tf_op jit(solution)/shard_map/ppermute | solution.py:403

commit v7 on v6

--- a/solution.py
+++ b/solution.py
@@ -226,12 +226,13 @@
         raws = []
         for lanes in groups:
             parts = jnp.dot(
-                band_t[...], volume[:, :, lanes].reshape(planes * channels, wide),
+                jnp.concatenate([band_t[0:planes], band_t[2 * planes :]], axis=0),
+                volume[:, :, lanes].reshape(planes * channels, wide),
                 preferred_element_type=F32,
             )
             raws.append(
                 parts[0:planes]
-                + (parts[2 * planes : 3 * planes] + parts[3 * planes : 4 * planes])
+                + (parts[planes : 2 * planes] + parts[2 * planes : 3 * planes])
             )
         stacks = []
         start = first * BLK

time: 41.2 us -> 41.3 us (level)
  no operation moved by 1% of the time
where the time goes in v7:
time: 41.3 us; the launch traced here: 41.1 us
  Pallas kernels  14.8 us (36%)
  waiting for transfers between devices  13.1 us (32%)
  starting transfers between devices  12.4 us (30%)
  between operations  0.76 us (2%)
    ppermute x13, starting transfers between devices, exchange(): return lax.ppermute(x, 'frame', [(i, i ^ distance) for i in range(count)])  10.7 us
    ppermute x13, waiting for transfers between devices, exchange(): return lax.ppermute(x, 'frame', [(i, i ^ distance) for i in range(count)])  9.07 us
    pallas_call x1, Pallas kernels, per_device(): big_call(depth_kernel, 2, 9 + frames // 2, (depth_half, depth_half, rim_s...  4.92 us
    ppermute x2, waiting for transfers between devices, swap_outer(): lax.ppermute(x, ('frame', 'tile'), pairs + [(b, a) for a, b in pairs])  3.98 us
    pallas_call x1, Pallas kernels, per_device(): big_call(forward_kernel, 2, 6 + frames // 2, (shape((planes, V, channels,...  3.49 us
    pallas_call x1, Pallas kernels, per_device(): big_call(backward_kernel, 2, 5, (shape((frames, half, channels, BLK), F32...  2.87 us
    pallas_call x1, Pallas kernels, per_device(): prepare(head_weight, reg_weight, pltpu.with_memory_space_constraint(kerne...  1.78 us
    ppermute x2, starting transfers between devices, swap_outer(): lax.ppermute(x, ('frame', 'tile'), pairs + [(b, a) for a, b in pairs])  1.66 us
  transfers between devices with their start and end apart: 15, of which 10 were waited for; matrix products, arithmetic and copies ran while one was open for 0% of the time, Pallas kernels for 15%

profile of v7, /device:TPU:0, one launch (start us, length us, event | category | flops | bytes accessed | tf_op | source)
XLA Modules:
  0.0 41.1 jit_solution(5255179637497928441)
XLA Ops:
  0.6 0.6 %collective-permute-start.1 = (bf16[1,32,1024]{2,1,0:T(8,128)(2,1)}, bf16[1,32,1024]{2,1,0:T(8,128)(2,1)S(1)}, u32[]{:S(2)}, u32[]{:S(2)}) collective-permute-start(bf16[1,32,1024]{2,1,0:T(8,128)(2,1)} %refs_0_.1), channel_id=1, source_target_pairs={{0,4},{4,0},{8,12},{12,8},{16,20},{20,16},{24,28},{28,24},{1,5},{5... | collective-permute-start | bytes 196616 | tf_op jit(solution)/shard_map/ppermute | solution.py:404
  1.2 0.9 %stage_arguments.1 = (bf16[1,32,1024]{2,1,0:T(8,128)(2,1)S(1)}, s32[4,8]{1,0:T(4,128)S(1)}, bf16[3,8,32]{2,1,0:T(8,128)(2,1)S(1)}, f32[8]{0:T(128)S(1)}, s32[1,4...) custom-call(bf16[1,32,1024]{2,1,0:T(8,128)(2,1)} %refs_0_.1, s32[4,8]{1,0:T(4,128)} %bitcast.4, bf16[3,8,32]{2,1,0:T(8,128)(2,1)} %refs_2_.1, ...), custom_call_target="tpu_custom_call" | custom-call | tf_op jit(solution)/shard_map/stage_arguments/pallas_call | solution.py:445
  2.3 3.8 %collective-permute-start.4 = (bf16[2,4,32,128]{3,2,1,0:T(8,128)(2,1)S(1)}, bf16[2,4,32,128]{3,2,1,0:T(8,128)(2,1)S(1)}, u32[]{:S(2)}, u32[]{:S(2)}) collective-permute-start(bf16[2,4,32,128]{3,2,1,0:T(8,128)(2,1)S(1)} %shard_map.88.refs_0_), channel_id=1, source_target_pairs={{0,24},{4,28},{8,16},{12,20},{16,8},{20,12},{24,0},{28,4},{1,25},{... | collective-permute-start | bytes 196616 | tf_op jit(solution)/shard_map/ppermute | solution.py:404
  6.2 0.5 %collective-permute-start.3 = (bf16[2,4,32,128]{3,2,1,0:T(8,128)(2,1)S(1)}, bf16[2,4,32,128]{3,2,1,0:T(8,128)(2,1)S(1)}, u32[]{:S(2)}, u32[]{:S(2)}) collective-permute-start(bf16[2,4,32,128]{3,2,1,0:T(8,128)(2,1)S(1)} %shard_map.88.refs_0_), channel_id=1, source_target_pairs={{0,16},{4,20},{8,24},{12,28},{16,0},{20,4},{24,8},{28,12},{1,17},{... | collective-permute-start | bytes 196616 | tf_op jit(solution)/shard_map/ppermute | solution.py:404
  6.8 1.8 %collective-permute-done.4.refs_3_ = bf16[2,4,32,128]{3,2,1,0:T(8,128)(2,1)S(1)} collective-permute-done((bf16[2,4,32,128]{3,2,1,0:T(8,128)(2,1)S(1)}, bf16[2,4,32,128]{3,2,1,0:T(8,128)(2,1)S(1)}, u32[]{:S(2)}, u32[]{:S(2)}) %collective-permute-start.4) | collective-permute-done | bytes 65568 | tf_op jit(solution)/shard_map/ppermute | solution.py:404
  8.6 1.9 %collective-permute-done.3.refs_2_ = bf16[2,4,32,128]{3,2,1,0:T(8,128)(2,1)S(1)} collective-permute-done((bf16[2,4,32,128]{3,2,1,0:T(8,128)(2,1)S(1)}, bf16[2,4,32,128]{3,2,1,0:T(8,128)(2,1)S(1)}, u32[]{:S(2)}, u32[]{:S(2)}) %collective-permute-start.3) | collective-permute-done | bytes 65568 | tf_op jit(solution)/shard_map/ppermute | solution.py:404
  10.4 0.5 %collective-permute-done.2.refs_1_ = bf16[2,4,32,128]{3,2,1,0:T(8,128)(2,1)S(1)} collective-permute-done((bf16[2,4,32,128]{3,2,1,0:T(8,128)(2,1)S(1)}, bf16[2,4,32,128]{3,2,1,0:T(8,128)(2,1)S(1)}, u32[]{:S(2)}, u32[]{:S(2)}) %collective-permute-start.2) | collective-permute-done | bytes 65568 | tf_op jit(solution)/shard_map/ppermute | solution.py:404
  11.1 0.8 %collective-permute-start.7 = (bf16[8,2,32,128]{3,2,1,0:T(8,128)(2,1)S(1)}, bf16[8,2,32,128]{3,2,1,0:T(8,128)(2,1)S(1)}, u32[]{:S(2)}, u32[]{:S(2)}) collective-permute-start(bf16[8,2,32,128]{3,2,1,0:T(8,128)(2,1)S(1)} %get-tuple-element.45), channel_id=1, source_target_pairs={{1,2},{4,5},{6,7},{9,10},{12,13},{14,15},{17,18},{20,21},{22,23},{... | collective-permute-start | bytes 393224 | tf_op jit(solution)/shard_map/ppermute | solution.py:419
  11.9 0.9 %collective-permute-start = (s32[1,4,8,32]{3,2,1,0:T(8,128)}, s32[1,4,8,32]{3,2,1,0:T(8,128)S(1)}, u32[]{:S(2)}, u32[]{:S(2)}) collective-permute-start(s32[1,4,8,32]{3,2,1,0:T(8,128)} %bitcast.3), channel_id=1, source_target_pairs={{0,4},{4,0},{8,12},{12,8},{16,20},{20,16},{24,28},{28,24},{1,5},{5... | collective-permute-start | bytes 12296 | tf_op jit(solution)/shard_map/ppermute | solution.py:404
  12.8 1.8 %shard_map.87 = (bf16[32,32,128]{2,1,0:T(8,128)(2,1)S(1)}, bf16[128,1024]{1,0:T(8,128)(2,1)S(1)}, bf16[32,128,128]{2,1,0:T(8,128)(2,1)S(1)}) custom-call(f32[8]{0:T(128)S(1)} %get-tuple-element.34.head, bf16[3,8,32]{2,1,0:T(8,128)(2,1)S(1)} %get-tuple-element.35.reg, bf16[32,128,128]{2,1,0:T(8,128)(2,1)} %kernels.1), custom_call_target="tpu_custom_call" | custom-call | tf_op jit(solution)/shard_map/pallas_call | solution.py:462
  14.8 3.5 %shard_map.90 = (f32[32,4,32,512]{3,2,1,0:T(8,128)S(1)}, f32[32,32,512]{2,1,0:T(8,128)S(1)}, bf16[32,32,512]{2,1,0:T(8,128)(2,1)S(1)}, f32[1,256]{1,0:T(1,128)S(1)}, f32[1,256]{1,0:T(1,128)S(1)}) custom-call(s32[4,8]{1,0:T(4,128)S(1)} %get-tuple-element.32.views, s32[8,128]{1,0:T(8,128)S(1)} %shard_map.86.table, ...), custom_call_target="tpu_custom_call" | custom-call | flops 536870912 | bytes 4194304 | tf_op jit(solution)/shard_map/pallas_call | solution.py:496
  18.3 4.9 %shard_map.91 = (f32[1,512]{1,0:T(1,128)S(1)}, f32[1,512]{1,0:T(1,128)S(1)}, bf16[8,2,32,128]{3,2,1,0:T(8,128)(2,1)S(1)}, f32[64,32,128]{2,1,0:T(8,128)S(1)}) custom-call(s32[4,8]{1,0:T(4,128)S(1)} %get-tuple-element.32.views, s32[8,128]{1,0:T(8,128)S(1)} %shard_map.86.table, bf16[8,2,32,128]{3,2,1,0:T(8,128)(2,1)S(1)} %collective-permute-done.7.outer, ...), custom_call_target="tpu_custom_call" | custom-call | flops 1073741824 | bytes 4194304 | tf_op jit(solution)/shard_map/pallas_call | solution.py:506
  23.2 2.9 %shard_map.92 = (f32[8,4,32,128]{3,2,1,0:T(8,128)S(1)}, bf16[8,2,32,128]{3,2,1,0:T(8,128)(2,1)S(1)}) custom-call(s32[4,8]{1,0:T(4,128)S(1)} %get-tuple-element.32.views, s32[8,128]{1,0:T(8,128)S(1)} %shard_map.86.table, bf16[32,128,128]{2,1,0:T(8,128)(2,1)S(1)} %get-tuple-element.36.matrices, f32[32,4,32,512]{3,2,1,0:T(8,128)S(1)} %get-tuple-element.42.shifted, ...), custom_call_target="tpu_custom_call" | custom-call | flops 536870912 | bytes 4194304 | tf_op jit(solution)/shard_map/pallas_call | solution.py:523
  26.1 0.5 %collective-permute-start.9 = (bf16[8,2,32,128]{3,2,1,0:T(8,128)(2,1)S(1)}, bf16[8,2,32,128]{3,2,1,0:T(8,128)(2,1)S(1)}, u32[]{:S(2)}, u32[]{:S(2)}) collective-permute-start(bf16[8,2,32,128]{3,2,1,0:T(8,128)(2,1)S(1)} %get-tuple-element.51), channel_id=1, source_target_pairs={{0,4},{4,0},{8,12},{12,8},{16,20},{20,16},{24,28},{28,24},{1,5},{5... | collective-permute-start | bytes 393224 | tf_op jit(solution)/shard_map/ppermute | solution.py:404
  26.6 0.8 %collective-permute-start.8 = (bf16[8,2,32,128]{3,2,1,0:T(8,128)(2,1)S(1)}, bf16[8,2,32,128]{3,2,1,0:T(8,128)(2,1)S(1)}, u32[]{:S(2)}, u32[]{:S(2)}) collective-permute-start(bf16[8,2,32,128]{3,2,1,0:T(8,128)(2,1)S(1)} %get-tuple-element.50), channel_id=1, source_target_pairs={{1,2},{4,5},{6,7},{9,10},{12,13},{14,15},{17,18},{20,21},{22,23},{... | collective-permute-start | bytes 393224 | tf_op jit(solution)/shard_map/ppermute | solution.py:419
  27.6 4.0 %collective-permute-done.8.outer = bf16[8,2,32,128]{3,2,1,0:T(8,128)(2,1)S(1)} collective-permute-done((bf16[8,2,32,128]{3,2,1,0:T(8,128)(2,1)S(1)}, bf16[8,2,32,128]{3,2,1,0:T(8,128)(2,1)S(1)}, u32[]{:S(2)}, u32[]{:S(2)}) %collective-permute-start.8) | collective-permute-done | bytes 131104 | tf_op jit(solution)/shard_map/ppermute | solution.py:419
  31.7 0.9 %collective-permute-start.10 = (bf16[2,4,32,128]{3,2,1,0:T(8,128)(2,1)S(1)}, bf16[2,4,32,128]{3,2,1,0:T(8,128)(2,1)S(1)}, u32[]{:S(2)}, u32[]{:S(2)}) collective-permute-start(bf16[2,4,32,128]{3,2,1,0:T(8,128)(2,1)S(1)} %get-tuple-element.53), channel_id=1, source_target_pairs={{0,8},{4,12},{8,0},{12,4},{16,24},{20,28},{24,16},{28,20},{1,9},{5... | collective-permute-start | bytes 196616 | tf_op jit(solution)/shard_map/ppermute | solution.py:404
  32.5 1.2 %collective-permute-start.11 = (bf16[2,4,32,128]{3,2,1,0:T(8,128)(2,1)S(1)}, bf16[2,4,32,128]{3,2,1,0:T(8,128)(2,1)S(1)}, u32[]{:S(2)}, u32[]{:S(2)}) collective-permute-start(bf16[2,4,32,128]{3,2,1,0:T(8,128)(2,1)S(1)} %get-tuple-element.54), channel_id=1, source_target_pairs={{0,16},{4,20},{8,24},{12,28},{16,0},{20,4},{24,8},{28,12},{1,17},{... | collective-permute-start | bytes 196616 | tf_op jit(solution)/shard_map/ppermute | solution.py:404
  33.8 1.4 %collective-permute-start.12 = (bf16[2,4,32,128]{3,2,1,0:T(8,128)(2,1)S(1)}, bf16[2,4,32,128]{3,2,1,0:T(8,128)(2,1)S(1)}, u32[]{:S(2)}, u32[]{:S(2)}) collective-permute-start(bf16[2,4,32,128]{3,2,1,0:T(8,128)(2,1)S(1)} %get-tuple-element.55), channel_id=1, source_target_pairs={{0,24},{4,28},{8,16},{12,20},{16,8},{20,12},{24,0},{28,4},{1,25},{... | collective-permute-start | bytes 196616 | tf_op jit(solution)/shard_map/ppermute | solution.py:404
  35.2 1.4 %collective-permute-done.10.refs_0_ = bf16[2,4,32,128]{3,2,1,0:T(8,128)(2,1)S(1)} collective-permute-done((bf16[2,4,32,128]{3,2,1,0:T(8,128)(2,1)S(1)}, bf16[2,4,32,128]{3,2,1,0:T(8,128)(2,1)S(1)}, u32[]{:S(2)}, u32[]{:S(2)}) %collective-permute-start.10) | collective-permute-done | bytes 65568 | tf_op jit(solution)/shard_map/ppermute | solution.py:404
  36.6 0.9 %collective-permute-done.11.refs_1_ = bf16[2,4,32,128]{3,2,1,0:T(8,128)(2,1)S(1)} collective-permute-done((bf16[2,4,32,128]{3,2,1,0:T(8,128)(2,1)S(1)}, bf16[2,4,32,128]{3,2,1,0:T(8,128)(2,1)S(1)}, u32[]{:S(2)}, u32[]{:S(2)}) %collective-permute-start.11) | collective-permute-done | bytes 65568 | tf_op jit(solution)/shard_map/ppermute | solution.py:404
  37.5 1.4 %collective-permute-done.12.refs_2_ = bf16[2,4,32,128]{3,2,1,0:T(8,128)(2,1)S(1)} collective-permute-done((bf16[2,4,32,128]{3,2,1,0:T(8,128)(2,1)S(1)}, bf16[2,4,32,128]{3,2,1,0:T(8,128)(2,1)S(1)}, u32[]{:S(2)}, u32[]{:S(2)}) %collective-permute-start.12) | collective-permute-done | bytes 65568 | tf_op jit(solution)/shard_map/ppermute | solution.py:404
  39.6 0.8 %collective-permute-done.14.depth_partner = f32[1,512]{1,0:T(1,128)S(1)} collective-permute-done((f32[1,512]{1,0:T(1,128)S(1)}, f32[1,512]{1,0:T(1,128)S(1)}, u32[]{:S(2)}, u32[]{:S(2)}) %collective-permute-start.14) | collective-permute-done | bytes 2080 | tf_op jit(solution)/shard_map/ppermute | solution.py:404
  40.4 0.7 %shard_map.95 = (f32[1,32,1024]{2,1,0:T(8,128)}, f32[1,1024]{1,0:T(1,128)}) custom-call(f32[4,32,128]{2,1,0:T(8,128)S(1)} %get-tuple-element.56.mine, bf16[4,32,128]{2,1,0:T(8,128)(2,1)S(1)} %collective-permute-done.13.partner, f32[1,512]{1,0:T(1,128)S(1)} %get-tuple-element.58.depth_mine, f32[1,512]{1,0:T(1,128)S(1)} %collective-permute-done.14.depth_partner), custom_call_target="tpu_custom_call" | custom-call | tf_op jit(solution)/shard_map/pallas_call | solution.py:543
  (17 shorter events, 1.4 us)
Async XLA Ops:
  0.6 1.7 %collective-permute-start.1 = (bf16[1,32,1024]{2,1,0:T(8,128)(2,1)}, bf16[1,32,1024]{2,1,0:T(8,128)(2,1)S(1)}, u32[]{:S(2)}, u32[]{:S(2)}) collective-permute-start(bf16[1,32,1024]{2,1,0:T(8,128)(2,1)} %refs_0_.1), channel_id=1, source_target_pairs={{0,4},{4,0},{8,12},{12,8},{16,20},{20,16},{24,28},{28,24},{1,5},{5... | collective-permute-start | bytes 196616 | tf_op jit(solution)/shard_map/ppermute | solution.py:404
  2.3 6.3 %collective-permute-start.4 = (bf16[2,4,32,128]{3,2,1,0:T(8,128)(2,1)S(1)}, bf16[2,4,32,128]{3,2,1,0:T(8,128)(2,1)S(1)}, u32[]{:S(2)}, u32[]{:S(2)}) collective-permute-start(bf16[2,4,32,128]{3,2,1,0:T(8,128)(2,1)S(1)} %shard_map.88.refs_0_), channel_id=1, source_target_pairs={{0,24},{4,28},{8,16},{12,20},{16,8},{20,12},{24,0},{28,4},{1,25},{... | collective-permute-start | bytes 196616 | tf_op jit(solution)/shard_map/ppermute | solution.py:404
  6.2 4.3 %collective-permute-start.3 = (bf16[2,4,32,128]{3,2,1,0:T(8,128)(2,1)S(1)}, bf16[2,4,32,128]{3,2,1,0:T(8,128)(2,1)S(1)}, u32[]{:S(2)}, u32[]{:S(2)}) collective-permute-start(bf16[2,4,32,128]{3,2,1,0:T(8,128)(2,1)S(1)} %shard_map.88.refs_0_), channel_id=1, source_target_pairs={{0,16},{4,20},{8,24},{12,28},{16,0},{20,4},{24,8},{28,12},{1,17},{... | collective-permute-start | bytes 196616 | tf_op jit(solution)/shard_map/ppermute | solution.py:404
  6.7 4.3 %collective-permute-start.2 = (bf16[2,4,32,128]{3,2,1,0:T(8,128)(2,1)S(1)}, bf16[2,4,32,128]{3,2,1,0:T(8,128)(2,1)S(1)}, u32[]{:S(2)}, u32[]{:S(2)}) collective-permute-start(bf16[2,4,32,128]{3,2,1,0:T(8,128)(2,1)S(1)} %shard_map.88.refs_0_), channel_id=1, source_target_pairs={{0,8},{4,12},{8,0},{12,4},{16,24},{20,28},{24,16},{28,20},{1,9},{5... | collective-permute-start | bytes 196616 | tf_op jit(solution)/shard_map/ppermute | solution.py:404
  11.0 3.8 %collective-permute-start.5 = (bf16[8,2,32,128]{3,2,1,0:T(8,128)(2,1)S(1)}, bf16[8,2,32,128]{3,2,1,0:T(8,128)(2,1)S(1)}, u32[]{:S(2)}, u32[]{:S(2)}) collective-permute-start(bf16[8,2,32,128]{3,2,1,0:T(8,128)(2,1)S(1)} %get-tuple-element.38), channel_id=1, source_target_pairs={{0,4},{4,0},{8,12},{12,8},{16,20},{20,16},{24,28},{28,24},{1,5},{5... | collective-permute-start | bytes 393224 | tf_op jit(solution)/shard_map/ppermute | solution.py:404
  11.1 7.2 %collective-permute-start.7 = (bf16[8,2,32,128]{3,2,1,0:T(8,128)(2,1)S(1)}, bf16[8,2,32,128]{3,2,1,0:T(8,128)(2,1)S(1)}, u32[]{:S(2)}, u32[]{:S(2)}) collective-permute-start(bf16[8,2,32,128]{3,2,1,0:T(8,128)(2,1)S(1)} %get-tuple-element.45), channel_id=1, source_target_pairs={{1,2},{4,5},{6,7},{9,10},{12,13},{14,15},{17,18},{20,21},{22,23},{... | collective-permute-start | bytes 393224 | tf_op jit(solution)/shard_map/ppermute | solution.py:419
  11.9 2.7 %collective-permute-start = (s32[1,4,8,32]{3,2,1,0:T(8,128)}, s32[1,4,8,32]{3,2,1,0:T(8,128)S(1)}, u32[]{:S(2)}, u32[]{:S(2)}) collective-permute-start(s32[1,4,8,32]{3,2,1,0:T(8,128)} %bitcast.3), channel_id=1, source_target_pairs={{0,4},{4,0},{8,12},{12,8},{16,20},{20,16},{24,28},{28,24},{1,5},{5... | collective-permute-start | bytes 12296 | tf_op jit(solution)/shard_map/ppermute | solution.py:404
  12.8 1.9 %collective-permute-start.6 = (f32[1,1024]{1,0:T(1,128)}, f32[1,1024]{1,0:T(1,128)S(1)}, u32[]{:S(2)}, u32[]{:S(2)}) collective-permute-start(f32[1,1024]{1,0:T(1,128)} %refs_5_.1), channel_id=1, source_target_pairs={{0,4},{4,0},{8,12},{12,8},{16,20},{20,16},{24,28},{28,24},{1,5},{5... | collective-permute-start | bytes 12296 | tf_op jit(solution)/shard_map/ppermute | solution.py:404
  26.1 1.5 %collective-permute-start.9 = (bf16[8,2,32,128]{3,2,1,0:T(8,128)(2,1)S(1)}, bf16[8,2,32,128]{3,2,1,0:T(8,128)(2,1)S(1)}, u32[]{:S(2)}, u32[]{:S(2)}) collective-permute-start(bf16[8,2,32,128]{3,2,1,0:T(8,128)(2,1)S(1)} %get-tuple-element.51), channel_id=1, source_target_pairs={{0,4},{4,0},{8,12},{12,8},{16,20},{20,16},{24,28},{28,24},{1,5},{5... | collective-permute-start | bytes 393224 | tf_op jit(solution)/shard_map/ppermute | solution.py:404
  26.6 5.0 %collective-permute-start.8 = (bf16[8,2,32,128]{3,2,1,0:T(8,128)(2,1)S(1)}, bf16[8,2,32,128]{3,2,1,0:T(8,128)(2,1)S(1)}, u32[]{:S(2)}, u32[]{:S(2)}) collective-permute-start(bf16[8,2,32,128]{3,2,1,0:T(8,128)(2,1)S(1)} %get-tuple-element.50), channel_id=1, source_target_pairs={{1,2},{4,5},{6,7},{9,10},{12,13},{14,15},{17,18},{20,21},{22,23},{... | collective-permute-start | bytes 393224 | tf_op jit(solution)/shard_map/ppermute | solution.py:419
  31.7 5.0 %collective-permute-start.10 = (bf16[2,4,32,128]{3,2,1,0:T(8,128)(2,1)S(1)}, bf16[2,4,32,128]{3,2,1,0:T(8,128)(2,1)S(1)}, u32[]{:S(2)}, u32[]{:S(2)}) collective-permute-start(bf16[2,4,32,128]{3,2,1,0:T(8,128)(2,1)S(1)} %get-tuple-element.53), channel_id=1, source_target_pairs={{0,8},{4,12},{8,0},{12,4},{16,24},{20,28},{24,16},{28,20},{1,9},{5... | collective-permute-start | bytes 196616 | tf_op jit(solution)/shard_map/ppermute | solution.py:404
  32.5 5.0 %collective-permute-start.11 = (bf16[2,4,32,128]{3,2,1,0:T(8,128)(2,1)S(1)}, bf16[2,4,32,128]{3,2,1,0:T(8,128)(2,1)S(1)}, u32[]{:S(2)}, u32[]{:S(2)}) collective-permute-start(bf16[2,4,32,128]{3,2,1,0:T(8,128)(2,1)S(1)} %get-tuple-element.54), channel_id=1, source_target_pairs={{0,16},{4,20},{8,24},{12,28},{16,0},{20,4},{24,8},{28,12},{1,17},{... | collective-permute-start | bytes 196616 | tf_op jit(solution)/shard_map/ppermute | solution.py:404
  33.8 5.2 %collective-permute-start.12 = (bf16[2,4,32,128]{3,2,1,0:T(8,128)(2,1)S(1)}, bf16[2,4,32,128]{3,2,1,0:T(8,128)(2,1)S(1)}, u32[]{:S(2)}, u32[]{:S(2)}) collective-permute-start(bf16[2,4,32,128]{3,2,1,0:T(8,128)(2,1)S(1)} %get-tuple-element.55), channel_id=1, source_target_pairs={{0,24},{4,28},{8,16},{12,20},{16,8},{20,12},{24,0},{28,4},{1,25},{... | collective-permute-start | bytes 196616 | tf_op jit(solution)/shard_map/ppermute | solution.py:404
  39.0 1.4 %collective-permute-start.13 = (bf16[4,32,128]{2,1,0:T(8,128)(2,1)S(1)}, bf16[4,32,128]{2,1,0:T(8,128)(2,1)S(1)}, u32[]{:S(2)}, u32[]{:S(2)}) collective-permute-start(bf16[4,32,128]{2,1,0:T(8,128)(2,1)S(1)} %get-tuple-element.57), channel_id=1, source_target_pairs={{0,4},{4,0},{8,12},{12,8},{16,20},{20,16},{24,28},{28,24},{1,5},{5... | collective-permute-start | bytes 98312 | tf_op jit(solution)/shard_map/ppermute | solution.py:404
  39.1 1.3 %collective-permute-start.14 = (f32[1,512]{1,0:T(1,128)S(1)}, f32[1,512]{1,0:T(1,128)S(1)}, u32[]{:S(2)}, u32[]{:S(2)}) collective-permute-start(f32[1,512]{1,0:T(1,128)S(1)} %get-tuple-element.59), channel_id=1, source_target_pairs={{0,4},{4,0},{8,12},{12,8},{16,20},{20,16},{24,28},{28,24},{1,5},{5... | collective-permute-start | bytes 6152 | tf_op jit(solution)/shard_map/ppermute | solution.py:404
